TPU v7x, 128 devices: a whole 4x4x4 slice. The times are simulated.
128 devices in a mesh: ctx: 4 (over x), ch: 32 (over z, y, core).
Axes of the slice: x: 4, y: 4, z: 4, core: 2. Of those that a mesh axis runs over, the one named last changes fastest.
Arguments:
- features: bfloat16 [3, 512, 8192], P(None, 'ctx', 'ch'), may hold values from -6 to 6
- short_kernel: float32 [3, 7, 8192], P(None, None, 'ch'), may hold values from -2 to 2
- long_filter: bfloat16 [512, 8192], P('ctx', 'ch'), may hold values from -0.25 to 0.25
- out_weight: bfloat16 [8192, 8192], P(None, 'ch'), may hold values from -0.0625 to 0.0625
- grad_out: bfloat16 [512, 8192], P('ctx', 'ch'), may hold values from -6 to 6
Outputs:
- grad_features: bfloat16 [3, 512, 8192], P(None, 'ctx', 'ch')
- grad_kernel: float32 [3, 7, 8192], P(None, None, 'ch')
- grad_filter: float32 [512, 8192], P('ctx', 'ch')
- grad_weight: float32 [8192, 8192], P('ctx', 'ch')
All inputs are finite; a program needn't handle non-finite values.
Results may differ from a plain program's by a relative error of at most 0.0051.
Values may be sent and summed in bfloat16 or wider, within the bound.
No kernel may reach another device: no remote copies, remote signals or barrier semaphores. Data moves between devices by JAX's collectives and lax.ppermute only.
A program may use at most 64 MiB of HBM per device.

v0:
```python
import math

import jax
import jax.numpy as jnp
from jax import lax
from jax.sharding import PartitionSpec as P

TRIPLE = lax.Precision.HIGH


def shifted(array, axis, by):
    peers = lax.axis_size(axis)
    pairs = [(i, i + by) for i in range(peers) if 0 <= i + by < peers]
    return lax.ppermute(array, axis, pairs)


def tables(period):
    index_row = lax.iota(jnp.int32, period)
    product = index_row[:, None] * index_row[None, :] % period
    angles = product.astype(jnp.float32) * (2.0 * math.pi / period)
    return (jnp.cos(angles), jnp.sin(angles))


def spectrum(cos_part, sin_part, block):
    values = block.astype(jnp.float32)
    real_part = jnp.dot(cos_part, values, precision=TRIPLE, preferred_element_type=jnp.float32)
    imag_part = -jnp.dot(sin_part, values, precision=TRIPLE, preferred_element_type=jnp.float32)
    return (real_part, imag_part)


def inverse(cos_part, sin_part, real_part, imag_part, period):
    first = jnp.dot(cos_part, real_part, precision=TRIPLE, preferred_element_type=jnp.float32)
    second = jnp.dot(sin_part, imag_part, precision=TRIPLE, preferred_element_type=jnp.float32)
    return (first - second) / period


def pick_lag(lag_real, lag_imag, lag_index):
    lag_index = jnp.asarray(lag_index, jnp.int32)
    active = (lag_index >= 0).astype(jnp.float32)
    clipped = jnp.maximum(lag_index, 0)
    real_part = lax.dynamic_index_in_dim(lag_real, clipped, 0, keepdims=False)
    imag_part = lax.dynamic_index_in_dim(lag_imag, clipped, 0, keepdims=False)
    return (real_part, imag_part, active, clipped)


def local(features, short_kernel, long_filter, out_weight, grad_out):
    block_len = features.shape[1]
    chans = features.shape[2]
    taps = short_kernel.shape[1]
    margin = taps - 1
    blocks = lax.axis_size("ctx")
    position = lax.axis_index("ctx")
    period = 2 * block_len
    cos_table, sin_table = tables(period)
    cos_low, sin_low = (cos_table[:, :block_len], sin_table[:, :block_len])
    cos_mid, sin_mid = (
        cos_table[:, block_len - 1 : period - 1],
        sin_table[:, block_len - 1 : period - 1],
    )
    before = shifted(features[:, block_len - margin :, :], "ctx", 1)
    extended = jnp.concatenate([before, features], axis=1).astype(jnp.float32)
    conv = jnp.zeros((3, block_len, chans), jnp.float32)
    for tap_index in range(taps):
        conv = (
            conv
            + short_kernel[:, tap_index, None, :]
            * extended[:, margin - tap_index : margin - tap_index + block_len, :]
        )
    q_conv, k_conv, v_conv = (conv[0], conv[1], conv[2])
    gated = (k_conv * v_conv).astype(jnp.bfloat16)
    whole_filter = lax.all_gather(long_filter, "ctx", axis=0, tiled=True).astype(jnp.float32)
    padded = jnp.concatenate(
        [
            jnp.zeros((block_len - 1, chans), jnp.float32),
            whole_filter,
            jnp.zeros((block_len + 1, chans), jnp.float32),
        ],
        axis=0,
    )
    padded = padded.reshape(blocks + 2, block_len, chans)
    lag_time = jnp.concatenate([padded[:blocks], padded[1 : blocks + 1]], axis=1)
    lag_real = jnp.einsum(
        "fn,mnc->mfc", cos_table, lag_time, precision=TRIPLE, preferred_element_type=jnp.float32
    )
    lag_imag = -jnp.einsum(
        "fn,mnc->mfc", sin_table, lag_time, precision=TRIPLE, preferred_element_type=jnp.float32
    )
    empty = jnp.zeros((period, chans), jnp.float32)
    totals = (empty, empty)
    pieces = lax.all_gather(gated, "ctx", axis=0, tiled=True)
    first = jnp.int32(0)
    for inner in range(pieces.shape[0] // block_len):
        lag_index = position - (first // block_len + inner)
        gated_real, gated_imag = spectrum(
            cos_low, sin_low, pieces[inner * block_len : (inner + 1) * block_len]
        )
        add_filt_real, add_filt_imag, add_active, add_clipped = pick_lag(
            lag_real, lag_imag, lag_index
        )
        totals = (
            totals[0] + add_active * (add_filt_real * gated_real - add_filt_imag * gated_imag),
            totals[1] + add_active * (add_filt_real * gated_imag + add_filt_imag * gated_real),
        )
    long_out = inverse(
        cos_table[block_len - 1 : period - 1],
        sin_table[block_len - 1 : period - 1],
        totals[0],
        totals[1],
        period,
    )
    mixed = (q_conv * long_out).astype(jnp.bfloat16)
    partial_mixed = jnp.einsum(
        "tc,dc->td", grad_out, out_weight, preferred_element_type=jnp.float32
    )
    grad_mixed = lax.psum_scatter(partial_mixed, "ch", scatter_dimension=1, tiled=True)
    grad_long = (grad_mixed * q_conv).astype(jnp.bfloat16)
    own_real, own_imag = spectrum(cos_low, sin_low, gated)
    lag_empty = jnp.zeros((blocks, period, chans), jnp.float32)
    start_carry = (empty, empty, lag_empty, lag_empty)
    carry = start_carry
    pieces = lax.all_gather(grad_long, "ctx", axis=0, tiled=True)
    first = jnp.int32(0)
    for inner in range(pieces.shape[0] // block_len):
        lag_index = first // block_len + inner - position
        grad_real, grad_imag = spectrum(
            cos_mid, sin_mid, pieces[inner * block_len : (inner + 1) * block_len]
        )
        filt_real, filt_imag, active, clipped = pick_lag(lag_real, lag_imag, lag_index)
        back_real = carry[0] + active * (filt_real * grad_real + filt_imag * grad_imag)
        back_imag = carry[1] + active * (filt_real * grad_imag - filt_imag * grad_real)
        pair_real = active * (own_real * grad_real + own_imag * grad_imag)
        pair_imag = active * (own_real * grad_imag - own_imag * grad_real)
        old_real = lax.dynamic_index_in_dim(carry[2], clipped, 0, keepdims=False)
        old_imag = lax.dynamic_index_in_dim(carry[3], clipped, 0, keepdims=False)
        lags_real = lax.dynamic_update_index_in_dim(carry[2], old_real + pair_real, clipped, 0)
        lags_imag = lax.dynamic_update_index_in_dim(carry[3], old_imag + pair_imag, clipped, 0)
        carry = (back_real, back_imag, lags_real, lags_imag)
    grad_gated = inverse(cos_table[:block_len], sin_table[:block_len], carry[0], carry[1], period)
    lag_grads = (
        jnp.einsum(
            "nf,mfc->mnc", cos_table, carry[2], precision=TRIPLE, preferred_element_type=jnp.float32
        )
        - jnp.einsum(
            "nf,mfc->mnc", sin_table, carry[3], precision=TRIPLE, preferred_element_type=jnp.float32
        )
    ) / period
    upper_part = lag_grads[:, block_len - 1 : period - 1]
    lower_next = jnp.concatenate(
        [lag_grads[1:, : block_len - 1], jnp.zeros((1, block_len - 1, chans), jnp.float32)], axis=0
    )
    lower_next = jnp.concatenate([jnp.zeros((blocks, 1, chans), jnp.float32), lower_next], axis=1)
    filter_terms = (upper_part + lower_next).reshape(blocks * block_len, chans)
    grad_filter = lax.psum_scatter(filter_terms, "ctx", scatter_dimension=0, tiled=True)
    grad_conv = jnp.stack([grad_mixed * long_out, grad_gated * v_conv, grad_gated * k_conv], axis=0)
    after = shifted(grad_conv[:, :margin, :], "ctx", -1)
    grad_extended = jnp.concatenate([grad_conv, after], axis=1)
    feature_total = jnp.zeros((3, block_len, chans), jnp.float32)
    kernel_rows = []
    for tap_index in range(taps):
        feature_total = (
            feature_total
            + short_kernel[:, tap_index, None, :]
            * grad_extended[:, tap_index : tap_index + block_len, :]
        )
        kernel_rows.append(
            jnp.sum(
                grad_conv * extended[:, margin - tap_index : margin - tap_index + block_len, :],
                axis=1,
            )
        )
    grad_features = feature_total.astype(jnp.bfloat16)
    grad_kernel = lax.psum(jnp.stack(kernel_rows, axis=1), "ctx")
    weight_terms = jnp.einsum(
        "tn,tc->nc",
        lax.all_gather(mixed, "ch", axis=1, tiled=True),
        grad_out,
        preferred_element_type=jnp.float32,
    )
    grad_weight = lax.psum_scatter(weight_terms, "ctx", scatter_dimension=0, tiled=True)
    return (grad_features, grad_kernel, grad_filter, grad_weight)


def solution(mesh):
    return jax.shard_map(
        local,
        mesh=mesh,
        in_specs=(
            P(None, "ctx", "ch"),
            P(None, None, "ch"),
            P("ctx", "ch"),
            P(None, "ch"),
            P("ctx", "ch"),
        ),
        out_specs=(P(None, "ctx", "ch"), P(None, None, "ch"), P("ctx", "ch"), P("ctx", "ch")),
        check_vma=False,
    )
```

profile of v0, /device:TPU:1, one launch (start us, length us, event | category | flops | bytes accessed | tf_op | source)
XLA Modules:
  0.0 292.3 jit_solution(14209133033880053549)
XLA Ops:
  8.0 5.6 %fusion.236 = f32[128,8192]{1,0:T(8,128)} fusion(bf16[128,256]{1,0:T(8,128)(2,1)S(1)} %copy-done, bf16[8192,256]{1,0:T(8,128)(2,1)} %param.8), kind=kOutput, calls=%fused_computation.317 | convolution fusion | flops 536870912 | bytes 8454144 | tf_op jit(solution)/shard_map/tc,dc->td/dot_general | solution.py:112
  14.6 3.9 %collective-permute-start = (bf16[3,6,256]{2,1,0:T(8,128)(2,1)S(1)}, bf16[3,6,256]{2,1,0:T(8,128)(2,1)S(1)}, u32[]{:S(2)}, u32[]{:S(2)}) collective-permute-start(bf16[3,6,256]{2,1,0:T(8,128)(2,1)S(1)} %slice.192), channel_id=1, source_target_pairs={{0,32},{32,64},{64,96},{1,33},{33,65},{65,97},{2,34},{34,66},{66,9... | collective-permute-start | bytes 27656 | tf_op jit(solution)/shard_map/ppermute | solution.py:14
  18.5 9.5 %all_gather.12 = bf16[512,256]{1,0:T(8,128)(2,1)S(1)} all-gather(bf16[128,256]{1,0:T(8,128)(2,1)S(1)} %copy-done.31), channel_id=1, replica_groups=mesh['ctx'=4,'ch'=32] {'ctx'}, dimensions={0}, use_global_device_ids=true | all-gather | bytes 327680 | tf_op jit(solution)/shard_map/all_gather | solution.py:71
  31.1 2.6 fusion.4
  35.3 9.4 %all_gather.13 = bf16[512,256]{1,0:T(8,128)(2,1)S(1)} all-gather(bf16[128,256]{1,0:T(8,128)(2,1)S(1)} %multiply_convert_fusion.2), channel_id=1, replica_groups=mesh['ctx'=4,'ch'=32] {'ctx'}, dimensions={0}, use_global_device_ids=true | all-gather | bytes 327680 | tf_op jit(solution)/shard_map/all_gather | solution.py:90
  49.6 47.9 %reduce-scatter.4.cloned.1.call-done = f32[128,256]{1,0:T(8,128)} async-done(((f32[128,8192]{1,0:T(8,128)}), f32[128,256]{1,0:T(8,128)}) %reduce-scatter.4.cloned.1.call-update) | async-done | bytes 131088 | tf_op jit(solution)/shard_map/reduce_scatter | solution.py:115
  97.5 2.7 multiply_convert_fusion
  100.2 9.7 %all_gather.14 = bf16[512,256]{1,0:T(8,128)(2,1)S(1)} all-gather(bf16[128,256]{1,0:T(8,128)(2,1)S(1)} %get-tuple-element.31), channel_id=1, replica_groups=mesh['ctx'=4,'ch'=32] {'ctx'}, dimensions={0}, use_global_device_ids=true | all-gather | bytes 327680 | tf_op jit(solution)/shard_map/all_gather | solution.py:121
  112.5 1.8 copy.102
  114.3 1.8 copy.124
  121.2 1.8 copy.125
  123.0 1.8 copy.103
  126.6 2.1 fusion.17
  128.8 1.8 copy.108
  130.6 1.8 copy.128
  134.0 1.7 constant_dynamic-slice_fusion.2
  135.7 1.8 copy.129
  140.9 1.8 copy.109
  145.1 2.2 fusion.16
  147.3 1.8 copy.114
  149.1 1.8 copy.132
  152.5 1.7 constant_dynamic-slice_fusion.1
  154.2 1.8 copy.133
  159.4 1.8 copy.115
  163.6 2.2 fusion.15
  166.9 1.8 copy.136
  171.1 2.8 fusion.85
  173.9 2.8 fusion.1
  177.8 6.2 %fusion.237 = f32[8192,256]{1,0:T(8,128)} fusion(bf16[128,8192]{1,0:T(8,128)(2,1)} %all-gather.2.cloned.1.call-done, bf16[128,256]{1,0:T(8,128)(2,1)S(1)} %copy-done), kind=kOutput, calls=%fused_computation.318 | convolution fusion | flops 536870912 | bytes 10551296 | tf_op jit(solution)/shard_map/tn,tc->nc/dot_general | solution.py:173
  184.9 2.0 fusion.24
  190.4 13.9 %psum.7 = f32[3,7,256]{2,0,1:T(4,128)S(1)} all-reduce(f32[3,7,256]{2,0,1:T(4,128)S(1)} %constant_dynamic-update-slice_fusion), channel_id=1, replica_groups=mesh['ctx'=4,'ch'=32] {'ctx'}, use_global_device_ids=true, to_apply=%region_8.9 | all-reduce | flops 5376 | bytes 43008 | tf_op jit(solution)/shard_map/psum | solution.py:172
  206.0 79.7 %reduce-scatter.8.cloned.1.call-done = f32[2048,256]{1,0:T(8,128)} async-done(((f32[8192,256]{1,0:T(8,128)}), f32[2048,256]{1,0:T(8,128)}) %reduce-scatter.8.cloned.1.call-update) | async-done | bytes 2097168 | tf_op jit(solution)/shard_map/reduce_scatter | solution.py:179
  (145 shorter events, 45.5 us)
Async XLA Ops:
  7.2 90.3 %reduce-scatter.4.cloned.1.call-start = ((), (), s32[]{:S(2)}) async-start(), calls=%async_computation.3 | async-start | bytes 4325376 | tf_op jit(solution)/shard_map/reduce_scatter | solution.py:115
  13.6 4.9 %copy-start.31 = (bf16[128,256]{1,0:T(8,128)(2,1)S(1)}, bf16[128,256]{1,0:T(8,128)(2,1)}, u32[]{:S(2)}) copy-start(bf16[128,256]{1,0:T(8,128)(2,1)} %param.7) | copy-start | bytes 196612
  13.7 164.1 %all-gather.2.cloned.1.call-start = ((), (), s32[]{:S(2)}) async-start(), calls=%async_computation.5 | async-start | bytes 2162688 | tf_op jit(solution)/shard_map/all_gather | solution.py:175
  14.6 20.3 %collective-permute-start = (bf16[3,6,256]{2,1,0:T(8,128)(2,1)S(1)}, bf16[3,6,256]{2,1,0:T(8,128)(2,1)S(1)}, u32[]{:S(2)}, u32[]{:S(2)}) collective-permute-start(bf16[3,6,256]{2,1,0:T(8,128)(2,1)S(1)} %slice.192), channel_id=1, source_target_pairs={{0,32},{32,64},{64,96},{1,33},{33,65},{65,97},{2,34},{34,66},{66,9... | collective-permute-start | bytes 27656 | tf_op jit(solution)/shard_map/ppermute | solution.py:14
  28.1 5.7 %copy-start.32 = (f32[3,7,256]{2,1,0:T(8,128)S(1)}, f32[3,7,256]{2,1,0:T(8,128)}, u32[]{:S(2)}) copy-start(f32[3,7,256]{2,1,0:T(8,128)} %param.6) | copy-start | bytes 64516
  35.3 10.9 %copy-start.28 = (f32[3,128,256]{2,1,0:T(8,128)}, f32[3,128,256]{2,1,0:T(8,128)S(1)}, u32[]{:S(2)}) copy-start(f32[3,128,256]{2,1,0:T(8,128)S(1)} %multiply_add_fusion) | copy-start | bytes 1179652
  45.0 3.3 %copy-start.20 = (f32[256,256]{0,1:T(8,128)}, f32[256,256]{0,1:T(8,128)S(1)}, u32[]{:S(2)}) copy-start(f32[256,256]{0,1:T(8,128)S(1)} %convolution_negate_fusion.1) | copy-start | bytes 786436
  45.3 3.0 %copy-start.21 = (f32[256,256]{0,1:T(8,128)}, f32[256,256]{0,1:T(8,128)S(1)}, u32[]{:S(2)}) copy-start(f32[256,256]{0,1:T(8,128)S(1)} %convolution_negate_fusion.2) | copy-start | bytes 786436
  45.6 2.7 copy-start.22
  45.9 2.4 copy-start.23
  46.2 2.1 copy-start.24
  46.5 1.9 copy-start.25
  46.8 1.6 copy-start.26
  47.0 1.3 copy-start.27
  97.5 14.1 %copy-start.3 = (f32[256,256]{0,1:T(8,128)S(1)}, f32[256,256]{0,1:T(8,128)}, u32[]{:S(2)}) copy-start(f32[256,256]{0,1:T(8,128)} %fusion.173) | copy-start | bytes 786436
  109.9 1.4 copy-start.19
  111.3 1.3 copy-start.15
  116.1 89.9 %reduce-scatter.6.cloned.1.call-start = ((), (), s32[]{:S(2)}) async-start(), calls=%async_computation.4 | async-start | bytes 655360 | tf_op jit(solution)/shard_map/reduce_scatter | solution.py:153
  117.4 3.0 %copy-start.2 = (f32[4,256,256]{2,1,0:T(8,128)}, f32[4,256,256]{2,1,0:T(8,128)S(1)}, u32[]{:S(2)}) copy-start(f32[4,256,256]{2,1,0:T(8,128)S(1)} %constant_dynamic-update-slice_fusion.7) | copy-start | bytes 3145732
  143.8 1.3 copy-start.7
  145.1 2.2 copy-start.9
  162.4 3.4 %copy-start.11 = (f32[256,256]{0,1:T(8,128)}, f32[256,256]{0,1:T(8,128)S(1)}, u32[]{:S(2)}) copy-start(f32[256,256]{0,1:T(8,128)S(1)} %fusion.165) | copy-start | bytes 786436
  163.6 2.2 copy-start.13
  177.7 108.0 %reduce-scatter.8.cloned.1.call-start = ((), (), s32[]{:S(2)}) async-start(), calls=%async_computation.6 | async-start | bytes 10485760 | tf_op jit(solution)/shard_map/reduce_scatter | solution.py:179
  184.9 2.1 copy-start.6
  184.9 2.1 copy-start.8
  184.9 2.1 copy-start.10
  184.9 2.1 copy-start.12
  184.9 2.1 copy-start.14
  184.9 2.1 copy-start.16
  184.9 2.1 copy-start.18
  189.0 15.9 %collective-permute-start.1 = (f32[3,6,256]{2,1,0:T(8,128)S(1)}, f32[3,6,256]{2,1,0:T(8,128)S(1)}, u32[]{:S(2)}, u32[]{:S(2)}) collective-permute-start(f32[3,6,256]{2,1,0:T(8,128)S(1)} %slice.258), channel_id=1, source_target_pairs={{32,0},{64,32},{96,64},{33,1},{65,33},{97,65},{34,2},{66,34},{98,6... | collective-permute-start | bytes 55304 | tf_op jit(solution)/shard_map/ppermute | solution.py:14
  (7 other events, 6.3 us)
Sparse Core Ops, SparseCore 0:
  13.8 83.6 reduce-scatter.3
  116.2 48.4 all-gather.1
  177.8 22.8 reduce-scatter.5
  203.8 81.8 reduce-scatter.7
where the time goes:
time: 294 us; the launch traced here: 292 us
  waiting for transfers between devices  128 us (44%)
  local copies, waits for them, and re-layouts  49.6 us (17%)
  blocking collectives  42.5 us (14%)
  matrix products  40.1 us (14%)
  between operations  14.6 us (5%)
  other arithmetic  12.1 us (4%)
  starting transfers between devices  5.57 us (2%)
    reduce_scatter x1, waiting for transfers between devices, local(): lax.psum_scatter(weight_terms, 'ctx', scatter_dimension=0, tiled=True)  79.7 us
    reduce_scatter x1, waiting for transfers between devices, local(): lax.psum_scatter(partial_mixed, 'ch', scatter_dimension=1, tiled=True)  47.9 us
    psum x1, blocking collectives, local(): grad_kernel = lax.psum(jnp.stack(kernel_rows, axis=1), 'ctx')  13.9 us
    all_gather x1, blocking collectives, local(): pieces = lax.all_gather(grad_long, 'ctx', axis=0, tiled=True)  9.67 us
    dynamic_slice x6, local copies, waits for them, and re-layouts, local(): old_imag = lax.dynamic_index_in_dim(carry[3], clipped, 0, keepdims=False)  9.54 us
    all_gather x1, blocking collectives, local(): lax.all_gather(long_filter, 'ctx', axis=0, tiled=True).astype(jnp.float32)  9.53 us
    dynamic_slice x6, local copies, waits for them, and re-layouts, local(): old_real = lax.dynamic_index_in_dim(carry[2], clipped, 0, keepdims=False)  9.5 us
    all_gather x1, blocking collectives, local(): pieces = lax.all_gather(gated, 'ctx', axis=0, tiled=True)  9.44 us
  transfers between devices with their start and end apart: 6, of which 2 were waited for; matrix products, arithmetic and copies ran while one was open for 28% of the time, Pallas kernels for 0%

commit v1 on v0

v1 whole, which is shorter than its diff:
```python
import functools
import math

import jax
import jax.numpy as jnp
import numpy as np
from jax import lax
from jax.experimental import pallas as pl
from jax.experimental.pallas import tpu as pltpu
from jax.sharding import PartitionSpec as P

F32 = jnp.float32
BF16 = jnp.bfloat16
NX, NZ, NY, NC = 4, 4, 4, 2
TAPS = 7
NT = (((1,), (1,)), ((), ()))
VMEM_LIMIT = 56 * 1024 * 1024


def coords():
    x = lax.axis_index("ctx")
    ch = lax.axis_index("ch")
    return x, ch // 8, lax.rem(ch // 2, 4), lax.rem(ch, 2)


def flat(x, z, y, c):
    return ((x * NZ + z) * NY + y) * NC + c


def move(array, rule):
    pairs = []
    for x in range(NX):
        for z in range(NZ):
            for y in range(NY):
                for c in range(NC):
                    pairs.append((flat(x, z, y, c), flat(*rule(x, z, y, c))))
    return lax.ppermute(array, ("ctx", "ch"), pairs)


def along_x(array, by):
    return move(array, lambda x, z, y, c: ((x + by) % NX, z, y, c))


def along_z(array, by):
    return move(array, lambda x, z, y, c: (x, (z + by) % NZ, y, c))


def along_y(array, by):
    return move(array, lambda x, z, y, c: (x, z, (y + by) % NY, c))


def other_core(array):
    return move(array, lambda x, z, y, c: (x, z, y, 1 - c))


def turned(array, by):
    return move(array, lambda x, z, y, c: (z, (x + by) % NZ, y, c))


def wave_table(length):
    period = 2 * length
    freq = 2 * np.arange(length) + 1
    steps = np.arange(length)
    angle = (steps[:, None] * freq[None, :] % (2 * period)) * (math.pi / period)
    table = np.concatenate([np.cos(angle), -np.sin(angle)], axis=1)
    high = table.astype(jnp.bfloat16)
    low = (table - high.astype(np.float64)).astype(jnp.bfloat16)
    return high, low


def call(kernel, out_shape, *args, scratch=(), in_specs=None):
    return pl.pallas_call(
        kernel,
        out_shape=out_shape,
        in_specs=in_specs or [pl.BlockSpec(memory_space=pltpu.VMEM)] * len(args),
        out_specs=jax.tree.map(lambda _: pl.BlockSpec(memory_space=pltpu.VMEM), out_shape),
        scratch_shapes=list(scratch),
        compiler_params=pltpu.CompilerParams(vmem_limit_bytes=VMEM_LIMIT),
    )(*args)


def shape(dims, dtype):
    return jax.ShapeDtypeStruct(dims, dtype)


def pack_kernel(feat_ref, filt_ref, taps_ref, p0, p1, p2, p3, taps_out, held, taps_held):
    x = coords()[0]
    for stream in range(4):
        block = feat_ref[stream] if stream < 3 else filt_ref[...]
        flipped = block.T
        for quarter in range(4):
            held[quarter, stream] = flipped[quarter * 64 : quarter * 64 + 64]
    for by, out in enumerate((p0, p1, p2, p3)):
        out[...] = held[lax.rem(x + by, 4)]
    rows = jnp.zeros((128, 256), F32)
    taps_held[0] = rows
    for stream in range(3):
        taps_held[0, stream * 8 : stream * 8 + TAPS, :] = taps_ref[stream]
    columns = taps_held[0].T
    for quarter in range(4):
        taps_held[1 + quarter, 0:64, 0:128] = columns[quarter * 64 : quarter * 64 + 64]
    taps_out[...] = taps_held[1 + x, 0:64, 0:128]


def lift_kernel(g0, g1, g2, g3, weight, whole_out, send_out, gathered, rows, sem):
    x, z, y, c = coords()
    copy = pltpu.make_async_copy(weight.at[:, :, 1 - c, x], rows, sem)
    copy.start()
    for by, block in enumerate((g0, g1, g2, g3)):
        gathered[lax.rem(x + 4 - by, 4)] = block[...]
    whole = gathered[...].reshape(512, 256)
    whole_out[...] = whole
    copy.wait()
    for zd in range(NZ):
        part = lax.dot_general(
            rows[zd].reshape(256, 256), whole, NT, preferred_element_type=F32
        )
        send_out[zd] = part.astype(BF16).reshape(NY, 64, 512)


def sum_core_kernel(recv, whole, weight, own_out, s1, s2, s3, rows, sem):
    x, z, y, c = coords()
    copy = pltpu.make_async_copy(weight.at[:, :, c, x], rows, sem)
    copy.start()
    copy.wait()
    for by, out in enumerate((own_out, s1, s2, s3)):
        zd = lax.rem(z + by, 4)
        part = lax.dot_general(
            rows[zd].reshape(256, 256), whole[...], NT, preferred_element_type=F32
        )
        total = part.reshape(NY, 64, 512) + recv[zd].astype(F32)
        out[...] = total.astype(out.dtype)


def sum_z_kernel(own, r1, r2, r3, own_out, s1, s2, s3):
    y = coords()[2]
    for by, out in enumerate((own_out, s1, s2, s3)):
        yd = lax.rem(y + by, 4)
        total = (
            own[yd] + r1[yd].astype(F32) + (r2[yd].astype(F32) + r3[yd].astype(F32))
        )
        out[...] = total.astype(out.dtype)


def later(values, by, lane):
    if by == 0:
        return values
    return jnp.where(lane >= by, pltpu.roll(values, by, 1), 0.0)


def sooner(values, by, lane):
    if by == 0:
        return values
    return jnp.where(lane < 512 - by, pltpu.roll(values, 512 - by, 1), 0.0)


def split(values):
    high = values.astype(BF16)
    return high, (values - high.astype(F32)).astype(BF16)


def forward(rows, high, low):
    return jnp.dot(rows, high[...], preferred_element_type=F32) + jnp.dot(
        rows, low[...], preferred_element_type=F32
    )


def backward(spectra, high, low):
    count = spectra.shape[0]
    big, small = split(spectra)
    first = lax.dot_general(
        jnp.concatenate([big, small], axis=0), high[...], NT, preferred_element_type=F32
    )
    second = lax.dot_general(big, low[...], NT, preferred_element_type=F32)
    return (first[:count] + first[count:] + second) * (1.0 / 512)


def pre_kernel(p0, r1, r2, r3, taps, high, low, mixed_out, conv_out, long_out, spec_out, feat_out, held):
    x = coords()[0]
    for by, block in enumerate((p0, r1, r2, r3)):
        held[lax.rem(x + 4 - by, 4)] = block[...]
    lane = lax.broadcasted_iota(jnp.int32, (64, 512), 1)
    convs = []
    for stream in range(3):
        feats = jnp.concatenate([held[b, stream] for b in range(4)], axis=1)
        feat_out[stream] = feats
        wide = feats.astype(F32)
        total = taps[:, stream * 8 : stream * 8 + 1] * wide
        for tap in range(1, TAPS):
            column = stream * 8 + tap
            total = total + taps[:, column : column + 1] * later(wide, tap, lane)
        conv_out[stream] = total
        convs.append(total)
    gated = (convs[1] * convs[2]).astype(BF16)
    filt = jnp.concatenate([held[b, 3] for b in range(4)], axis=1)
    spec = forward(jnp.concatenate([gated, filt], axis=0), high, low)
    spec_out[...] = spec
    gr, gi = spec[:64, :512], spec[:64, 512:]
    hr, hi = spec[64:, :512], spec[64:, 512:]
    product = jnp.concatenate([gr * hr - gi * hi, gr * hi + gi * hr], axis=1)
    long = backward(product, high, low)
    long_out[...] = long
    mixed_out[...] = (convs[0] * long).astype(BF16)


def post_kernel(own, r1, r2, r3, conv, long, spec, feats, taps, high, low, o0, o1, o2, o3, held):
    x = coords()[0]
    lane = lax.broadcasted_iota(jnp.int32, (64, 512), 1)
    grad_mixed = own[...] + r1[...].astype(F32) + (r2[...].astype(F32) + r3[...].astype(F32))
    grad_long = (grad_mixed * conv[0]).astype(BF16)
    lspec = forward(grad_long, high, low)
    lr, li = lspec[:, :512], lspec[:, 512:]
    gr, gi = spec[:64, :512], spec[:64, 512:]
    hr, hi = spec[64:, :512], spec[64:, 512:]
    to_gated = jnp.concatenate([hr * lr + hi * li, hr * li - hi * lr], axis=1)
    to_filter = jnp.concatenate([gr * lr + gi * li, gr * li - gi * lr], axis=1)
    both = backward(jnp.concatenate([to_gated, to_filter], axis=0), high, low)
    grad_gated, grad_filter = both[:64], both[64:]
    grad_conv = (grad_mixed * long[...], grad_gated * conv[2], grad_gated * conv[1])
    slot = lax.broadcasted_iota(jnp.int32, (64, 128), 1)
    sums = jnp.zeros((64, 128), F32)
    for stream in range(3):
        wide = feats[stream].astype(F32)
        total = None
        for tap in range(TAPS):
            column = stream * 8 + tap
            term = taps[:, column : column + 1] * sooner(grad_conv[stream], tap, lane)
            total = term if total is None else total + term
            row = jnp.sum(grad_conv[stream] * later(wide, tap, lane), axis=1, keepdims=True)
            sums = jnp.where(slot == column, row, sums)
        rounded = total.astype(BF16)
        for b in range(4):
            held[b, stream] = rounded[:, b * 128 : b * 128 + 128]
    high_part, low_part = split(grad_filter)
    sums_high, sums_low = split(sums)
    sums_both = sums_high.astype(F32) + pltpu.roll(sums_low.astype(F32), 32, 1)
    for b in range(4):
        held[b, 3] = high_part[:, b * 128 : b * 128 + 128]
        held[b, 4] = low_part[:, b * 128 : b * 128 + 128]
        held[b, 5] = sums_both.astype(BF16)
    for by, out in enumerate((o0, o1, o2, o3)):
        out[...] = held[lax.rem(x + by, 4)]


def out_kernel(o0, r1, r2, r3, feat_out, taps_out, filt_out, held):
    x = coords()[0]
    for by, block in enumerate((o0, r1, r2, r3)):
        held[lax.rem(x + 4 - by, 4)] = block[...]
    for stream in range(3):
        columns = jnp.concatenate([held[q, stream] for q in range(4)], axis=0)
        feat_out[stream] = columns.T
    filt = jnp.concatenate(
        [held[q, 3].astype(F32) + held[q, 4].astype(F32) for q in range(4)], axis=0
    )
    filt_out[...] = filt.T
    sums = jnp.concatenate([held[q, 5].astype(F32) for q in range(4)], axis=0)
    sums = sums + pltpu.roll(sums, 96, 1)
    rows = sums.T
    for stream in range(3):
        taps_out[stream] = rows[stream * 8 : stream * 8 + TAPS]


def weight_kernel(mine, theirs, whole, out):
    x, z, y, c = coords()
    for half, block in enumerate((mine, theirs)):
        core = c if half == 0 else 1 - c
        for back in range(4):
            for along in range(4):
                src = lax.rem(z + 4 - back, 4)
                yd = lax.rem(y + 4 - along, 4)
                part = jnp.dot(block[back, along], whole[...], preferred_element_type=F32)
                start = pl.multiple_of(yd * 512 + core * 256 + src * 64, 64)
                out[pl.ds(start, 64), :] = part


def local(high, low, features, short_kernel, long_filter, out_weight, grad_out):
    high, low = jnp.asarray(high), jnp.asarray(low)
    weight = out_weight.reshape(NZ, NY, NC, NX, 64, 256)
    piece = shape((4, 64, 128), BF16)
    g = [grad_out] + [along_x(grad_out, k) for k in (1, 2, 3)]
    *pay, taps = call(
        pack_kernel,
        [piece] * 4 + [shape((64, 128), F32)],
        features,
        long_filter,
        short_kernel,
        scratch=[pltpu.VMEM((4, 4, 64, 128), BF16), pltpu.VMEM((5, 128, 256), F32)],
    )
    got = [pay[0]] + [along_x(pay[k], k) for k in (1, 2, 3)]
    vmem = pl.BlockSpec(memory_space=pltpu.VMEM)
    hbm = pl.BlockSpec(memory_space=pl.ANY)
    whole, send = call(
        lift_kernel,
        [shape((512, 256), BF16), shape((NZ, NY, 64, 512), BF16)],
        *g,
        weight,
        in_specs=[vmem] * 4 + [hbm],
        scratch=[
            pltpu.VMEM((4, 128, 256), BF16),
            pltpu.VMEM((NZ, NY, 64, 256), BF16),
            pltpu.SemaphoreType.DMA,
        ],
    )
    recv = other_core(send)
    own, *sends = call(
        sum_core_kernel,
        [shape((NY, 64, 512), F32)] + [shape((NY, 64, 512), BF16)] * 3,
        recv,
        whole,
        weight,
        in_specs=[vmem, vmem, hbm],
        scratch=[pltpu.VMEM((NZ, NY, 64, 256), BF16), pltpu.SemaphoreType.DMA],
    )
    recvs = [along_z(sends[k - 1], k) for k in (1, 2, 3)]
    mixed, conv, long, spec, feats = call(
        pre_kernel,
        [
            shape((64, 512), BF16),
            shape((3, 64, 512), F32),
            shape((64, 512), F32),
            shape((128, 1024), F32),
            shape((3, 64, 512), BF16),
        ],
        *got,
        taps,
        high,
        low,
        scratch=[pltpu.VMEM((4, 4, 64, 128), BF16)],
    )
    mixed_y = jnp.stack([mixed] + [along_y(mixed, k) for k in (1, 2, 3)])
    own, *sends = call(
        sum_z_kernel,
        [shape((64, 512), F32)] + [shape((64, 512), BF16)] * 3,
        own,
        *recvs,
    )
    recvs = [along_y(sends[k - 1], k) for k in (1, 2, 3)]
    mine = jnp.stack([turned(mixed_y, k) for k in range(4)])
    theirs = other_core(mine)
    piece = shape((6, 64, 128), BF16)
    outs = call(
        post_kernel,
        [piece] * 4,
        own,
        *recvs,
        conv,
        long,
        spec,
        feats,
        taps,
        high,
        low,
        scratch=[pltpu.VMEM((4, 6, 64, 128), BF16)],
    )
    backs = [outs[0]] + [along_x(outs[k], k) for k in (1, 2, 3)]
    grad_features, grad_kernel, grad_filter = call(
        out_kernel,
        [shape((3, 128, 256), BF16), shape((3, TAPS, 256), F32), shape((128, 256), F32)],
        *backs,
        scratch=[pltpu.VMEM((4, 6, 64, 128), BF16)],
    )
    grad_weight = call(weight_kernel, shape((2048, 256), F32), mine, theirs, whole)
    return grad_features, grad_kernel, grad_filter, grad_weight


def solution(mesh):
    high, low = wave_table(512)
    return jax.shard_map(
        functools.partial(local, high, low),
        mesh=mesh,
        in_specs=(
            P(None, "ctx", "ch"),
            P(None, None, "ch"),
            P("ctx", "ch"),
            P(None, "ch"),
            P("ctx", "ch"),
        ),
        out_specs=(P(None, "ctx", "ch"), P(None, None, "ch"), P("ctx", "ch"), P("ctx", "ch")),
        check_vma=False,
    )
```

time: 294 us -> 130 us (0.44)
  waiting for transfers between devices: 128 us -> 56.6 us
  local copies, waits for them, and re-layouts: 49.6 us -> 5.32 us
  blocking collectives: 42.5 us -> 0 us
  matrix products: 40.1 us -> 0 us
  starting transfers between devices: 5.57 us -> 37.9 us
  Pallas kernels: 0 us -> 27.5 us
  between operations: 14.6 us -> 0.81 us
  other arithmetic: 12.1 us -> 0.17 us
    reduce_scatter x3 -> x0, waiting for transfers between devices: 128 us -> none  [the longest x1 79.7 us: local(): lax.psum_scatter(weight_terms, 'ctx', scatter_dimension=0, tiled=True)]
    ppermute x2 -> x24, waiting for transfers between devices: 0.01 us -> 56.6 us  [move(): return lax.ppermute(array, ('ctx', 'ch'), pairs)]
    dot_general x28 -> x0, matrix products: 40.1 us -> none  [the longest x1 6.15 us: local(): jnp.einsum('tn,tc->nc', lax.all_gather(mixed, 'ch', axis=1, tiled=True),...]
    ppermute x2 -> x24, starting transfers between devices: 5.23 us -> 37.9 us  [move(): return lax.ppermute(array, ('ctx', 'ch'), pairs)]
    all_gather x3 -> x0, blocking collectives: 28.6 us -> none  [the longest x1 9.67 us: local(): pieces = lax.all_gather(grad_long, 'ctx', axis=0, tiled=True)]
    pallas_call x0 -> x8, Pallas kernels: none -> 27.5 us  [call(): pl.pallas_call(kernel, out_shape=out_shape, in_specs=in_specs or [pl.Bloc...]
    dynamic_slice x12 -> x0, local copies, waits for them, and re-layouts: 19 us -> none  [the longest x6 9.54 us: local(): old_imag = lax.dynamic_index_in_dim(carry[3], clipped, 0, keepdims=False)]
    psum x1 -> x0, blocking collectives: 13.9 us -> none  [local(): grad_kernel = lax.psum(jnp.stack(kernel_rows, axis=1), 'ctx')]
  transfers between devices with their start and end apart: 6 -> 24, of which waited for: 2 -> 7; matrix products, arithmetic and copies ran while one was open for 28% -> 0% of each run, Pallas kernels for 0% -> 19%
where the time goes in v1:
time: 130 us; the launch traced here: 128 us
  waiting for transfers between devices  56.6 us (44%)
  starting transfers between devices  37.9 us (29%)
  Pallas kernels  27.5 us (21%)
  local copies, waits for them, and re-layouts  5.32 us (4%)
    ppermute x24, waiting for transfers between devices, move(): return lax.ppermute(array, ('ctx', 'ch'), pairs)  56.6 us
    ppermute x24, starting transfers between devices, move(): return lax.ppermute(array, ('ctx', 'ch'), pairs)  37.9 us
    pallas_call x8, Pallas kernels, call(): pl.pallas_call(kernel, out_shape=out_shape, in_specs=in_specs or [pl.Bloc...  27.5 us
    unnamed x38, local copies, waits for them, and re-layouts  5.32 us
  transfers between devices with their start and end apart: 24, of which 7 were waited for; matrix products, arithmetic and copies ran while one was open for 0% of the time, Pallas kernels for 19%

profile of v1, /device:TPU:1, one launch (start us, length us, event | category | flops | bytes accessed | tf_op | source)
XLA Modules:
  0.0 128.3 jit_solution(10998698423003058213)
XLA Ops:
  0.6 1.8 %shard_map.105 = (bf16[4,64,128]{2,1,0:T(8,128)(2,1)}, bf16[4,64,128]{2,1,0:T(8,128)(2,1)}, bf16[4,64,128]{2,1,0:T(8,128)(2,1)}, bf16[4,64,128]{2,1,0:T(8,128)(2,1)}, f32[64,128]{1,0:T(8,128)}) custom-call(bf16[3,128,256]{2,1,0:T(8,128)(2,1)} %feat_ref.1, bf16[128,256]{1,0:T(8,128)(2,1)} %filt_ref.1, f32[3,7,256]{2,1,0:T(8,128)} %taps_ref.1), custom_call_target="tpu_custom_call" | custom-call | tf_op jit(solution)/shard_map/pallas_call | solution.py:72
  2.5 2.0 %collective-permute-start.10 = (bf16[4,64,128]{2,1,0:T(8,128)(2,1)}, bf16[4,64,128]{2,1,0:T(8,128)(2,1)S(1)}, u32[]{:S(2)}, u32[]{:S(2)}) collective-permute-start(bf16[4,64,128]{2,1,0:T(8,128)(2,1)} %get-tuple-element.42), channel_id=1, source_target_pairs={{0,32},{1,33},{2,34},{3,35},{4,36},{5,37},{6,38},{7,39},{8,40},{9,... | collective-permute-start | bytes 196616 | tf_op jit(solution)/shard_map/ppermute | solution.py:37
  4.5 2.5 %collective-permute-start.11 = (bf16[4,64,128]{2,1,0:T(8,128)(2,1)}, bf16[4,64,128]{2,1,0:T(8,128)(2,1)S(1)}, u32[]{:S(2)}, u32[]{:S(2)}) collective-permute-start(bf16[4,64,128]{2,1,0:T(8,128)(2,1)} %get-tuple-element.43), channel_id=1, source_target_pairs={{0,64},{1,65},{2,66},{3,67},{4,68},{5,69},{6,70},{7,71},{8,72},{9,... | collective-permute-start | bytes 196616 | tf_op jit(solution)/shard_map/ppermute | solution.py:37
  7.0 1.2 collective-permute-start.12
  8.4 0.9 collective-permute-start.1
  9.3 1.6 %collective-permute-start.2 = (bf16[128,256]{1,0:T(8,128)(2,1)}, bf16[128,256]{1,0:T(8,128)(2,1)S(1)}, u32[]{:S(2)}, u32[]{:S(2)}) collective-permute-start(bf16[128,256]{1,0:T(8,128)(2,1)} %g0.1), channel_id=1, source_target_pairs={{0,96},{1,97},{2,98},{3,99},{4,100},{5,101},{6,102},{7,103},{8,104... | collective-permute-start | bytes 196616 | tf_op jit(solution)/shard_map/ppermute | solution.py:37
  11.5 4.0 %shard_map.106 = (bf16[64,512]{1,0:T(8,128)(2,1)}, f32[3,64,512]{2,1,0:T(8,128)}, f32[64,512]{1,0:T(8,128)}, f32[128,1024]{1,0:T(8,128)}, bf16[3,64,512]{2,1,0:T(8,128)(2,1)}) custom-call(bf16[4,64,128]{2,1,0:T(8,128)(2,1)} %get-tuple-element.41.p0, bf16[4,64,128]{2,1,0:T(8,128)(2,1)} %copy-done.15, bf16[4,64,128]{2,1,0:T(8,128)(2,1)} %copy-done.16, ...), custom_call_target="tpu_custom_call" | custom-call | tf_op jit(solution)/shard_map/pallas_call | solution.py:72
  15.5 2.7 %collective-permute-start.18 = (bf16[64,512]{1,0:T(8,128)(2,1)}, bf16[64,512]{1,0:T(8,128)(2,1)S(1)}, u32[]{:S(2)}, u32[]{:S(2)}) collective-permute-start(bf16[64,512]{1,0:T(8,128)(2,1)} %get-tuple-element.57), channel_id=1, source_target_pairs={{0,6},{1,7},{2,0},{3,1},{4,2},{5,3},{6,4},{7,5},{8,14},{9,15},{10,... | collective-permute-start | bytes 196616 | tf_op jit(solution)/shard_map/ppermute | solution.py:37
  20.0 3.4 %shard_map.102 = (bf16[512,256]{1,0:T(8,128)(2,1)}, bf16[4,4,64,512]{3,2,1,0:T(8,128)(2,1)}) custom-call(bf16[128,256]{1,0:T(8,128)(2,1)} %g0.1, bf16[128,256]{1,0:T(8,128)(2,1)} %copy-done.9, bf16[128,256]{1,0:T(8,128)(2,1)} %copy-done.10, bf16[128,256]{1,0:T(8,128)(2,1)} %copy-done.11, bf16[4,4,2,4,64,256]{5,4,3,2,1,0:T(8,128)(2,1)} %bitcast.9), custom_call_target="tpu_custom_call" | custom-call | tf_op jit(solution)/shard_map/pallas_call | solution.py:72
  23.4 3.0 %collective-permute-start.3 = (bf16[4,4,64,512]{3,2,1,0:T(8,128)(2,1)}, bf16[4,4,64,512]{3,2,1,0:T(8,128)(2,1)S(1)}, u32[]{:S(2)}, u32[]{:S(2)}) collective-permute-start(bf16[4,4,64,512]{3,2,1,0:T(8,128)(2,1)} %get-tuple-element.31), channel_id=1, source_target_pairs={{0,1},{1,0},{2,3},{3,2},{4,5},{5,4},{6,7},{7,6},{8,9},{9,8},{10,11... | collective-permute-start | bytes 3145736 | tf_op jit(solution)/shard_map/ppermute | solution.py:37
  26.5 3.8 %collective-permute-start.22 = (bf16[4,64,512]{2,1,0:T(8,128)(2,1)S(1)}, bf16[4,64,512]{2,1,0:T(8,128)(2,1)S(1)}, u32[]{:S(2)}, u32[]{:S(2)}) collective-permute-start(bf16[4,64,512]{2,1,0:T(8,128)(2,1)S(1)} %pad_maximum_fusion.1), channel_id=1, source_target_pairs={{0,24},{1,25},{2,26},{3,27},{4,28},{5,29},{6,30},{7,31},{8,56},{9,... | collective-permute-start | bytes 786440 | tf_op jit(solution)/shard_map/ppermute | solution.py:37
  30.3 3.5 %collective-permute-start.21 = (bf16[4,64,512]{2,1,0:T(8,128)(2,1)S(1)}, bf16[4,64,512]{2,1,0:T(8,128)(2,1)S(1)}, u32[]{:S(2)}, u32[]{:S(2)}) collective-permute-start(bf16[4,64,512]{2,1,0:T(8,128)(2,1)S(1)} %pad_maximum_fusion.1), channel_id=1, source_target_pairs={{0,16},{1,17},{2,18},{3,19},{4,20},{5,21},{6,22},{7,23},{8,48},{9,... | collective-permute-start | bytes 786440 | tf_op jit(solution)/shard_map/ppermute | solution.py:37
  34.5 5.3 %collective-permute-done.22 = bf16[4,64,512]{2,1,0:T(8,128)(2,1)S(1)} collective-permute-done((bf16[4,64,512]{2,1,0:T(8,128)(2,1)S(1)}, bf16[4,64,512]{2,1,0:T(8,128)(2,1)S(1)}, u32[]{:S(2)}, u32[]{:S(2)}) %collective-permute-start.22) | collective-permute-done | bytes 262176 | tf_op jit(solution)/shard_map/ppermute | solution.py:37
  39.8 30.4 %collective-permute-done.21 = bf16[4,64,512]{2,1,0:T(8,128)(2,1)S(1)} collective-permute-done((bf16[4,64,512]{2,1,0:T(8,128)(2,1)S(1)}, bf16[4,64,512]{2,1,0:T(8,128)(2,1)S(1)}, u32[]{:S(2)}, u32[]{:S(2)}) %collective-permute-start.21) | collective-permute-done | bytes 262176 | tf_op jit(solution)/shard_map/ppermute | solution.py:37
  70.2 5.6 %collective-permute-done.20 = bf16[4,64,512]{2,1,0:T(8,128)(2,1)S(1)} collective-permute-done((bf16[4,64,512]{2,1,0:T(8,128)(2,1)S(1)}, bf16[4,64,512]{2,1,0:T(8,128)(2,1)S(1)}, u32[]{:S(2)}, u32[]{:S(2)}) %collective-permute-start.20) | collective-permute-done | bytes 262176 | tf_op jit(solution)/shard_map/ppermute | solution.py:37
  76.0 0.7 collective-permute-start.23
  76.7 1.0 copy-done.2
  77.6 3.6 %shard_map.103 = (f32[4,64,512]{2,1,0:T(8,128)}, bf16[4,64,512]{2,1,0:T(8,128)(2,1)}, bf16[4,64,512]{2,1,0:T(8,128)(2,1)}, bf16[4,64,512]{2,1,0:T(8,128)(2,1)}) custom-call(bf16[4,4,64,512]{3,2,1,0:T(8,128)(2,1)} %copy-done.2, bf16[512,256]{1,0:T(8,128)(2,1)} %get-tuple-element.32.whole, bf16[4,4,2,4,64,256]{5,4,3,2,1,0:T(8,128)(2,1)} %bitcast.10), custom_call_target="tpu_custom_call" | custom-call | tf_op jit(solution)/shard_map/pallas_call | solution.py:72
  81.3 2.3 %collective-permute-start.4 = (bf16[4,64,512]{2,1,0:T(8,128)(2,1)}, bf16[4,64,512]{2,1,0:T(8,128)(2,1)S(1)}, u32[]{:S(2)}, u32[]{:S(2)}) collective-permute-start(bf16[4,64,512]{2,1,0:T(8,128)(2,1)} %get-tuple-element.34), channel_id=1, source_target_pairs={{0,8},{1,9},{2,10},{3,11},{4,12},{5,13},{6,14},{7,15},{8,16},{9,17... | collective-permute-start | bytes 786440 | tf_op jit(solution)/shard_map/ppermute | solution.py:37
  83.6 5.0 %collective-permute-start.5 = (bf16[4,64,512]{2,1,0:T(8,128)(2,1)}, bf16[4,64,512]{2,1,0:T(8,128)(2,1)S(1)}, u32[]{:S(2)}, u32[]{:S(2)}) collective-permute-start(bf16[4,64,512]{2,1,0:T(8,128)(2,1)} %get-tuple-element.35), channel_id=1, source_target_pairs={{0,16},{1,17},{2,18},{3,19},{4,20},{5,21},{6,22},{7,23},{8,24},{9,... | collective-permute-start | bytes 786440 | tf_op jit(solution)/shard_map/ppermute | solution.py:37
  88.6 5.6 %collective-permute-done.4.r1 = bf16[4,64,512]{2,1,0:T(8,128)(2,1)S(1)} collective-permute-done((bf16[4,64,512]{2,1,0:T(8,128)(2,1)}, bf16[4,64,512]{2,1,0:T(8,128)(2,1)S(1)}, u32[]{:S(2)}, u32[]{:S(2)}) %collective-permute-start.4) | collective-permute-done | bytes 262176 | tf_op jit(solution)/shard_map/ppermute | solution.py:37
  94.2 6.6 %collective-permute-done.5.r2 = bf16[4,64,512]{2,1,0:T(8,128)(2,1)S(1)} collective-permute-done((bf16[4,64,512]{2,1,0:T(8,128)(2,1)}, bf16[4,64,512]{2,1,0:T(8,128)(2,1)S(1)}, u32[]{:S(2)}, u32[]{:S(2)}) %collective-permute-start.5) | collective-permute-done | bytes 262176 | tf_op jit(solution)/shard_map/ppermute | solution.py:37
  101.6 2.0 %shard_map.104 = (f32[64,512]{1,0:T(8,128)}, bf16[64,512]{1,0:T(8,128)(2,1)}, bf16[64,512]{1,0:T(8,128)(2,1)}, bf16[64,512]{1,0:T(8,128)(2,1)}) custom-call(f32[4,64,512]{2,1,0:T(8,128)} %get-tuple-element.33.own, bf16[4,64,512]{2,1,0:T(8,128)(2,1)} %copy-done.3, bf16[4,64,512]{2,1,0:T(8,128)(2,1)} %copy-done.4, bf16[4,64,512]{2,1,0:T(8,128)(2,1)} %copy-done.5), custom_call_target="tpu_custom_call" | custom-call | tf_op jit(solution)/shard_map/pallas_call | solution.py:72
  103.6 1.6 %collective-permute-start.7 = (bf16[64,512]{1,0:T(8,128)(2,1)}, bf16[64,512]{1,0:T(8,128)(2,1)S(1)}, u32[]{:S(2)}, u32[]{:S(2)}) collective-permute-start(bf16[64,512]{1,0:T(8,128)(2,1)} %get-tuple-element.38), channel_id=1, source_target_pairs={{0,2},{1,3},{2,4},{3,5},{4,6},{5,7},{6,0},{7,1},{8,10},{9,11},{10,... | collective-permute-start | bytes 196616 | tf_op jit(solution)/shard_map/ppermute | solution.py:37
  105.2 1.6 %collective-permute-start.8 = (bf16[64,512]{1,0:T(8,128)(2,1)}, bf16[64,512]{1,0:T(8,128)(2,1)S(1)}, u32[]{:S(2)}, u32[]{:S(2)}) collective-permute-start(bf16[64,512]{1,0:T(8,128)(2,1)} %get-tuple-element.39), channel_id=1, source_target_pairs={{0,4},{1,5},{2,6},{3,7},{4,0},{5,1},{6,2},{7,3},{8,12},{9,13},{10,... | collective-permute-start | bytes 196616 | tf_op jit(solution)/shard_map/ppermute | solution.py:37
  106.7 0.9 collective-permute-start.9
  108.2 2.5 %collective-permute-done.8.r2 = bf16[64,512]{1,0:T(8,128)(2,1)S(1)} collective-permute-done((bf16[64,512]{1,0:T(8,128)(2,1)}, bf16[64,512]{1,0:T(8,128)(2,1)S(1)}, u32[]{:S(2)}, u32[]{:S(2)}) %collective-permute-start.8) | collective-permute-done | bytes 65568 | tf_op jit(solution)/shard_map/ppermute | solution.py:37
  111.3 6.2 %shard_map.107 = (bf16[6,64,128]{2,1,0:T(8,128)(2,1)}, bf16[6,64,128]{2,1,0:T(8,128)(2,1)}, bf16[6,64,128]{2,1,0:T(8,128)(2,1)}, bf16[6,64,128]{2,1,0:T(8,128)(2,1)}) custom-call(f32[64,512]{1,0:T(8,128)} %get-tuple-element.37.own, bf16[64,512]{1,0:T(8,128)(2,1)} %copy-done.12, bf16[64,512]{1,0:T(8,128)(2,1)} %copy-done.13, bf16[64,512]{1,0:T(8,128)(2,1)} %copy-done.14, ...), custom_call_target="tpu_custom_call" | custom-call | tf_op jit(solution)/shard_map/pallas_call | solution.py:72
  118.1 2.2 %collective-permute-start.15 = (bf16[6,64,128]{2,1,0:T(8,128)(2,1)}, bf16[6,64,128]{2,1,0:T(8,128)(2,1)S(1)}, u32[]{:S(2)}, u32[]{:S(2)}) collective-permute-start(bf16[6,64,128]{2,1,0:T(8,128)(2,1)} %get-tuple-element.53), channel_id=1, source_target_pairs={{0,96},{1,97},{2,98},{3,99},{4,100},{5,101},{6,102},{7,103},{8,104... | collective-permute-start | bytes 294920 | tf_op jit(solution)/shard_map/ppermute | solution.py:37
  120.2 1.0 copy-done.1
  121.2 4.5 %shard_map.109 = f32[2048,256]{1,0:T(8,128)} custom-call(bf16[4,4,64,512]{3,2,1,0:T(8,128)(2,1)} %copy-done, bf16[4,4,64,512]{3,2,1,0:T(8,128)(2,1)} %copy-done.1, bf16[512,256]{1,0:T(8,128)(2,1)} %get-tuple-element.32.whole), custom_call_target="tpu_custom_call" | custom-call | tf_op jit(solution)/shard_map/pallas_call | solution.py:72
  126.4 1.9 %shard_map.108 = (bf16[3,128,256]{2,1,0:T(8,128)(2,1)}, f32[3,7,256]{2,1,0:T(8,128)}, f32[128,256]{1,0:T(8,128)}) custom-call(bf16[6,64,128]{2,1,0:T(8,128)(2,1)} %get-tuple-element.50.o0, bf16[6,64,128]{2,1,0:T(8,128)(2,1)} %copy-done.6, bf16[6,64,128]{2,1,0:T(8,128)(2,1)} %copy-done.7, bf16[6,64,128]{2,1,0:T(8,128)(2,1)} %copy-done.8), custom_call_target="tpu_custom_call" | custom-call | tf_op jit(solution)/shard_map/pallas_call | solution.py:72
  (64 shorter events, 6.7 us)
Async XLA Ops:
  2.5 6.8 %collective-permute-start.10 = (bf16[4,64,128]{2,1,0:T(8,128)(2,1)}, bf16[4,64,128]{2,1,0:T(8,128)(2,1)S(1)}, u32[]{:S(2)}, u32[]{:S(2)}) collective-permute-start(bf16[4,64,128]{2,1,0:T(8,128)(2,1)} %get-tuple-element.42), channel_id=1, source_target_pairs={{0,32},{1,33},{2,34},{3,35},{4,36},{5,37},{6,38},{7,39},{8,40},{9,... | collective-permute-start | bytes 196616 | tf_op jit(solution)/shard_map/ppermute | solution.py:37
  4.5 6.4 %collective-permute-start.11 = (bf16[4,64,128]{2,1,0:T(8,128)(2,1)}, bf16[4,64,128]{2,1,0:T(8,128)(2,1)S(1)}, u32[]{:S(2)}, u32[]{:S(2)}) collective-permute-start(bf16[4,64,128]{2,1,0:T(8,128)(2,1)} %get-tuple-element.43), channel_id=1, source_target_pairs={{0,64},{1,65},{2,66},{3,67},{4,68},{5,69},{6,70},{7,71},{8,72},{9,... | collective-permute-start | bytes 196616 | tf_op jit(solution)/shard_map/ppermute | solution.py:37
  7.0 3.9 %collective-permute-start.12 = (bf16[4,64,128]{2,1,0:T(8,128)(2,1)}, bf16[4,64,128]{2,1,0:T(8,128)(2,1)S(1)}, u32[]{:S(2)}, u32[]{:S(2)}) collective-permute-start(bf16[4,64,128]{2,1,0:T(8,128)(2,1)} %get-tuple-element.44), channel_id=1, source_target_pairs={{0,96},{1,97},{2,98},{3,99},{4,100},{5,101},{6,102},{7,103},{8,104... | collective-permute-start | bytes 196616 | tf_op jit(solution)/shard_map/ppermute | solution.py:37
  8.1 10.5 %collective-permute-start = (bf16[128,256]{1,0:T(8,128)(2,1)}, bf16[128,256]{1,0:T(8,128)(2,1)S(1)}, u32[]{:S(2)}, u32[]{:S(2)}) collective-permute-start(bf16[128,256]{1,0:T(8,128)(2,1)} %g0.1), channel_id=1, source_target_pairs={{0,32},{1,33},{2,34},{3,35},{4,36},{5,37},{6,38},{7,39},{8,40},{9,... | collective-permute-start | bytes 196616 | tf_op jit(solution)/shard_map/ppermute | solution.py:37
  8.4 10.9 %collective-permute-start.1 = (bf16[128,256]{1,0:T(8,128)(2,1)}, bf16[128,256]{1,0:T(8,128)(2,1)S(1)}, u32[]{:S(2)}, u32[]{:S(2)}) collective-permute-start(bf16[128,256]{1,0:T(8,128)(2,1)} %g0.1), channel_id=1, source_target_pairs={{0,64},{1,65},{2,66},{3,67},{4,68},{5,69},{6,70},{7,71},{8,72},{9,... | collective-permute-start | bytes 196616 | tf_op jit(solution)/shard_map/ppermute | solution.py:37
  9.3 1.6 %copy-start.15 = (bf16[4,64,128]{2,1,0:T(8,128)(2,1)}, bf16[4,64,128]{2,1,0:T(8,128)(2,1)S(1)}, u32[]{:S(2)}) copy-start(bf16[4,64,128]{2,1,0:T(8,128)(2,1)S(1)} %collective-permute-done.10.r1) | copy-start | bytes 196612
  9.3 10.0 %collective-permute-start.2 = (bf16[128,256]{1,0:T(8,128)(2,1)}, bf16[128,256]{1,0:T(8,128)(2,1)S(1)}, u32[]{:S(2)}, u32[]{:S(2)}) collective-permute-start(bf16[128,256]{1,0:T(8,128)(2,1)} %g0.1), channel_id=1, source_target_pairs={{0,96},{1,97},{2,98},{3,99},{4,100},{5,101},{6,102},{7,103},{8,104... | collective-permute-start | bytes 196616 | tf_op jit(solution)/shard_map/ppermute | solution.py:37
  15.5 10.9 %copy-start.18 = (bf16[64,512]{1,0:T(8,128)(2,1)S(1)}, bf16[64,512]{1,0:T(8,128)(2,1)}, u32[]{:S(2)}) copy-start(bf16[64,512]{1,0:T(8,128)(2,1)} %get-tuple-element.57) | copy-start | bytes 196612
  15.5 10.9 %collective-permute-start.18 = (bf16[64,512]{1,0:T(8,128)(2,1)}, bf16[64,512]{1,0:T(8,128)(2,1)S(1)}, u32[]{:S(2)}, u32[]{:S(2)}) collective-permute-start(bf16[64,512]{1,0:T(8,128)(2,1)} %get-tuple-element.57), channel_id=1, source_target_pairs={{0,6},{1,7},{2,0},{3,1},{4,2},{5,3},{6,4},{7,5},{8,14},{9,15},{10,... | collective-permute-start | bytes 196616 | tf_op jit(solution)/shard_map/ppermute | solution.py:37
  18.3 8.1 %collective-permute-start.17 = (bf16[64,512]{1,0:T(8,128)(2,1)}, bf16[64,512]{1,0:T(8,128)(2,1)S(1)}, u32[]{:S(2)}, u32[]{:S(2)}) collective-permute-start(bf16[64,512]{1,0:T(8,128)(2,1)} %get-tuple-element.57), channel_id=1, source_target_pairs={{0,4},{1,5},{2,6},{3,7},{4,0},{5,1},{6,2},{7,3},{8,12},{9,13},{10,... | collective-permute-start | bytes 196616 | tf_op jit(solution)/shard_map/ppermute | solution.py:37
  18.6 7.8 %collective-permute-start.16 = (bf16[64,512]{1,0:T(8,128)(2,1)}, bf16[64,512]{1,0:T(8,128)(2,1)S(1)}, u32[]{:S(2)}, u32[]{:S(2)}) collective-permute-start(bf16[64,512]{1,0:T(8,128)(2,1)} %get-tuple-element.57), channel_id=1, source_target_pairs={{0,2},{1,3},{2,4},{3,5},{4,6},{5,7},{6,0},{7,1},{8,10},{9,11},{10,... | collective-permute-start | bytes 196616 | tf_op jit(solution)/shard_map/ppermute | solution.py:37
  23.4 53.3 %collective-permute-start.3 = (bf16[4,4,64,512]{3,2,1,0:T(8,128)(2,1)}, bf16[4,4,64,512]{3,2,1,0:T(8,128)(2,1)S(1)}, u32[]{:S(2)}, u32[]{:S(2)}) collective-permute-start(bf16[4,4,64,512]{3,2,1,0:T(8,128)(2,1)} %get-tuple-element.31), channel_id=1, source_target_pairs={{0,1},{1,0},{2,3},{3,2},{4,5},{5,4},{6,7},{7,6},{8,9},{9,8},{10,11... | collective-permute-start | bytes 3145736 | tf_op jit(solution)/shard_map/ppermute | solution.py:37
  26.5 13.3 %collective-permute-start.22 = (bf16[4,64,512]{2,1,0:T(8,128)(2,1)S(1)}, bf16[4,64,512]{2,1,0:T(8,128)(2,1)S(1)}, u32[]{:S(2)}, u32[]{:S(2)}) collective-permute-start(bf16[4,64,512]{2,1,0:T(8,128)(2,1)S(1)} %pad_maximum_fusion.1), channel_id=1, source_target_pairs={{0,24},{1,25},{2,26},{3,27},{4,28},{5,29},{6,30},{7,31},{8,56},{9,... | collective-permute-start | bytes 786440 | tf_op jit(solution)/shard_map/ppermute | solution.py:37
  30.3 39.9 %collective-permute-start.21 = (bf16[4,64,512]{2,1,0:T(8,128)(2,1)S(1)}, bf16[4,64,512]{2,1,0:T(8,128)(2,1)S(1)}, u32[]{:S(2)}, u32[]{:S(2)}) collective-permute-start(bf16[4,64,512]{2,1,0:T(8,128)(2,1)S(1)} %pad_maximum_fusion.1), channel_id=1, source_target_pairs={{0,16},{1,17},{2,18},{3,19},{4,20},{5,21},{6,22},{7,23},{8,48},{9,... | collective-permute-start | bytes 786440 | tf_op jit(solution)/shard_map/ppermute | solution.py:37
  33.8 42.0 %collective-permute-start.20 = (bf16[4,64,512]{2,1,0:T(8,128)(2,1)S(1)}, bf16[4,64,512]{2,1,0:T(8,128)(2,1)S(1)}, u32[]{:S(2)}, u32[]{:S(2)}) collective-permute-start(bf16[4,64,512]{2,1,0:T(8,128)(2,1)S(1)} %pad_maximum_fusion.1), channel_id=1, source_target_pairs={{0,8},{1,9},{2,10},{3,11},{4,12},{5,13},{6,14},{7,15},{8,40},{9,41... | collective-permute-start | bytes 786440 | tf_op jit(solution)/shard_map/ppermute | solution.py:37
  33.8 42.0 %collective-permute-start.19 = (bf16[4,64,512]{2,1,0:T(8,128)(2,1)S(1)}, bf16[4,64,512]{2,1,0:T(8,128)(2,1)S(1)}, u32[]{:S(2)}, u32[]{:S(2)}) collective-permute-start(bf16[4,64,512]{2,1,0:T(8,128)(2,1)S(1)} %pad_maximum_fusion.1), channel_id=1, source_target_pairs={{0,0},{1,1},{2,2},{3,3},{4,4},{5,5},{6,6},{7,7},{8,32},{9,33},{10,... | collective-permute-start | bytes 786440 | tf_op jit(solution)/shard_map/ppermute | solution.py:37
  76.0 41.5 %copy-start = (bf16[4,4,64,512]{3,2,1,0:T(8,128)(2,1)}, bf16[4,4,64,512]{3,2,1,0:T(8,128)(2,1)S(1)}, u32[]{:S(2)}) copy-start(bf16[4,4,64,512]{3,2,1,0:T(8,128)(2,1)S(1)} %pad_maximum_fusion.mine) | copy-start | bytes 3145732
  76.0 44.3 %collective-permute-start.23 = (bf16[4,4,64,512]{3,2,1,0:T(8,128)(2,1)S(1)}, bf16[4,4,64,512]{3,2,1,0:T(8,128)(2,1)S(1)}, u32[]{:S(2)}, u32[]{:S(2)}) collective-permute-start(bf16[4,4,64,512]{3,2,1,0:T(8,128)(2,1)S(1)} %pad_maximum_fusion.mine), channel_id=1, source_target_pairs={{0,1},{1,0},{2,3},{3,2},{4,5},{5,4},{6,7},{7,6},{8,9},{9,8},{10,11... | collective-permute-start | bytes 3145736 | tf_op jit(solution)/shard_map/ppermute | solution.py:37
  76.7 1.0 copy-start.2
  81.3 12.9 %collective-permute-start.4 = (bf16[4,64,512]{2,1,0:T(8,128)(2,1)}, bf16[4,64,512]{2,1,0:T(8,128)(2,1)S(1)}, u32[]{:S(2)}, u32[]{:S(2)}) collective-permute-start(bf16[4,64,512]{2,1,0:T(8,128)(2,1)} %get-tuple-element.34), channel_id=1, source_target_pairs={{0,8},{1,9},{2,10},{3,11},{4,12},{5,13},{6,14},{7,15},{8,16},{9,17... | collective-permute-start | bytes 786440 | tf_op jit(solution)/shard_map/ppermute | solution.py:37
  83.6 17.2 %collective-permute-start.5 = (bf16[4,64,512]{2,1,0:T(8,128)(2,1)}, bf16[4,64,512]{2,1,0:T(8,128)(2,1)S(1)}, u32[]{:S(2)}, u32[]{:S(2)}) collective-permute-start(bf16[4,64,512]{2,1,0:T(8,128)(2,1)} %get-tuple-element.35), channel_id=1, source_target_pairs={{0,16},{1,17},{2,18},{3,19},{4,20},{5,21},{6,22},{7,23},{8,24},{9,... | collective-permute-start | bytes 786440 | tf_op jit(solution)/shard_map/ppermute | solution.py:37
  88.6 12.2 %collective-permute-start.6 = (bf16[4,64,512]{2,1,0:T(8,128)(2,1)}, bf16[4,64,512]{2,1,0:T(8,128)(2,1)S(1)}, u32[]{:S(2)}, u32[]{:S(2)}) collective-permute-start(bf16[4,64,512]{2,1,0:T(8,128)(2,1)} %get-tuple-element.36), channel_id=1, source_target_pairs={{0,24},{1,25},{2,26},{3,27},{4,28},{5,29},{6,30},{7,31},{8,0},{9,1... | collective-permute-start | bytes 786440 | tf_op jit(solution)/shard_map/ppermute | solution.py:37
  94.2 6.6 %copy-start.3 = (bf16[4,64,512]{2,1,0:T(8,128)(2,1)}, bf16[4,64,512]{2,1,0:T(8,128)(2,1)S(1)}, u32[]{:S(2)}) copy-start(bf16[4,64,512]{2,1,0:T(8,128)(2,1)S(1)} %collective-permute-done.4.r1) | copy-start | bytes 786436
  100.8 0.8 copy-start.5
  103.6 4.5 %collective-permute-start.7 = (bf16[64,512]{1,0:T(8,128)(2,1)}, bf16[64,512]{1,0:T(8,128)(2,1)S(1)}, u32[]{:S(2)}, u32[]{:S(2)}) collective-permute-start(bf16[64,512]{1,0:T(8,128)(2,1)} %get-tuple-element.38), channel_id=1, source_target_pairs={{0,2},{1,3},{2,4},{3,5},{4,6},{5,7},{6,0},{7,1},{8,10},{9,11},{10,... | collective-permute-start | bytes 196616 | tf_op jit(solution)/shard_map/ppermute | solution.py:37
  105.2 5.5 %collective-permute-start.8 = (bf16[64,512]{1,0:T(8,128)(2,1)}, bf16[64,512]{1,0:T(8,128)(2,1)S(1)}, u32[]{:S(2)}, u32[]{:S(2)}) collective-permute-start(bf16[64,512]{1,0:T(8,128)(2,1)} %get-tuple-element.39), channel_id=1, source_target_pairs={{0,4},{1,5},{2,6},{3,7},{4,0},{5,1},{6,2},{7,3},{8,12},{9,13},{10,... | collective-permute-start | bytes 196616 | tf_op jit(solution)/shard_map/ppermute | solution.py:37
  106.7 3.9 %collective-permute-start.9 = (bf16[64,512]{1,0:T(8,128)(2,1)}, bf16[64,512]{1,0:T(8,128)(2,1)S(1)}, u32[]{:S(2)}, u32[]{:S(2)}) collective-permute-start(bf16[64,512]{1,0:T(8,128)(2,1)} %get-tuple-element.40), channel_id=1, source_target_pairs={{0,6},{1,7},{2,0},{3,1},{4,2},{5,3},{6,4},{7,5},{8,14},{9,15},{10,... | collective-permute-start | bytes 196616 | tf_op jit(solution)/shard_map/ppermute | solution.py:37
  108.2 2.5 %copy-start.12 = (bf16[64,512]{1,0:T(8,128)(2,1)}, bf16[64,512]{1,0:T(8,128)(2,1)S(1)}, u32[]{:S(2)}) copy-start(bf16[64,512]{1,0:T(8,128)(2,1)S(1)} %collective-permute-done.7.r1) | copy-start | bytes 196612
  117.5 8.2 %collective-permute-start.13 = (bf16[6,64,128]{2,1,0:T(8,128)(2,1)}, bf16[6,64,128]{2,1,0:T(8,128)(2,1)S(1)}, u32[]{:S(2)}, u32[]{:S(2)}) collective-permute-start(bf16[6,64,128]{2,1,0:T(8,128)(2,1)} %get-tuple-element.51), channel_id=1, source_target_pairs={{0,32},{1,33},{2,34},{3,35},{4,36},{5,37},{6,38},{7,39},{8,40},{9,... | collective-permute-start | bytes 294920 | tf_op jit(solution)/shard_map/ppermute | solution.py:37
  117.6 8.1 %collective-permute-start.14 = (bf16[6,64,128]{2,1,0:T(8,128)(2,1)}, bf16[6,64,128]{2,1,0:T(8,128)(2,1)S(1)}, u32[]{:S(2)}, u32[]{:S(2)}) collective-permute-start(bf16[6,64,128]{2,1,0:T(8,128)(2,1)} %get-tuple-element.52), channel_id=1, source_target_pairs={{0,64},{1,65},{2,66},{3,67},{4,68},{5,69},{6,70},{7,71},{8,72},{9,... | collective-permute-start | bytes 294920 | tf_op jit(solution)/shard_map/ppermute | solution.py:37
  118.1 7.7 %collective-permute-start.15 = (bf16[6,64,128]{2,1,0:T(8,128)(2,1)}, bf16[6,64,128]{2,1,0:T(8,128)(2,1)S(1)}, u32[]{:S(2)}, u32[]{:S(2)}) collective-permute-start(bf16[6,64,128]{2,1,0:T(8,128)(2,1)} %get-tuple-element.53), channel_id=1, source_target_pairs={{0,96},{1,97},{2,98},{3,99},{4,100},{5,101},{6,102},{7,103},{8,104... | collective-permute-start | bytes 294920 | tf_op jit(solution)/shard_map/ppermute | solution.py:37
  120.2 1.0 copy-start.1
  (11 other events, 7.2 us)

commit v2 on v1

--- a/solution.py
+++ b/solution.py
@@ -14,7 +14,8 @@
 NX, NZ, NY, NC = 4, 4, 4, 2
 TAPS = 7
 NT = (((1,), (1,)), ((), ()))
-VMEM_LIMIT = 56 * 1024 * 1024
+VMEM_LIMIT = 20 * 1024 * 1024
+WEIGHT = 3.5e10
 
 
 def coords():
@@ -53,8 +54,8 @@
     return move(array, lambda x, z, y, c: (x, z, y, 1 - c))
 
 
-def turned(array, by):
-    return move(array, lambda x, z, y, c: (z, (x + by) % NZ, y, c))
+def turned(array):
+    return move(array, lambda x, z, y, c: (z, x, y, c))
 
 
 def wave_table(length):
@@ -68,19 +69,34 @@
     return high, low
 
 
-def call(kernel, out_shape, *args, scratch=(), in_specs=None):
+def call(kernel, out_shape, *args, scratch=(), in_hbm=(), time=2.0):
+    specs, operands = [], []
+    for place, arg in enumerate(args):
+        if place in in_hbm:
+            specs.append(pl.BlockSpec(memory_space=pl.ANY))
+            operands.append(pltpu.with_memory_space_constraint(arg, pltpu.HBM))
+        else:
+            specs.append(pl.BlockSpec(memory_space=pltpu.VMEM))
+            operands.append(pltpu.with_memory_space_constraint(arg, pltpu.VMEM))
     return pl.pallas_call(
         kernel,
         out_shape=out_shape,
-        in_specs=in_specs or [pl.BlockSpec(memory_space=pltpu.VMEM)] * len(args),
+        in_specs=specs,
         out_specs=jax.tree.map(lambda _: pl.BlockSpec(memory_space=pltpu.VMEM), out_shape),
         scratch_shapes=list(scratch),
+        cost_estimate=pl.CostEstimate(
+            flops=int(time * WEIGHT), transcendentals=0, bytes_accessed=int(time * 3.5e6)
+        ),
         compiler_params=pltpu.CompilerParams(vmem_limit_bytes=VMEM_LIMIT),
-    )(*args)
+    )(*operands)
 
 
 def shape(dims, dtype):
     return jax.ShapeDtypeStruct(dims, dtype)
+
+
+def kept(dims, dtype):
+    return pltpu.VMEM(dims, dtype)
 
 
 def pack_kernel(feat_ref, filt_ref, taps_ref, p0, p1, p2, p3, taps_out, held, taps_held):
@@ -102,7 +118,7 @@
     taps_out[...] = taps_held[1 + x, 0:64, 0:128]
 
 
-def lift_kernel(g0, g1, g2, g3, weight, whole_out, send_out, gathered, rows, sem):
+def lift_kernel(g0, g1, g2, g3, weight, behind, whole_out, send_out, gathered, rows, sem):
     x, z, y, c = coords()
     copy = pltpu.make_async_copy(weight.at[:, :, 1 - c, x], rows, sem)
     copy.start()
@@ -175,7 +191,7 @@
     return (first[:count] + first[count:] + second) * (1.0 / 512)
 
 
-def pre_kernel(p0, r1, r2, r3, taps, high, low, mixed_out, conv_out, long_out, spec_out, feat_out, held):
+def pre_kernel(p0, r1, r2, r3, taps, high, low, behind, mixed_out, conv_out, long_out, spec_out, feat_out, held):
     x = coords()[0]
     for by, block in enumerate((p0, r1, r2, r3)):
         held[lax.rem(x + 4 - by, 4)] = block[...]
@@ -262,39 +278,39 @@
 
 def weight_kernel(mine, theirs, whole, out):
     x, z, y, c = coords()
-    for half, block in enumerate((mine, theirs)):
+    for half, blocks in enumerate((mine, theirs)):
         core = c if half == 0 else 1 - c
-        for back in range(4):
+        for across in range(4):
+            src = lax.rem(z + 4 - across, 4)
+            part = jnp.dot(
+                blocks[across].reshape(256, 512), whole[...], preferred_element_type=F32
+            )
             for along in range(4):
-                src = lax.rem(z + 4 - back, 4)
                 yd = lax.rem(y + 4 - along, 4)
-                part = jnp.dot(block[back, along], whole[...], preferred_element_type=F32)
                 start = pl.multiple_of(yd * 512 + core * 256 + src * 64, 64)
-                out[pl.ds(start, 64), :] = part
+                out[pl.ds(start, 64), :] = part[along * 64 : along * 64 + 64]
 
 
 def local(high, low, features, short_kernel, long_filter, out_weight, grad_out):
     high, low = jnp.asarray(high), jnp.asarray(low)
     weight = out_weight.reshape(NZ, NY, NC, NX, 64, 256)
-    piece = shape((4, 64, 128), BF16)
     g = [grad_out] + [along_x(grad_out, k) for k in (1, 2, 3)]
     *pay, taps = call(
         pack_kernel,
-        [piece] * 4 + [shape((64, 128), F32)],
+        [kept((4, 64, 128), BF16)] * 4 + [kept((64, 128), F32)],
         features,
         long_filter,
         short_kernel,
         scratch=[pltpu.VMEM((4, 4, 64, 128), BF16), pltpu.VMEM((5, 128, 256), F32)],
     )
     got = [pay[0]] + [along_x(pay[k], k) for k in (1, 2, 3)]
-    vmem = pl.BlockSpec(memory_space=pltpu.VMEM)
-    hbm = pl.BlockSpec(memory_space=pl.ANY)
     whole, send = call(
         lift_kernel,
-        [shape((512, 256), BF16), shape((NZ, NY, 64, 512), BF16)],
+        [kept((512, 256), BF16), kept((NZ, NY, 64, 512), BF16)],
         *g,
         weight,
-        in_specs=[vmem] * 4 + [hbm],
+        taps,
+        in_hbm=(4,),
         scratch=[
             pltpu.VMEM((4, 128, 256), BF16),
             pltpu.VMEM((NZ, NY, 64, 256), BF16),
@@ -304,43 +320,45 @@
     recv = other_core(send)
     own, *sends = call(
         sum_core_kernel,
-        [shape((NY, 64, 512), F32)] + [shape((NY, 64, 512), BF16)] * 3,
+        [kept((NY, 64, 512), F32)] + [kept((NY, 64, 512), BF16)] * 3,
         recv,
         whole,
         weight,
-        in_specs=[vmem, vmem, hbm],
+        in_hbm=(2,),
         scratch=[pltpu.VMEM((NZ, NY, 64, 256), BF16), pltpu.SemaphoreType.DMA],
     )
     recvs = [along_z(sends[k - 1], k) for k in (1, 2, 3)]
     mixed, conv, long, spec, feats = call(
         pre_kernel,
         [
-            shape((64, 512), BF16),
-            shape((3, 64, 512), F32),
-            shape((64, 512), F32),
-            shape((128, 1024), F32),
-            shape((3, 64, 512), BF16),
+            kept((64, 512), BF16),
+            kept((3, 64, 512), F32),
+            kept((64, 512), F32),
+            kept((128, 1024), F32),
+            kept((3, 64, 512), BF16),
         ],
         *got,
         taps,
         high,
         low,
+        sends[2],
         scratch=[pltpu.VMEM((4, 4, 64, 128), BF16)],
-    )
-    mixed_y = jnp.stack([mixed] + [along_y(mixed, k) for k in (1, 2, 3)])
+        time=3.0,
+    )
+    moved = turned(mixed)
+    column = jnp.stack([moved] + [along_y(moved, k) for k in (1, 2, 3)])
+    mine = jnp.stack([column] + [along_z(column, k) for k in (1, 2, 3)])
+    theirs = other_core(mine)
     own, *sends = call(
         sum_z_kernel,
-        [shape((64, 512), F32)] + [shape((64, 512), BF16)] * 3,
+        [kept((64, 512), F32)] + [kept((64, 512), BF16)] * 3,
         own,
         *recvs,
     )
     recvs = [along_y(sends[k - 1], k) for k in (1, 2, 3)]
-    mine = jnp.stack([turned(mixed_y, k) for k in range(4)])
-    theirs = other_core(mine)
-    piece = shape((6, 64, 128), BF16)
     outs = call(
         post_kernel,
-        [piece] * 4,
+        [kept((6, 64, 128), BF16)] * 4,
         own,
         *recvs,
         conv,
@@ -351,6 +369,7 @@
         high,
         low,
         scratch=[pltpu.VMEM((4, 6, 64, 128), BF16)],
+        time=5.0,
     )
     backs = [outs[0]] + [along_x(outs[k], k) for k in (1, 2, 3)]
     grad_features, grad_kernel, grad_filter = call(
@@ -359,7 +378,7 @@
         *backs,
         scratch=[pltpu.VMEM((4, 6, 64, 128), BF16)],
     )
-    grad_weight = call(weight_kernel, shape((2048, 256), F32), mine, theirs, whole)
+    grad_weight = call(weight_kernel, shape((2048, 256), F32), mine, theirs, whole, time=3.0)
     return grad_features, grad_kernel, grad_filter, grad_weight
 
 

time: 130 us -> 65.5 us (0.50)
  waiting for transfers between devices: 56.6 us -> 8.86 us
  Pallas kernels: 27.5 us -> 11.4 us
  local copies, waits for them, and re-layouts: 5.32 us -> 3.14 us
  other arithmetic: 0.17 us -> 2.08 us
    ppermute x24, waiting for transfers between devices: 56.6 us -> 8.86 us  [move(): return lax.ppermute(array, ('ctx', 'ch'), pairs)]
    pallas_call x8, Pallas kernels: 27.5 us -> 11.4 us  [call(): pl.pallas_call(kernel, out_shape=out_shape, in_specs=specs, out_specs=jax...]
    unnamed x38 -> x18, local copies, waits for them, and re-layouts: 5.32 us -> 3.14 us
    another operation x2, other arithmetic: 0.17 us -> 2.08 us  [local(): mine = jnp.stack([column] + [along_z(column, k) for k in (1, 2, 3)])]
  transfers between devices with their start and end apart: 24 -> 24, of which waited for: 7 -> 4; matrix products, arithmetic and copies ran while one was open for 0% -> 3% of each run, Pallas kernels for 19% -> 12%
where the time goes in v2:
time: 65.5 us; the launch traced here: 65.1 us
  starting transfers between devices  38.8 us (59%)
  Pallas kernels  11.4 us (17%)
  waiting for transfers between devices  8.86 us (14%)
  local copies, waits for them, and re-layouts  3.14 us (5%)
  other arithmetic  2.08 us (3%)
  between operations  0.79 us (1%)
    ppermute x24, starting transfers between devices, move(): return lax.ppermute(array, ('ctx', 'ch'), pairs)  38.8 us
    pallas_call x8, Pallas kernels, call(): pl.pallas_call(kernel, out_shape=out_shape, in_specs=specs, out_specs=jax...  11.4 us
    ppermute x24, waiting for transfers between devices, move(): return lax.ppermute(array, ('ctx', 'ch'), pairs)  8.86 us
    unnamed x18, local copies, waits for them, and re-layouts  3.14 us
    another operation x2, other arithmetic, local(): mine = jnp.stack([column] + [along_z(column, k) for k in (1, 2, 3)])  2.08 us
  transfers between devices with their start and end apart: 24, of which 4 were waited for; matrix products, arithmetic and copies ran while one was open for 3% of the time, Pallas kernels for 12%

profile of v2, /device:TPU:1, one launch (start us, length us, event | category | flops | bytes accessed | tf_op | source)
XLA Modules:
  0.0 65.1 jit_solution(12941967123147336636)
XLA Ops:
  0.6 3.7 %collective-permute-start.1 = (bf16[128,256]{1,0:T(8,128)(2,1)}, bf16[128,256]{1,0:T(8,128)(2,1)S(1)}, u32[]{:S(2)}, u32[]{:S(2)}) collective-permute-start(bf16[128,256]{1,0:T(8,128)(2,1)} %g0.1), channel_id=1, source_target_pairs={{0,64},{1,65},{2,66},{3,67},{4,68},{5,69},{6,70},{7,71},{8,72},{9,... | collective-permute-start | bytes 196616 | tf_op jit(solution)/shard_map/ppermute | solution.py:38
  4.6 2.4 %collective-permute-start.2 = (bf16[128,256]{1,0:T(8,128)(2,1)}, bf16[128,256]{1,0:T(8,128)(2,1)S(1)}, u32[]{:S(2)}, u32[]{:S(2)}) collective-permute-start(bf16[128,256]{1,0:T(8,128)(2,1)} %g0.1), channel_id=1, source_target_pairs={{0,96},{1,97},{2,98},{3,99},{4,100},{5,101},{6,102},{7,103},{8,104... | collective-permute-start | bytes 196616 | tf_op jit(solution)/shard_map/ppermute | solution.py:38
  7.0 0.9 %copy-done = bf16[3,128,256]{2,1,0:T(8,128)(2,1)S(1)} copy-done((bf16[3,128,256]{2,1,0:T(8,128)(2,1)S(1)}, bf16[3,128,256]{2,1,0:T(8,128)(2,1)}, u32[]{:S(2)}) %copy-start) | copy-done | bytes 196632
  7.9 0.8 %copy-done.1 = bf16[128,256]{1,0:T(8,128)(2,1)S(1)} copy-done((bf16[128,256]{1,0:T(8,128)(2,1)S(1)}, bf16[128,256]{1,0:T(8,128)(2,1)}, u32[]{:S(2)}) %copy-start.1) | copy-done | bytes 65560
  8.7 0.7 %copy-done.3 = f32[3,7,256]{2,1,0:T(8,128)S(1)} copy-done((f32[3,7,256]{2,1,0:T(8,128)S(1)}, f32[3,7,256]{2,1,0:T(8,128)}, u32[]{:S(2)}) %copy-start.3) | copy-done | bytes 21528
  10.3 1.5 %shard_map.103 = (bf16[512,256]{1,0:T(8,128)(2,1)S(1)}, bf16[4,4,64,512]{3,2,1,0:T(8,128)(2,1)S(1)}) custom-call(bf16[128,256]{1,0:T(8,128)(2,1)S(1)} %copy-done.2, bf16[128,256]{1,0:T(8,128)(2,1)S(1)} %collective-permute-done.g1, bf16[128,256]{1,0:T(8,128)(2,1)S(1)} %collective-permute-done.1.g2, bf16[128,256]{1,0:T(8,128)(2,1)S(1)} %collective-permute-done.2.g3, ...), custom_call_target="tpu_custom_call" | custom-call | flops 70000001024 | bytes 7000000 | tf_op jit(solution)/shard_map/pallas_call | solution.py:81
  11.9 1.6 %collective-permute-start.3 = (bf16[4,4,64,512]{3,2,1,0:T(8,128)(2,1)S(1)}, bf16[4,4,64,512]{3,2,1,0:T(8,128)(2,1)S(1)}, u32[]{:S(2)}, u32[]{:S(2)}) collective-permute-start(bf16[4,4,64,512]{3,2,1,0:T(8,128)(2,1)S(1)} %get-tuple-element.32), channel_id=1, source_target_pairs={{0,1},{1,0},{2,3},{3,2},{4,5},{5,4},{6,7},{7,6},{8,9},{9,8},{10,11... | collective-permute-start | bytes 3145736 | tf_op jit(solution)/shard_map/ppermute | solution.py:38
  13.5 3.3 %collective-permute-start.11 = (bf16[4,64,128]{2,1,0:T(8,128)(2,1)S(1)}, bf16[4,64,128]{2,1,0:T(8,128)(2,1)S(1)}, u32[]{:S(2)}, u32[]{:S(2)}) collective-permute-start(bf16[4,64,128]{2,1,0:T(8,128)(2,1)S(1)} %get-tuple-element.44), channel_id=1, source_target_pairs={{0,64},{1,65},{2,66},{3,67},{4,68},{5,69},{6,70},{7,71},{8,72},{9,... | collective-permute-start | bytes 196616 | tf_op jit(solution)/shard_map/ppermute | solution.py:38
  16.7 1.7 %shard_map.104 = (f32[4,64,512]{2,1,0:T(8,128)S(1)}, bf16[4,64,512]{2,1,0:T(8,128)(2,1)S(1)}, bf16[4,64,512]{2,1,0:T(8,128)(2,1)S(1)}, bf16[4,64,512]{2,1,0:T(8,128)(2,1)S(1)}) custom-call(bf16[4,4,64,512]{3,2,1,0:T(8,128)(2,1)S(1)} %collective-permute-done.3.recv, bf16[512,256]{1,0:T(8,128)(2,1)S(1)} %get-tuple-element.33.whole, ...), custom_call_target="tpu_custom_call" | custom-call | flops 70000001024 | bytes 7000000 | tf_op jit(solution)/shard_map/pallas_call | solution.py:81
  18.4 1.7 %collective-permute-start.4 = (bf16[4,64,512]{2,1,0:T(8,128)(2,1)S(1)}, bf16[4,64,512]{2,1,0:T(8,128)(2,1)S(1)}, u32[]{:S(2)}, u32[]{:S(2)}) collective-permute-start(bf16[4,64,512]{2,1,0:T(8,128)(2,1)S(1)} %get-tuple-element.35), channel_id=1, source_target_pairs={{0,8},{1,9},{2,10},{3,11},{4,12},{5,13},{6,14},{7,15},{8,16},{9,17... | collective-permute-start | bytes 786440 | tf_op jit(solution)/shard_map/ppermute | solution.py:38
  20.1 3.3 %collective-permute-start.5 = (bf16[4,64,512]{2,1,0:T(8,128)(2,1)S(1)}, bf16[4,64,512]{2,1,0:T(8,128)(2,1)S(1)}, u32[]{:S(2)}, u32[]{:S(2)}) collective-permute-start(bf16[4,64,512]{2,1,0:T(8,128)(2,1)S(1)} %get-tuple-element.36), channel_id=1, source_target_pairs={{0,16},{1,17},{2,18},{3,19},{4,20},{5,21},{6,22},{7,23},{8,24},{9,... | collective-permute-start | bytes 786440 | tf_op jit(solution)/shard_map/ppermute | solution.py:38
  23.5 0.7 %collective-permute-start.6 = (bf16[4,64,512]{2,1,0:T(8,128)(2,1)S(1)}, bf16[4,64,512]{2,1,0:T(8,128)(2,1)S(1)}, u32[]{:S(2)}, u32[]{:S(2)}) collective-permute-start(bf16[4,64,512]{2,1,0:T(8,128)(2,1)S(1)} %get-tuple-element.37.behind), channel_id=1, source_target_pairs={{0,24},{1,25},{2,26},{3,27},{4,28},{5,29},{6,30},{7,31},{8,0},{9,1... | collective-permute-start | bytes 786440 | tf_op jit(solution)/shard_map/ppermute | solution.py:38
  24.2 1.7 %shard_map.106 = (bf16[64,512]{1,0:T(8,128)(2,1)S(1)}, f32[3,64,512]{2,1,0:T(8,128)S(1)}, f32[64,512]{1,0:T(8,128)S(1)}, f32[128,1024]{1,0:T(8,128)S(1)}, bf16[3,64,512]{2,1,0:T(8,128)(2,1)S(1)}) custom-call(bf16[4,64,128]{2,1,0:T(8,128)(2,1)S(1)} %get-tuple-element.42.p0, bf16[4,64,128]{2,1,0:T(8,128)(2,1)S(1)} %collective-permute-done.10.r1, ...), custom_call_target="tpu_custom_call" | custom-call | flops 105000001536 | bytes 10500000 | tf_op jit(solution)/shard_map/pallas_call | solution.py:81
  26.6 2.8 %collective-permute-start.19 = (bf16[64,512]{1,0:T(8,128)(2,1)S(1)}, bf16[64,512]{1,0:T(8,128)(2,1)S(1)}, u32[]{:S(2)}, u32[]{:S(2)}) collective-permute-start(bf16[64,512]{1,0:T(8,128)(2,1)S(1)} %collective-permute-done.16), channel_id=1, source_target_pairs={{0,6},{1,7},{2,0},{3,1},{4,2},{5,3},{6,4},{7,5},{8,14},{9,15},{10,... | collective-permute-start | bytes 196616 | tf_op jit(solution)/shard_map/ppermute | solution.py:38
  29.7 0.7 %collective-permute-start.17 = (bf16[64,512]{1,0:T(8,128)(2,1)S(1)}, bf16[64,512]{1,0:T(8,128)(2,1)S(1)}, u32[]{:S(2)}, u32[]{:S(2)}) collective-permute-start(bf16[64,512]{1,0:T(8,128)(2,1)S(1)} %collective-permute-done.16), channel_id=1, source_target_pairs={{0,2},{1,3},{2,4},{3,5},{4,6},{5,7},{6,0},{7,1},{8,10},{9,11},{10,... | collective-permute-start | bytes 196616 | tf_op jit(solution)/shard_map/ppermute | solution.py:38
  30.4 4.4 %collective-permute-done.5.r2 = bf16[4,64,512]{2,1,0:T(8,128)(2,1)S(1)} collective-permute-done((bf16[4,64,512]{2,1,0:T(8,128)(2,1)S(1)}, bf16[4,64,512]{2,1,0:T(8,128)(2,1)S(1)}, u32[]{:S(2)}, u32[]{:S(2)}) %collective-permute-start.5) | collective-permute-done | bytes 262176 | tf_op jit(solution)/shard_map/ppermute | solution.py:38
  34.8 0.9 %collective-permute-done.6.r3 = bf16[4,64,512]{2,1,0:T(8,128)(2,1)S(1)} collective-permute-done((bf16[4,64,512]{2,1,0:T(8,128)(2,1)S(1)}, bf16[4,64,512]{2,1,0:T(8,128)(2,1)S(1)}, u32[]{:S(2)}, u32[]{:S(2)}) %collective-permute-start.6) | collective-permute-done | bytes 262176 | tf_op jit(solution)/shard_map/ppermute | solution.py:38
  35.8 1.4 %collective-permute-start.7 = (bf16[64,512]{1,0:T(8,128)(2,1)S(1)}, bf16[64,512]{1,0:T(8,128)(2,1)S(1)}, u32[]{:S(2)}, u32[]{:S(2)}) collective-permute-start(bf16[64,512]{1,0:T(8,128)(2,1)S(1)} %get-tuple-element.39), channel_id=1, source_target_pairs={{0,2},{1,3},{2,4},{3,5},{4,6},{5,7},{6,0},{7,1},{8,10},{9,11},{10,... | collective-permute-start | bytes 196616 | tf_op jit(solution)/shard_map/ppermute | solution.py:38
  37.2 2.6 %collective-permute-start.8 = (bf16[64,512]{1,0:T(8,128)(2,1)S(1)}, bf16[64,512]{1,0:T(8,128)(2,1)S(1)}, u32[]{:S(2)}, u32[]{:S(2)}) collective-permute-start(bf16[64,512]{1,0:T(8,128)(2,1)S(1)} %get-tuple-element.40), channel_id=1, source_target_pairs={{0,4},{1,5},{2,6},{3,7},{4,0},{5,1},{6,2},{7,3},{8,12},{9,13},{10,... | collective-permute-start | bytes 196616 | tf_op jit(solution)/shard_map/ppermute | solution.py:38
  39.8 1.1 %collective-permute-start.9 = (bf16[64,512]{1,0:T(8,128)(2,1)S(1)}, bf16[64,512]{1,0:T(8,128)(2,1)S(1)}, u32[]{:S(2)}, u32[]{:S(2)}) collective-permute-start(bf16[64,512]{1,0:T(8,128)(2,1)S(1)} %get-tuple-element.41), channel_id=1, source_target_pairs={{0,6},{1,7},{2,0},{3,1},{4,2},{5,3},{6,4},{7,5},{8,14},{9,15},{10,... | collective-permute-start | bytes 196616 | tf_op jit(solution)/shard_map/ppermute | solution.py:38
  40.9 0.8 %fusion = (bf16[1,4,64,512]{3,2,1,0:T(8,128)(2,1)}, bf16[4,64,512]{2,1,0:T(8,128)(2,1)}) fusion(bf16[1,64,512]{2,1,0:T(8,128)(2,1)S(1)} %bitcast.11, bf16[1,64,512]{2,1,0:T(8,128)(2,1)S(1)} %bitcast.12, bf16[1,64,512]{2,1,0:T(8,128)(2,1)S(1)} %bitcast.13, bf16[1,64,512]{2,1,0:T(8,128)(2,1)S(1)} %bitcast.10), kind=kLoop, calls=%fused_computation.2 | loop fusion | flops 393216 | bytes 786432 | tf_op jit(solution)/shard_map/stack | solution.py:350
  41.7 2.7 %collective-permute-start.21 = (bf16[4,64,512]{2,1,0:T(8,128)(2,1)}, bf16[4,64,512]{2,1,0:T(8,128)(2,1)}, u32[]{:S(2)}, u32[]{:S(2)}) collective-permute-start(bf16[4,64,512]{2,1,0:T(8,128)(2,1)} %get-tuple-element.59), channel_id=1, source_target_pairs={{0,16},{1,17},{2,18},{3,19},{4,20},{5,21},{6,22},{7,23},{8,24},{9,... | collective-permute-start | bytes 786440 | tf_op jit(solution)/shard_map/ppermute | solution.py:38
  44.4 1.3 %collective-permute-start.20 = (bf16[4,64,512]{2,1,0:T(8,128)(2,1)}, bf16[4,64,512]{2,1,0:T(8,128)(2,1)}, u32[]{:S(2)}, u32[]{:S(2)}) collective-permute-start(bf16[4,64,512]{2,1,0:T(8,128)(2,1)} %get-tuple-element.59), channel_id=1, source_target_pairs={{0,8},{1,9},{2,10},{3,11},{4,12},{5,13},{6,14},{7,15},{8,16},{9,17... | collective-permute-start | bytes 786440 | tf_op jit(solution)/shard_map/ppermute | solution.py:38
  45.7 1.4 %collective-permute-start.22 = (bf16[4,64,512]{2,1,0:T(8,128)(2,1)}, bf16[4,64,512]{2,1,0:T(8,128)(2,1)}, u32[]{:S(2)}, u32[]{:S(2)}) collective-permute-start(bf16[4,64,512]{2,1,0:T(8,128)(2,1)} %get-tuple-element.59), channel_id=1, source_target_pairs={{0,24},{1,25},{2,26},{3,27},{4,28},{5,29},{6,30},{7,31},{8,0},{9,1... | collective-permute-start | bytes 786440 | tf_op jit(solution)/shard_map/ppermute | solution.py:38
  47.1 3.3 %shard_map.107 = (bf16[6,64,128]{2,1,0:T(8,128)(2,1)S(1)}, bf16[6,64,128]{2,1,0:T(8,128)(2,1)S(1)}, bf16[6,64,128]{2,1,0:T(8,128)(2,1)S(1)}, bf16[6,64,128]{2,1,0:T(8,128)(2,1)S(1)}) custom-call(f32[64,512]{1,0:T(8,128)S(1)} %get-tuple-element.38.own, bf16[64,512]{1,0:T(8,128)(2,1)S(1)} %collective-permute-done.7.r1, ...), custom_call_target="tpu_custom_call" | custom-call | flops 174999994368 | bytes 17500000 | tf_op jit(solution)/shard_map/pallas_call | solution.py:81
  50.6 3.4 %collective-permute-start.14 = (bf16[6,64,128]{2,1,0:T(8,128)(2,1)S(1)}, bf16[6,64,128]{2,1,0:T(8,128)(2,1)S(1)}, u32[]{:S(2)}, u32[]{:S(2)}) collective-permute-start(bf16[6,64,128]{2,1,0:T(8,128)(2,1)S(1)} %get-tuple-element.52), channel_id=1, source_target_pairs={{0,64},{1,65},{2,66},{3,67},{4,68},{5,69},{6,70},{7,71},{8,72},{9,... | collective-permute-start | bytes 294920 | tf_op jit(solution)/shard_map/ppermute | solution.py:38
  54.0 2.1 %collective-permute-done.22 = bf16[4,64,512]{2,1,0:T(8,128)(2,1)} collective-permute-done((bf16[4,64,512]{2,1,0:T(8,128)(2,1)}, bf16[4,64,512]{2,1,0:T(8,128)(2,1)}, u32[]{:S(2)}, u32[]{:S(2)}) %collective-permute-start.22) | collective-permute-done | bytes 262176 | tf_op jit(solution)/shard_map/ppermute | solution.py:38
  56.1 1.2 %pad_maximum_fusion.mine = bf16[4,4,64,512]{3,2,1,0:T(8,128)(2,1)S(1)} fusion(bf16[1,4,64,512]{3,2,1,0:T(8,128)(2,1)} %bitcast.8, bf16[1,4,64,512]{3,2,1,0:T(8,128)(2,1)} %bitcast.7, bf16[1,4,64,512]{3,2,1,0:T(8,128)(2,1)} %bitcast.6, bf16[1,4,64,512]{3,2,1,0:T(8,128)(2,1)S(1)} %copy-done.8), kind=kLoop, calls=%fused_computation | loop fusion | flops 1572864 | bytes 2097152 | tf_op jit(solution)/shard_map/stack | solution.py:350
  57.3 3.4 %collective-permute-start.23 = (bf16[4,4,64,512]{3,2,1,0:T(8,128)(2,1)S(1)}, bf16[4,4,64,512]{3,2,1,0:T(8,128)(2,1)S(1)}, u32[]{:S(2)}, u32[]{:S(2)}) collective-permute-start(bf16[4,4,64,512]{3,2,1,0:T(8,128)(2,1)S(1)} %pad_maximum_fusion.mine), channel_id=1, source_target_pairs={{0,1},{1,0},{2,3},{3,2},{4,5},{5,4},{6,7},{7,6},{8,9},{9,8},{10,11... | collective-permute-start | bytes 3145736 | tf_op jit(solution)/shard_map/ppermute | solution.py:38
  60.8 0.9 %shard_map.108 = (bf16[3,128,256]{2,1,0:T(8,128)(2,1)}, f32[3,7,256]{2,1,0:T(8,128)}, f32[128,256]{1,0:T(8,128)}) custom-call(bf16[6,64,128]{2,1,0:T(8,128)(2,1)S(1)} %get-tuple-element.50.o0, bf16[6,64,128]{2,1,0:T(8,128)(2,1)S(1)} %collective-permute-done.13.r1, bf16[6,64,128]{2,1,0:T(8,128)(2,1)S(1)} %collective-permute-done.14.r2, ...), custom_call_target="tpu_custom_call" | custom-call | flops 70000001024 | bytes 7000000 | tf_op jit(solution)/shard_map/pallas_call | solution.py:81
  61.7 1.4 %collective-permute-done.23.theirs = bf16[4,4,64,512]{3,2,1,0:T(8,128)(2,1)S(1)} collective-permute-done((bf16[4,4,64,512]{3,2,1,0:T(8,128)(2,1)S(1)}, bf16[4,4,64,512]{3,2,1,0:T(8,128)(2,1)S(1)}, u32[]{:S(2)}, u32[]{:S(2)}) %collective-permute-start.23) | collective-permute-done | bytes 1048608 | tf_op jit(solution)/shard_map/ppermute | solution.py:38
  63.1 2.1 %shard_map.109 = f32[2048,256]{1,0:T(8,128)} custom-call(bf16[4,4,64,512]{3,2,1,0:T(8,128)(2,1)S(1)} %pad_maximum_fusion.mine, bf16[4,4,64,512]{3,2,1,0:T(8,128)(2,1)S(1)} %collective-permute-done.23.theirs, bf16[512,256]{1,0:T(8,128)(2,1)S(1)} %copy-done.7), custom_call_target="tpu_custom_call" | custom-call | flops 105000001536 | bytes 10500000 | tf_op jit(solution)/shard_map/pallas_call | solution.py:81
  (44 shorter events, 2.4 us)
Async XLA Ops:
  0.6 9.0 %collective-permute-start.1 = (bf16[128,256]{1,0:T(8,128)(2,1)}, bf16[128,256]{1,0:T(8,128)(2,1)S(1)}, u32[]{:S(2)}, u32[]{:S(2)}) collective-permute-start(bf16[128,256]{1,0:T(8,128)(2,1)} %g0.1), channel_id=1, source_target_pairs={{0,64},{1,65},{2,66},{3,67},{4,68},{5,69},{6,70},{7,71},{8,72},{9,... | collective-permute-start | bytes 196616 | tf_op jit(solution)/shard_map/ppermute | solution.py:38
  4.3 5.4 %collective-permute-start = (bf16[128,256]{1,0:T(8,128)(2,1)}, bf16[128,256]{1,0:T(8,128)(2,1)S(1)}, u32[]{:S(2)}, u32[]{:S(2)}) collective-permute-start(bf16[128,256]{1,0:T(8,128)(2,1)} %g0.1), channel_id=1, source_target_pairs={{0,32},{1,33},{2,34},{3,35},{4,36},{5,37},{6,38},{7,39},{8,40},{9,... | collective-permute-start | bytes 196616 | tf_op jit(solution)/shard_map/ppermute | solution.py:38
  4.6 5.1 %collective-permute-start.2 = (bf16[128,256]{1,0:T(8,128)(2,1)}, bf16[128,256]{1,0:T(8,128)(2,1)S(1)}, u32[]{:S(2)}, u32[]{:S(2)}) collective-permute-start(bf16[128,256]{1,0:T(8,128)(2,1)} %g0.1), channel_id=1, source_target_pairs={{0,96},{1,97},{2,98},{3,99},{4,100},{5,101},{6,102},{7,103},{8,104... | collective-permute-start | bytes 196616 | tf_op jit(solution)/shard_map/ppermute | solution.py:38
  7.0 0.9 %copy-start = (bf16[3,128,256]{2,1,0:T(8,128)(2,1)S(1)}, bf16[3,128,256]{2,1,0:T(8,128)(2,1)}, u32[]{:S(2)}) copy-start(bf16[3,128,256]{2,1,0:T(8,128)(2,1)} %feat_ref.1) | copy-start | bytes 589828
  7.9 0.8 %copy-start.1 = (bf16[128,256]{1,0:T(8,128)(2,1)S(1)}, bf16[128,256]{1,0:T(8,128)(2,1)}, u32[]{:S(2)}) copy-start(bf16[128,256]{1,0:T(8,128)(2,1)} %filt_ref.1) | copy-start | bytes 196612
  9.5 0.8 %copy-start.2 = (bf16[128,256]{1,0:T(8,128)(2,1)S(1)}, bf16[128,256]{1,0:T(8,128)(2,1)}, u32[]{:S(2)}) copy-start(bf16[128,256]{1,0:T(8,128)(2,1)} %g0.1) | copy-start | bytes 196612
  11.8 6.6 %copy-start.6 = (bf16[512,256]{1,0:T(8,128)(2,1)}, bf16[512,256]{1,0:T(8,128)(2,1)S(1)}, u32[]{:S(2)}) copy-start(bf16[512,256]{1,0:T(8,128)(2,1)S(1)} %get-tuple-element.33.whole) | copy-start | bytes 786436
  11.9 4.9 %collective-permute-start.3 = (bf16[4,4,64,512]{3,2,1,0:T(8,128)(2,1)S(1)}, bf16[4,4,64,512]{3,2,1,0:T(8,128)(2,1)S(1)}, u32[]{:S(2)}, u32[]{:S(2)}) collective-permute-start(bf16[4,4,64,512]{3,2,1,0:T(8,128)(2,1)S(1)} %get-tuple-element.32), channel_id=1, source_target_pairs={{0,1},{1,0},{2,3},{3,2},{4,5},{5,4},{6,7},{7,6},{8,9},{9,8},{10,11... | collective-permute-start | bytes 3145736 | tf_op jit(solution)/shard_map/ppermute | solution.py:38
  13.5 10.0 %collective-permute-start.10 = (bf16[4,64,128]{2,1,0:T(8,128)(2,1)S(1)}, bf16[4,64,128]{2,1,0:T(8,128)(2,1)S(1)}, u32[]{:S(2)}, u32[]{:S(2)}) collective-permute-start(bf16[4,64,128]{2,1,0:T(8,128)(2,1)S(1)} %get-tuple-element.43), channel_id=1, source_target_pairs={{0,32},{1,33},{2,34},{3,35},{4,36},{5,37},{6,38},{7,39},{8,40},{9,... | collective-permute-start | bytes 196616 | tf_op jit(solution)/shard_map/ppermute | solution.py:38
  13.5 10.7 %collective-permute-start.11 = (bf16[4,64,128]{2,1,0:T(8,128)(2,1)S(1)}, bf16[4,64,128]{2,1,0:T(8,128)(2,1)S(1)}, u32[]{:S(2)}, u32[]{:S(2)}) collective-permute-start(bf16[4,64,128]{2,1,0:T(8,128)(2,1)S(1)} %get-tuple-element.44), channel_id=1, source_target_pairs={{0,64},{1,65},{2,66},{3,67},{4,68},{5,69},{6,70},{7,71},{8,72},{9,... | collective-permute-start | bytes 196616 | tf_op jit(solution)/shard_map/ppermute | solution.py:38
  16.7 7.5 %collective-permute-start.12 = (bf16[4,64,128]{2,1,0:T(8,128)(2,1)S(1)}, bf16[4,64,128]{2,1,0:T(8,128)(2,1)S(1)}, u32[]{:S(2)}, u32[]{:S(2)}) collective-permute-start(bf16[4,64,128]{2,1,0:T(8,128)(2,1)S(1)} %get-tuple-element.45), channel_id=1, source_target_pairs={{0,96},{1,97},{2,98},{3,99},{4,100},{5,101},{6,102},{7,103},{8,104... | collective-permute-start | bytes 196616 | tf_op jit(solution)/shard_map/ppermute | solution.py:38
  16.7 7.5 %copy-start.4 = (bf16[512,1024]{1,0:T(8,128)(2,1)S(1)}, bf16[512,1024]{1,0:T(8,128)(2,1)}, u32[]{:S(2)}) copy-start(bf16[512,1024]{1,0:T(8,128)(2,1)} %constant.5.clone.low) | copy-start | bytes 3145732
  16.7 7.5 %copy-start.5 = (bf16[512,1024]{1,0:T(8,128)(2,1)S(1)}, bf16[512,1024]{1,0:T(8,128)(2,1)}, u32[]{:S(2)}) copy-start(bf16[512,1024]{1,0:T(8,128)(2,1)} %constant.4.clone.high) | copy-start | bytes 3145732
  18.4 11.3 %collective-permute-start.4 = (bf16[4,64,512]{2,1,0:T(8,128)(2,1)S(1)}, bf16[4,64,512]{2,1,0:T(8,128)(2,1)S(1)}, u32[]{:S(2)}, u32[]{:S(2)}) collective-permute-start(bf16[4,64,512]{2,1,0:T(8,128)(2,1)S(1)} %get-tuple-element.35), channel_id=1, source_target_pairs={{0,8},{1,9},{2,10},{3,11},{4,12},{5,13},{6,14},{7,15},{8,16},{9,17... | collective-permute-start | bytes 786440 | tf_op jit(solution)/shard_map/ppermute | solution.py:38
  20.1 14.7 %collective-permute-start.5 = (bf16[4,64,512]{2,1,0:T(8,128)(2,1)S(1)}, bf16[4,64,512]{2,1,0:T(8,128)(2,1)S(1)}, u32[]{:S(2)}, u32[]{:S(2)}) collective-permute-start(bf16[4,64,512]{2,1,0:T(8,128)(2,1)S(1)} %get-tuple-element.36), channel_id=1, source_target_pairs={{0,16},{1,17},{2,18},{3,19},{4,20},{5,21},{6,22},{7,23},{8,24},{9,... | collective-permute-start | bytes 786440 | tf_op jit(solution)/shard_map/ppermute | solution.py:38
  23.5 12.2 %collective-permute-start.6 = (bf16[4,64,512]{2,1,0:T(8,128)(2,1)S(1)}, bf16[4,64,512]{2,1,0:T(8,128)(2,1)S(1)}, u32[]{:S(2)}, u32[]{:S(2)}) collective-permute-start(bf16[4,64,512]{2,1,0:T(8,128)(2,1)S(1)} %get-tuple-element.37.behind), channel_id=1, source_target_pairs={{0,24},{1,25},{2,26},{3,27},{4,28},{5,29},{6,30},{7,31},{8,0},{9,1... | collective-permute-start | bytes 786440 | tf_op jit(solution)/shard_map/ppermute | solution.py:38
  25.9 0.7 %collective-permute-start.16 = (bf16[64,512]{1,0:T(8,128)(2,1)S(1)}, bf16[64,512]{1,0:T(8,128)(2,1)S(1)}, u32[]{:S(2)}, u32[]{:S(2)}) collective-permute-start(bf16[64,512]{1,0:T(8,128)(2,1)S(1)} %get-tuple-element.57), channel_id=1, source_target_pairs={{0,0},{1,1},{2,2},{3,3},{4,4},{5,5},{6,6},{7,7},{8,32},{9,33},{10,... | collective-permute-start | bytes 196616 | tf_op jit(solution)/shard_map/ppermute | solution.py:38
  26.6 13.3 %collective-permute-start.19 = (bf16[64,512]{1,0:T(8,128)(2,1)S(1)}, bf16[64,512]{1,0:T(8,128)(2,1)S(1)}, u32[]{:S(2)}, u32[]{:S(2)}) collective-permute-start(bf16[64,512]{1,0:T(8,128)(2,1)S(1)} %collective-permute-done.16), channel_id=1, source_target_pairs={{0,6},{1,7},{2,0},{3,1},{4,2},{5,3},{6,4},{7,5},{8,14},{9,15},{10,... | collective-permute-start | bytes 196616 | tf_op jit(solution)/shard_map/ppermute | solution.py:38
  29.4 11.5 %collective-permute-start.18 = (bf16[64,512]{1,0:T(8,128)(2,1)S(1)}, bf16[64,512]{1,0:T(8,128)(2,1)S(1)}, u32[]{:S(2)}, u32[]{:S(2)}) collective-permute-start(bf16[64,512]{1,0:T(8,128)(2,1)S(1)} %collective-permute-done.16), channel_id=1, source_target_pairs={{0,4},{1,5},{2,6},{3,7},{4,0},{5,1},{6,2},{7,3},{8,12},{9,13},{10,... | collective-permute-start | bytes 196616 | tf_op jit(solution)/shard_map/ppermute | solution.py:38
  29.7 11.2 %collective-permute-start.17 = (bf16[64,512]{1,0:T(8,128)(2,1)S(1)}, bf16[64,512]{1,0:T(8,128)(2,1)S(1)}, u32[]{:S(2)}, u32[]{:S(2)}) collective-permute-start(bf16[64,512]{1,0:T(8,128)(2,1)S(1)} %collective-permute-done.16), channel_id=1, source_target_pairs={{0,2},{1,3},{2,4},{3,5},{4,6},{5,7},{6,0},{7,1},{8,10},{9,11},{10,... | collective-permute-start | bytes 196616 | tf_op jit(solution)/shard_map/ppermute | solution.py:38
  35.8 9.9 %collective-permute-start.7 = (bf16[64,512]{1,0:T(8,128)(2,1)S(1)}, bf16[64,512]{1,0:T(8,128)(2,1)S(1)}, u32[]{:S(2)}, u32[]{:S(2)}) collective-permute-start(bf16[64,512]{1,0:T(8,128)(2,1)S(1)} %get-tuple-element.39), channel_id=1, source_target_pairs={{0,2},{1,3},{2,4},{3,5},{4,6},{5,7},{6,0},{7,1},{8,10},{9,11},{10,... | collective-permute-start | bytes 196616 | tf_op jit(solution)/shard_map/ppermute | solution.py:38
  37.2 9.9 %collective-permute-start.8 = (bf16[64,512]{1,0:T(8,128)(2,1)S(1)}, bf16[64,512]{1,0:T(8,128)(2,1)S(1)}, u32[]{:S(2)}, u32[]{:S(2)}) collective-permute-start(bf16[64,512]{1,0:T(8,128)(2,1)S(1)} %get-tuple-element.40), channel_id=1, source_target_pairs={{0,4},{1,5},{2,6},{3,7},{4,0},{5,1},{6,2},{7,3},{8,12},{9,13},{10,... | collective-permute-start | bytes 196616 | tf_op jit(solution)/shard_map/ppermute | solution.py:38
  39.8 7.3 %collective-permute-start.9 = (bf16[64,512]{1,0:T(8,128)(2,1)S(1)}, bf16[64,512]{1,0:T(8,128)(2,1)S(1)}, u32[]{:S(2)}, u32[]{:S(2)}) collective-permute-start(bf16[64,512]{1,0:T(8,128)(2,1)S(1)} %get-tuple-element.41), channel_id=1, source_target_pairs={{0,6},{1,7},{2,0},{3,1},{4,2},{5,3},{6,4},{7,5},{8,14},{9,15},{10,... | collective-permute-start | bytes 196616 | tf_op jit(solution)/shard_map/ppermute | solution.py:38
  41.7 12.2 %collective-permute-start.21 = (bf16[4,64,512]{2,1,0:T(8,128)(2,1)}, bf16[4,64,512]{2,1,0:T(8,128)(2,1)}, u32[]{:S(2)}, u32[]{:S(2)}) collective-permute-start(bf16[4,64,512]{2,1,0:T(8,128)(2,1)} %get-tuple-element.59), channel_id=1, source_target_pairs={{0,16},{1,17},{2,18},{3,19},{4,20},{5,21},{6,22},{7,23},{8,24},{9,... | collective-permute-start | bytes 786440 | tf_op jit(solution)/shard_map/ppermute | solution.py:38
  44.4 9.5 %collective-permute-start.20 = (bf16[4,64,512]{2,1,0:T(8,128)(2,1)}, bf16[4,64,512]{2,1,0:T(8,128)(2,1)}, u32[]{:S(2)}, u32[]{:S(2)}) collective-permute-start(bf16[4,64,512]{2,1,0:T(8,128)(2,1)} %get-tuple-element.59), channel_id=1, source_target_pairs={{0,8},{1,9},{2,10},{3,11},{4,12},{5,13},{6,14},{7,15},{8,16},{9,17... | collective-permute-start | bytes 786440 | tf_op jit(solution)/shard_map/ppermute | solution.py:38
  45.7 10.4 %collective-permute-start.22 = (bf16[4,64,512]{2,1,0:T(8,128)(2,1)}, bf16[4,64,512]{2,1,0:T(8,128)(2,1)}, u32[]{:S(2)}, u32[]{:S(2)}) collective-permute-start(bf16[4,64,512]{2,1,0:T(8,128)(2,1)} %get-tuple-element.59), channel_id=1, source_target_pairs={{0,24},{1,25},{2,26},{3,27},{4,28},{5,29},{6,30},{7,31},{8,0},{9,1... | collective-permute-start | bytes 786440 | tf_op jit(solution)/shard_map/ppermute | solution.py:38
  47.1 9.0 %copy-start.8 = (bf16[1,4,64,512]{3,2,1,0:T(8,128)(2,1)S(1)}, bf16[1,4,64,512]{3,2,1,0:T(8,128)(2,1)}, u32[]{:S(2)}) copy-start(bf16[1,4,64,512]{3,2,1,0:T(8,128)(2,1)} %get-tuple-element.58) | copy-start | bytes 786436
  50.5 10.3 %collective-permute-start.13 = (bf16[6,64,128]{2,1,0:T(8,128)(2,1)S(1)}, bf16[6,64,128]{2,1,0:T(8,128)(2,1)S(1)}, u32[]{:S(2)}, u32[]{:S(2)}) collective-permute-start(bf16[6,64,128]{2,1,0:T(8,128)(2,1)S(1)} %get-tuple-element.51), channel_id=1, source_target_pairs={{0,32},{1,33},{2,34},{3,35},{4,36},{5,37},{6,38},{7,39},{8,40},{9,... | collective-permute-start | bytes 294920 | tf_op jit(solution)/shard_map/ppermute | solution.py:38
  50.6 10.2 %collective-permute-start.14 = (bf16[6,64,128]{2,1,0:T(8,128)(2,1)S(1)}, bf16[6,64,128]{2,1,0:T(8,128)(2,1)S(1)}, u32[]{:S(2)}, u32[]{:S(2)}) collective-permute-start(bf16[6,64,128]{2,1,0:T(8,128)(2,1)S(1)} %get-tuple-element.52), channel_id=1, source_target_pairs={{0,64},{1,65},{2,66},{3,67},{4,68},{5,69},{6,70},{7,71},{8,72},{9,... | collective-permute-start | bytes 294920 | tf_op jit(solution)/shard_map/ppermute | solution.py:38
  53.9 6.8 %collective-permute-start.15 = (bf16[6,64,128]{2,1,0:T(8,128)(2,1)S(1)}, bf16[6,64,128]{2,1,0:T(8,128)(2,1)S(1)}, u32[]{:S(2)}, u32[]{:S(2)}) collective-permute-start(bf16[6,64,128]{2,1,0:T(8,128)(2,1)S(1)} %get-tuple-element.53), channel_id=1, source_target_pairs={{0,96},{1,97},{2,98},{3,99},{4,100},{5,101},{6,102},{7,103},{8,104... | collective-permute-start | bytes 294920 | tf_op jit(solution)/shard_map/ppermute | solution.py:38
  57.3 5.7 %collective-permute-start.23 = (bf16[4,4,64,512]{3,2,1,0:T(8,128)(2,1)S(1)}, bf16[4,4,64,512]{3,2,1,0:T(8,128)(2,1)S(1)}, u32[]{:S(2)}, u32[]{:S(2)}) collective-permute-start(bf16[4,4,64,512]{3,2,1,0:T(8,128)(2,1)S(1)} %pad_maximum_fusion.mine), channel_id=1, source_target_pairs={{0,1},{1,0},{2,3},{3,2},{4,5},{5,4},{6,7},{7,6},{8,9},{9,8},{10,11... | collective-permute-start | bytes 3145736 | tf_op jit(solution)/shard_map/ppermute | solution.py:38
  60.8 2.3 %copy-start.7 = (bf16[512,256]{1,0:T(8,128)(2,1)S(1)}, bf16[512,256]{1,0:T(8,128)(2,1)}, u32[]{:S(2)}) copy-start(bf16[512,256]{1,0:T(8,128)(2,1)} %copy-done.6) | copy-start | bytes 786436
  (1 other events, 0.7 us)

commit v3 on v2

--- a/solution.py
+++ b/solution.py
@@ -81,6 +81,7 @@
     return pl.pallas_call(
         kernel,
         out_shape=out_shape,
+        name=kernel.__name__,
         in_specs=specs,
         out_specs=jax.tree.map(lambda _: pl.BlockSpec(memory_space=pltpu.VMEM), out_shape),
         scratch_shapes=list(scratch),
@@ -99,17 +100,52 @@
     return pltpu.VMEM(dims, dtype)
 
 
-def pack_kernel(feat_ref, filt_ref, taps_ref, p0, p1, p2, p3, taps_out, held, taps_held):
+def pack_kernel(
+    feat_hbm,
+    filt_hbm,
+    taps_hbm,
+    grad_hbm,
+    p0,
+    p1,
+    p2,
+    p3,
+    taps_out,
+    feat_ref,
+    filt_ref,
+    taps_ref,
+    grad_ref,
+    held,
+    taps_held,
+    sems,
+):
     x = coords()[0]
+    copies = []
+    for place, (src, dst) in enumerate(
+        (
+            (feat_hbm, feat_ref),
+            (filt_hbm, filt_ref),
+            (grad_hbm, grad_ref),
+            (taps_hbm, taps_ref),
+        )
+    ):
+        copy = pltpu.make_async_copy(src, dst, sems.at[place])
+        copy.start()
+        copies.append(copy)
+    for copy in copies:
+        copy.wait()
     for stream in range(4):
         block = feat_ref[stream] if stream < 3 else filt_ref[...]
         flipped = block.T
         for quarter in range(4):
             held[quarter, stream] = flipped[quarter * 64 : quarter * 64 + 64]
     for by, out in enumerate((p0, p1, p2, p3)):
-        out[...] = held[lax.rem(x + by, 4)]
-    rows = jnp.zeros((128, 256), F32)
-    taps_held[0] = rows
+        out[0:4] = held[lax.rem(x + by, 4)]
+        for row in range(2):
+            for column in range(2):
+                out[4 + 2 * row + column] = grad_ref[
+                    row * 64 : row * 64 + 64, column * 128 : column * 128 + 128
+                ]
+    taps_held[0] = jnp.zeros((128, 256), F32)
     for stream in range(3):
         taps_held[0, stream * 8 : stream * 8 + TAPS, :] = taps_ref[stream]
     columns = taps_held[0].T
@@ -118,37 +154,48 @@
     taps_out[...] = taps_held[1 + x, 0:64, 0:128]
 
 
-def lift_kernel(g0, g1, g2, g3, weight, behind, whole_out, send_out, gathered, rows, sem):
+def fetch_kernel(weight, behind, out, sems):
     x, z, y, c = coords()
-    copy = pltpu.make_async_copy(weight.at[:, :, 1 - c, x], rows, sem)
-    copy.start()
-    for by, block in enumerate((g0, g1, g2, g3)):
-        gathered[lax.rem(x + 4 - by, 4)] = block[...]
+    copies = []
+    for half in range(2):
+        core = c if half == 0 else 1 - c
+        copy = pltpu.make_async_copy(weight.at[:, :, core, x], out.at[half], sems.at[half])
+        copy.start()
+        copies.append(copy)
+    for copy in copies:
+        copy.wait()
+
+
+def lift_kernel(p0, r1, r2, r3, rows, whole_out, send_out, gathered):
+    x, z, y, c = coords()
+    for by, block in enumerate((p0, r1, r2, r3)):
+        slot = lax.rem(x + 4 - by, 4)
+        for row in range(2):
+            for column in range(2):
+                gathered[
+                    slot, row * 64 : row * 64 + 64, column * 128 : column * 128 + 128
+                ] = block[4 + 2 * row + column]
     whole = gathered[...].reshape(512, 256)
     whole_out[...] = whole
-    copy.wait()
     for zd in range(NZ):
         part = lax.dot_general(
-            rows[zd].reshape(256, 256), whole, NT, preferred_element_type=F32
+            rows[1, zd].reshape(256, 256), whole, NT, preferred_element_type=F32
         )
         send_out[zd] = part.astype(BF16).reshape(NY, 64, 512)
 
 
-def sum_core_kernel(recv, whole, weight, own_out, s1, s2, s3, rows, sem):
+def sum_core_kernel(recv, whole, rows, behind, own_out, s1, s2, s3):
     x, z, y, c = coords()
-    copy = pltpu.make_async_copy(weight.at[:, :, c, x], rows, sem)
-    copy.start()
-    copy.wait()
     for by, out in enumerate((own_out, s1, s2, s3)):
         zd = lax.rem(z + by, 4)
         part = lax.dot_general(
-            rows[zd].reshape(256, 256), whole[...], NT, preferred_element_type=F32
+            rows[0, zd].reshape(256, 256), whole[...], NT, preferred_element_type=F32
         )
         total = part.reshape(NY, 64, 512) + recv[zd].astype(F32)
         out[...] = total.astype(out.dtype)
 
 
-def sum_z_kernel(own, r1, r2, r3, own_out, s1, s2, s3):
+def sum_z_kernel(own, r1, r2, r3, behind, own_out, s1, s2, s3):
     y = coords()[2]
     for by, out in enumerate((own_out, s1, s2, s3)):
         yd = lax.rem(y + by, 4)
@@ -194,7 +241,7 @@
 def pre_kernel(p0, r1, r2, r3, taps, high, low, behind, mixed_out, conv_out, long_out, spec_out, feat_out, held):
     x = coords()[0]
     for by, block in enumerate((p0, r1, r2, r3)):
-        held[lax.rem(x + 4 - by, 4)] = block[...]
+        held[lax.rem(x + 4 - by, 4)] = block[0:4]
     lane = lax.broadcasted_iota(jnp.int32, (64, 512), 1)
     convs = []
     for stream in range(3):
@@ -240,9 +287,10 @@
         total = None
         for tap in range(TAPS):
             column = stream * 8 + tap
-            term = taps[:, column : column + 1] * sooner(grad_conv[stream], tap, lane)
+            ahead = sooner(grad_conv[stream], tap, lane)
+            term = taps[:, column : column + 1] * ahead
             total = term if total is None else total + term
-            row = jnp.sum(grad_conv[stream] * later(wide, tap, lane), axis=1, keepdims=True)
+            row = jnp.sum(ahead * wide, axis=1, keepdims=True)
             sums = jnp.where(slot == column, row, sums)
         rounded = total.astype(BF16)
         for b in range(4):
@@ -276,58 +324,68 @@
         taps_out[stream] = rows[stream * 8 : stream * 8 + TAPS]
 
 
+def relay_kernel(block, behind, out):
+    out[...] = block[...]
+
+
+def collect_kernel(b0, b1, b2, b3, out):
+    for place, block in enumerate((b0, b1, b2, b3)):
+        out[place] = block[...]
+
+
 def weight_kernel(mine, theirs, whole, out):
     x, z, y, c = coords()
     for half, blocks in enumerate((mine, theirs)):
         core = c if half == 0 else 1 - c
-        for across in range(4):
-            src = lax.rem(z + 4 - across, 4)
+        for along in range(4):
+            yd = lax.rem(y + 4 - along, 4)
             part = jnp.dot(
-                blocks[across].reshape(256, 512), whole[...], preferred_element_type=F32
+                blocks[along].reshape(256, 512), whole[...], preferred_element_type=F32
             )
-            for along in range(4):
-                yd = lax.rem(y + 4 - along, 4)
+            for across in range(4):
+                src = lax.rem(z + 4 - across, 4)
                 start = pl.multiple_of(yd * 512 + core * 256 + src * 64, 64)
-                out[pl.ds(start, 64), :] = part[along * 64 : along * 64 + 64]
+                out[pl.ds(start, 64), :] = part[across * 64 : across * 64 + 64]
 
 
 def local(high, low, features, short_kernel, long_filter, out_weight, grad_out):
     high, low = jnp.asarray(high), jnp.asarray(low)
     weight = out_weight.reshape(NZ, NY, NC, NX, 64, 256)
-    g = [grad_out] + [along_x(grad_out, k) for k in (1, 2, 3)]
     *pay, taps = call(
         pack_kernel,
-        [kept((4, 64, 128), BF16)] * 4 + [kept((64, 128), F32)],
+        [kept((8, 64, 128), BF16)] * 4 + [kept((64, 128), F32)],
         features,
         long_filter,
         short_kernel,
-        scratch=[pltpu.VMEM((4, 4, 64, 128), BF16), pltpu.VMEM((5, 128, 256), F32)],
+        grad_out,
+        in_hbm=(0, 1, 2, 3),
+        scratch=[
+            pltpu.VMEM((3, 128, 256), BF16),
+            pltpu.VMEM((128, 256), BF16),
+            pltpu.VMEM((3, TAPS, 256), F32),
+            pltpu.VMEM((128, 256), BF16),
+            pltpu.VMEM((4, 4, 64, 128), BF16),
+            pltpu.VMEM((5, 128, 256), F32),
+            pltpu.SemaphoreType.DMA((4,)),
+        ],
     )
     got = [pay[0]] + [along_x(pay[k], k) for k in (1, 2, 3)]
+    rows = call(
+        fetch_kernel,
+        kept((2, NZ, NY, 64, 256), BF16),
+        weight,
+        taps,
+        in_hbm=(0,),
+        scratch=[pltpu.SemaphoreType.DMA((2,))],
+    )
     whole, send = call(
         lift_kernel,
         [kept((512, 256), BF16), kept((NZ, NY, 64, 512), BF16)],
-        *g,
-        weight,
-        taps,
-        in_hbm=(4,),
-        scratch=[
-            pltpu.VMEM((4, 128, 256), BF16),
-            pltpu.VMEM((NZ, NY, 64, 256), BF16),
-            pltpu.SemaphoreType.DMA,
-        ],
+        *got,
+        rows,
+        scratch=[pltpu.VMEM((4, 128, 256), BF16)],
     )
     recv = other_core(send)
-    own, *sends = call(
-        sum_core_kernel,
-        [kept((NY, 64, 512), F32)] + [kept((NY, 64, 512), BF16)] * 3,
-        recv,
-        whole,
-        weight,
-        in_hbm=(2,),
-        scratch=[pltpu.VMEM((NZ, NY, 64, 256), BF16), pltpu.SemaphoreType.DMA],
-    )
-    recvs = [along_z(sends[k - 1], k) for k in (1, 2, 3)]
     mixed, conv, long, spec, feats = call(
         pre_kernel,
         [
@@ -341,19 +399,41 @@
         taps,
         high,
         low,
-        sends[2],
+        whole,
         scratch=[pltpu.VMEM((4, 4, 64, 128), BF16)],
-        time=3.0,
-    )
-    moved = turned(mixed)
-    column = jnp.stack([moved] + [along_y(moved, k) for k in (1, 2, 3)])
-    mine = jnp.stack([column] + [along_z(column, k) for k in (1, 2, 3)])
+    )
+    own, *sends = call(
+        sum_core_kernel,
+        [kept((NY, 64, 512), F32)] + [kept((NY, 64, 512), BF16)] * 3,
+        recv,
+        whole,
+        rows,
+        mixed,
+    )
+    recvs = [along_z(sends[k - 1], k) for k in (1, 2, 3)]
+    moved = call(relay_kernel, kept((64, 512), BF16), turned(mixed), sends[2], time=0.0)
+    column = call(
+        collect_kernel,
+        kept((4, 64, 512), BF16),
+        moved,
+        *[along_z(moved, k) for k in (1, 2, 3)],
+        time=0.0,
+    )
+    mine = call(
+        collect_kernel,
+        kept((4, 4, 64, 512), BF16),
+        column,
+        *[along_y(column, k) for k in (1, 2, 3)],
+        time=0.0,
+    )
     theirs = other_core(mine)
     own, *sends = call(
         sum_z_kernel,
         [kept((64, 512), F32)] + [kept((64, 512), BF16)] * 3,
         own,
         *recvs,
+        column,
+        time=0.3,
     )
     recvs = [along_y(sends[k - 1], k) for k in (1, 2, 3)]
     outs = call(
@@ -369,7 +449,7 @@
         high,
         low,
         scratch=[pltpu.VMEM((4, 6, 64, 128), BF16)],
-        time=5.0,
+        time=3.0,
     )
     backs = [outs[0]] + [along_x(outs[k], k) for k in (1, 2, 3)]
     grad_features, grad_kernel, grad_filter = call(
@@ -377,8 +457,9 @@
         [shape((3, 128, 256), BF16), shape((3, TAPS, 256), F32), shape((128, 256), F32)],
         *backs,
         scratch=[pltpu.VMEM((4, 6, 64, 128), BF16)],
-    )
-    grad_weight = call(weight_kernel, shape((2048, 256), F32), mine, theirs, whole, time=3.0)
+        time=1.0,
+    )
+    grad_weight = call(weight_kernel, shape((2048, 256), F32), mine, theirs, whole)
     return grad_features, grad_kernel, grad_filter, grad_weight
 
 

time: 65.5 us -> 69.3 us (1.058)
  waiting for transfers between devices: 8.86 us -> 14.5 us
  starting transfers between devices: 38.8 us -> 42.9 us
  local copies, waits for them, and re-layouts: 3.14 us -> 0.02 us
  other arithmetic: 2.08 us -> 0 us
    ppermute x24 -> x21, waiting for transfers between devices: 8.86 us -> 14.5 us  [move(): return lax.ppermute(array, ('ctx', 'ch'), pairs)]
    ppermute x24 -> x21, starting transfers between devices: 38.8 us -> 42.9 us  [move(): return lax.ppermute(array, ('ctx', 'ch'), pairs)]
    unnamed x18 -> x8, local copies, waits for them, and re-layouts: 3.14 us -> 0.02 us
    another operation x2 -> x0, other arithmetic: 2.08 us -> none  [local(): mine = jnp.stack([column] + [along_z(column, k) for k in (1, 2, 3)])]
    pallas_call x8 -> x12, Pallas kernels: 11.4 us -> 10.8 us  [call(): pl.pallas_call(kernel, out_shape=out_shape, name=kernel.__name__, in_spec...]
  transfers between devices with their start and end apart: 24 -> 21, of which waited for: 4 -> 7; matrix products, arithmetic and copies ran while one was open for 3% -> 0% of each run, Pallas kernels for 12% -> 9%
where the time goes in v3:
time: 69.3 us; the launch traced here: 69 us
  starting transfers between devices  42.9 us (62%)
  waiting for transfers between devices  14.5 us (21%)
  Pallas kernels  10.8 us (16%)
  between operations  0.79 us (1%)
    ppermute x21, starting transfers between devices, move(): return lax.ppermute(array, ('ctx', 'ch'), pairs)  42.9 us
    ppermute x21, waiting for transfers between devices, move(): return lax.ppermute(array, ('ctx', 'ch'), pairs)  14.5 us
    pallas_call x12, Pallas kernels, call(): pl.pallas_call(kernel, out_shape=out_shape, name=kernel.__name__, in_spec...  10.8 us
  transfers between devices with their start and end apart: 21, of which 7 were waited for; matrix products, arithmetic and copies ran while one was open for 0% of the time, Pallas kernels for 9%

profile of v3, /device:TPU:1, one launch (start us, length us, event | category | flops | bytes accessed | tf_op | source)
XLA Modules:
  0.0 69.0 jit_solution(10407567481769111250)
XLA Ops:
  0.6 1.2 %pack_kernel.1 = (bf16[8,64,128]{2,1,0:T(8,128)(2,1)S(1)}, bf16[8,64,128]{2,1,0:T(8,128)(2,1)S(1)}, bf16[8,64,128]{2,1,0:T(8,128)(2,1)S(1)}, bf16[8,64,128]{2,1,0:T(8,128)(2,1)S(1)}, f32[64,128]{1,0:T(8,128)S(1)}) custom-call(bf16[3,128,256]{2,1,0:T(8,128)(2,1)} %feat_hbm.1, bf16[128,256]{1,0:T(8,128)(2,1)} %filt_hbm.1, f32[3,7,256]{2,1,0:T(8,128)} %taps_hbm.1, ...), custom_call_target="tpu_custom_call" | custom-call | flops 70000001024 | bytes 7000000 | tf_op jit(solution)/shard_map/pack_kernel/pallas_call | solution.py:81
  1.9 2.1 %collective-permute-start = (bf16[8,64,128]{2,1,0:T(8,128)(2,1)S(1)}, bf16[8,64,128]{2,1,0:T(8,128)(2,1)S(1)}, u32[]{:S(2)}, u32[]{:S(2)}) collective-permute-start(bf16[8,64,128]{2,1,0:T(8,128)(2,1)S(1)} %get-tuple-element.32), channel_id=1, source_target_pairs={{0,32},{1,33},{2,34},{3,35},{4,36},{5,37},{6,38},{7,39},{8,40},{9,... | collective-permute-start | bytes 393224 | tf_op jit(solution)/shard_map/ppermute | solution.py:38
  4.0 2.5 %collective-permute-start.1 = (bf16[8,64,128]{2,1,0:T(8,128)(2,1)S(1)}, bf16[8,64,128]{2,1,0:T(8,128)(2,1)S(1)}, u32[]{:S(2)}, u32[]{:S(2)}) collective-permute-start(bf16[8,64,128]{2,1,0:T(8,128)(2,1)S(1)} %get-tuple-element.33), channel_id=1, source_target_pairs={{0,64},{1,65},{2,66},{3,67},{4,68},{5,69},{6,70},{7,71},{8,72},{9,... | collective-permute-start | bytes 393224 | tf_op jit(solution)/shard_map/ppermute | solution.py:38
  6.4 1.1 %collective-permute-start.2 = (bf16[8,64,128]{2,1,0:T(8,128)(2,1)S(1)}, bf16[8,64,128]{2,1,0:T(8,128)(2,1)S(1)}, u32[]{:S(2)}, u32[]{:S(2)}) collective-permute-start(bf16[8,64,128]{2,1,0:T(8,128)(2,1)S(1)} %get-tuple-element.34), channel_id=1, source_target_pairs={{0,96},{1,97},{2,98},{3,99},{4,100},{5,101},{6,102},{7,103},{8,104... | collective-permute-start | bytes 393224 | tf_op jit(solution)/shard_map/ppermute | solution.py:38
  7.6 1.2 %fetch_kernel.1.rows = bf16[2,4,4,64,256]{4,3,2,1,0:T(8,128)(2,1)S(1)} custom-call(bf16[4,4,2,4,64,256]{5,4,3,2,1,0:T(8,128)(2,1)} %bitcast.1, f32[64,128]{1,0:T(8,128)S(1)} %get-tuple-element.35.behind.taps), custom_call_target="tpu_custom_call" | custom-call | flops 70000001024 | bytes 7000000 | tf_op jit(solution)/shard_map/fetch_kernel/pallas_call | solution.py:81
  8.8 3.3 %collective-permute-done.1.r2 = bf16[8,64,128]{2,1,0:T(8,128)(2,1)S(1)} collective-permute-done((bf16[8,64,128]{2,1,0:T(8,128)(2,1)S(1)}, bf16[8,64,128]{2,1,0:T(8,128)(2,1)S(1)}, u32[]{:S(2)}, u32[]{:S(2)}) %collective-permute-start.1) | collective-permute-done | bytes 131104 | tf_op jit(solution)/shard_map/ppermute | solution.py:38
  12.7 1.6 %collective-permute-start.3 = (bf16[4,4,64,512]{3,2,1,0:T(8,128)(2,1)S(1)}, bf16[4,4,64,512]{3,2,1,0:T(8,128)(2,1)S(1)}, u32[]{:S(2)}, u32[]{:S(2)}) collective-permute-start(bf16[4,4,64,512]{3,2,1,0:T(8,128)(2,1)S(1)} %get-tuple-element.36), channel_id=1, source_target_pairs={{0,1},{1,0},{2,3},{3,2},{4,5},{5,4},{6,7},{7,6},{8,9},{9,8},{10,11... | collective-permute-start | bytes 3145736 | tf_op jit(solution)/shard_map/ppermute | solution.py:38
  14.3 1.7 %pre_kernel.1 = (bf16[64,512]{1,0:T(8,128)(2,1)S(1)}, f32[3,64,512]{2,1,0:T(8,128)S(1)}, f32[64,512]{1,0:T(8,128)S(1)}, f32[128,1024]{1,0:T(8,128)S(1)}, bf16[3,64,512]{2,1,0:T(8,128)(2,1)S(1)}) custom-call(bf16[8,64,128]{2,1,0:T(8,128)(2,1)S(1)} %get-tuple-element.31.p0, bf16[8,64,128]{2,1,0:T(8,128)(2,1)S(1)} %collective-permute-done.r1, ...), custom_call_target="tpu_custom_call" | custom-call | flops 70000001024 | bytes 7000000 | tf_op jit(solution)/shard_map/pre_kernel/pallas_call | solution.py:81
  16.0 0.6 collective-permute-done.3.recv
  17.1 1.7 %collective-permute-start.4 = (bf16[4,64,512]{2,1,0:T(8,128)(2,1)S(1)}, bf16[4,64,512]{2,1,0:T(8,128)(2,1)S(1)}, u32[]{:S(2)}, u32[]{:S(2)}) collective-permute-start(bf16[4,64,512]{2,1,0:T(8,128)(2,1)S(1)} %get-tuple-element.40), channel_id=1, source_target_pairs={{0,8},{1,9},{2,10},{3,11},{4,12},{5,13},{6,14},{7,15},{8,16},{9,17... | collective-permute-start | bytes 786440 | tf_op jit(solution)/shard_map/ppermute | solution.py:38
  18.8 3.3 %collective-permute-start.5 = (bf16[4,64,512]{2,1,0:T(8,128)(2,1)S(1)}, bf16[4,64,512]{2,1,0:T(8,128)(2,1)S(1)}, u32[]{:S(2)}, u32[]{:S(2)}) collective-permute-start(bf16[4,64,512]{2,1,0:T(8,128)(2,1)S(1)} %get-tuple-element.41), channel_id=1, source_target_pairs={{0,16},{1,17},{2,18},{3,19},{4,20},{5,21},{6,22},{7,23},{8,24},{9,... | collective-permute-start | bytes 786440 | tf_op jit(solution)/shard_map/ppermute | solution.py:38
  22.1 0.7 %collective-permute-start.6 = (bf16[4,64,512]{2,1,0:T(8,128)(2,1)S(1)}, bf16[4,64,512]{2,1,0:T(8,128)(2,1)S(1)}, u32[]{:S(2)}, u32[]{:S(2)}) collective-permute-start(bf16[4,64,512]{2,1,0:T(8,128)(2,1)S(1)} %get-tuple-element.42.behind), channel_id=1, source_target_pairs={{0,24},{1,25},{2,26},{3,27},{4,28},{5,29},{6,30},{7,31},{8,0},{9,1... | collective-permute-start | bytes 786440 | tf_op jit(solution)/shard_map/ppermute | solution.py:38
  22.8 0.7 collective-permute-start.7
  23.5 6.3 %collective-permute-start.8 = (bf16[64,512]{1,0:T(8,128)(2,1)S(1)}, bf16[64,512]{1,0:T(8,128)(2,1)S(1)}, u32[]{:S(2)}, u32[]{:S(2)}) collective-permute-start(bf16[64,512]{1,0:T(8,128)(2,1)S(1)} %relay_kernel.1.b0), channel_id=1, source_target_pairs={{0,8},{1,9},{2,10},{3,11},{4,12},{5,13},{6,14},{7,15},{8,16},{9,17... | collective-permute-start | bytes 196616 | tf_op jit(solution)/shard_map/ppermute | solution.py:38
  29.8 3.0 %collective-permute-start.9 = (bf16[64,512]{1,0:T(8,128)(2,1)S(1)}, bf16[64,512]{1,0:T(8,128)(2,1)S(1)}, u32[]{:S(2)}, u32[]{:S(2)}) collective-permute-start(bf16[64,512]{1,0:T(8,128)(2,1)S(1)} %relay_kernel.1.b0), channel_id=1, source_target_pairs={{0,16},{1,17},{2,18},{3,19},{4,20},{5,21},{6,22},{7,23},{8,24},{9,... | collective-permute-start | bytes 196616 | tf_op jit(solution)/shard_map/ppermute | solution.py:38
  32.8 3.4 %collective-permute-done.8.b1 = bf16[64,512]{1,0:T(8,128)(2,1)S(1)} collective-permute-done((bf16[64,512]{1,0:T(8,128)(2,1)S(1)}, bf16[64,512]{1,0:T(8,128)(2,1)S(1)}, u32[]{:S(2)}, u32[]{:S(2)}) %collective-permute-start.8) | collective-permute-done | bytes 65568 | tf_op jit(solution)/shard_map/ppermute | solution.py:38
  36.2 3.1 %collective-permute-done.10.b3 = bf16[64,512]{1,0:T(8,128)(2,1)S(1)} collective-permute-done((bf16[64,512]{1,0:T(8,128)(2,1)S(1)}, bf16[64,512]{1,0:T(8,128)(2,1)S(1)}, u32[]{:S(2)}, u32[]{:S(2)}) %collective-permute-start.10) | collective-permute-done | bytes 65568 | tf_op jit(solution)/shard_map/ppermute | solution.py:38
  39.5 1.4 %collective-permute-start.11 = (bf16[64,512]{1,0:T(8,128)(2,1)S(1)}, bf16[64,512]{1,0:T(8,128)(2,1)S(1)}, u32[]{:S(2)}, u32[]{:S(2)}) collective-permute-start(bf16[64,512]{1,0:T(8,128)(2,1)S(1)} %get-tuple-element.44), channel_id=1, source_target_pairs={{0,2},{1,3},{2,4},{3,5},{4,6},{5,7},{6,0},{7,1},{8,10},{9,11},{10,... | collective-permute-start | bytes 196616 | tf_op jit(solution)/shard_map/ppermute | solution.py:38
  40.9 2.6 %collective-permute-start.12 = (bf16[64,512]{1,0:T(8,128)(2,1)S(1)}, bf16[64,512]{1,0:T(8,128)(2,1)S(1)}, u32[]{:S(2)}, u32[]{:S(2)}) collective-permute-start(bf16[64,512]{1,0:T(8,128)(2,1)S(1)} %get-tuple-element.45), channel_id=1, source_target_pairs={{0,4},{1,5},{2,6},{3,7},{4,0},{5,1},{6,2},{7,3},{8,12},{9,13},{10,... | collective-permute-start | bytes 196616 | tf_op jit(solution)/shard_map/ppermute | solution.py:38
  43.5 1.1 %collective-permute-start.13 = (bf16[64,512]{1,0:T(8,128)(2,1)S(1)}, bf16[64,512]{1,0:T(8,128)(2,1)S(1)}, u32[]{:S(2)}, u32[]{:S(2)}) collective-permute-start(bf16[64,512]{1,0:T(8,128)(2,1)S(1)} %get-tuple-element.46), channel_id=1, source_target_pairs={{0,6},{1,7},{2,0},{3,1},{4,2},{5,3},{6,4},{7,5},{8,14},{9,15},{10,... | collective-permute-start | bytes 196616 | tf_op jit(solution)/shard_map/ppermute | solution.py:38
  44.9 0.8 %collective-permute-start.18 = (bf16[4,64,512]{2,1,0:T(8,128)(2,1)S(1)}, bf16[4,64,512]{2,1,0:T(8,128)(2,1)S(1)}, u32[]{:S(2)}, u32[]{:S(2)}) collective-permute-start(bf16[4,64,512]{2,1,0:T(8,128)(2,1)S(1)} %collect_kernel.2.behind.b0), channel_id=1, source_target_pairs={{0,4},{1,5},{2,6},{3,7},{4,0},{5,1},{6,2},{7,3},{8,12},{9,13},{10,... | collective-permute-start | bytes 786440 | tf_op jit(solution)/shard_map/ppermute | solution.py:38
  45.7 1.6 %collective-permute-start.19 = (bf16[4,64,512]{2,1,0:T(8,128)(2,1)S(1)}, bf16[4,64,512]{2,1,0:T(8,128)(2,1)S(1)}, u32[]{:S(2)}, u32[]{:S(2)}) collective-permute-start(bf16[4,64,512]{2,1,0:T(8,128)(2,1)S(1)} %collect_kernel.2.behind.b0), channel_id=1, source_target_pairs={{0,6},{1,7},{2,0},{3,1},{4,2},{5,3},{6,4},{7,5},{8,14},{9,15},{10,... | collective-permute-start | bytes 786440 | tf_op jit(solution)/shard_map/ppermute | solution.py:38
  47.4 2.5 %post_kernel.1 = (bf16[6,64,128]{2,1,0:T(8,128)(2,1)S(1)}, bf16[6,64,128]{2,1,0:T(8,128)(2,1)S(1)}, bf16[6,64,128]{2,1,0:T(8,128)(2,1)S(1)}, bf16[6,64,128]{2,1,0:T(8,128)(2,1)S(1)}) custom-call(f32[64,512]{1,0:T(8,128)S(1)} %get-tuple-element.43.own, bf16[64,512]{1,0:T(8,128)(2,1)S(1)} %collective-permute-done.11.r1, ...), custom_call_target="tpu_custom_call" | custom-call | flops 105000001536 | bytes 10500000 | tf_op jit(solution)/shard_map/post_kernel/pallas_call | solution.py:81
  49.9 0.6 collective-permute-start.14
  50.5 4.1 %collective-permute-start.15 = (bf16[6,64,128]{2,1,0:T(8,128)(2,1)S(1)}, bf16[6,64,128]{2,1,0:T(8,128)(2,1)S(1)}, u32[]{:S(2)}, u32[]{:S(2)}) collective-permute-start(bf16[6,64,128]{2,1,0:T(8,128)(2,1)S(1)} %get-tuple-element.53), channel_id=1, source_target_pairs={{0,64},{1,65},{2,66},{3,67},{4,68},{5,69},{6,70},{7,71},{8,72},{9,... | collective-permute-start | bytes 294920 | tf_op jit(solution)/shard_map/ppermute | solution.py:38
  54.5 1.7 %collective-permute-start.16 = (bf16[6,64,128]{2,1,0:T(8,128)(2,1)S(1)}, bf16[6,64,128]{2,1,0:T(8,128)(2,1)S(1)}, u32[]{:S(2)}, u32[]{:S(2)}) collective-permute-start(bf16[6,64,128]{2,1,0:T(8,128)(2,1)S(1)} %get-tuple-element.54), channel_id=1, source_target_pairs={{0,96},{1,97},{2,98},{3,99},{4,100},{5,101},{6,102},{7,103},{8,104... | collective-permute-start | bytes 294920 | tf_op jit(solution)/shard_map/ppermute | solution.py:38
  56.2 1.8 %collective-permute-done.18.b2 = bf16[4,64,512]{2,1,0:T(8,128)(2,1)S(1)} collective-permute-done((bf16[4,64,512]{2,1,0:T(8,128)(2,1)S(1)}, bf16[4,64,512]{2,1,0:T(8,128)(2,1)S(1)}, u32[]{:S(2)}, u32[]{:S(2)}) %collective-permute-start.18) | collective-permute-done | bytes 262176 | tf_op jit(solution)/shard_map/ppermute | solution.py:38
  57.9 0.9 %collective-permute-done.19.b3 = bf16[4,64,512]{2,1,0:T(8,128)(2,1)S(1)} collective-permute-done((bf16[4,64,512]{2,1,0:T(8,128)(2,1)S(1)}, bf16[4,64,512]{2,1,0:T(8,128)(2,1)S(1)}, u32[]{:S(2)}, u32[]{:S(2)}) %collective-permute-start.19) | collective-permute-done | bytes 262176 | tf_op jit(solution)/shard_map/ppermute | solution.py:38
  58.9 5.8 %collective-permute-start.20 = (bf16[4,4,64,512]{3,2,1,0:T(8,128)(2,1)S(1)}, bf16[4,4,64,512]{3,2,1,0:T(8,128)(2,1)S(1)}, u32[]{:S(2)}, u32[]{:S(2)}) collective-permute-start(bf16[4,4,64,512]{3,2,1,0:T(8,128)(2,1)S(1)} %collect_kernel.3.mine), channel_id=1, source_target_pairs={{0,1},{1,0},{2,3},{3,2},{4,5},{5,4},{6,7},{7,6},{8,9},{9,8},{10,11... | collective-permute-start | bytes 3145736 | tf_op jit(solution)/shard_map/ppermute | solution.py:38
  64.7 0.9 %out_kernel.1 = (bf16[3,128,256]{2,1,0:T(8,128)(2,1)}, f32[3,7,256]{2,1,0:T(8,128)}, f32[128,256]{1,0:T(8,128)}) custom-call(bf16[6,64,128]{2,1,0:T(8,128)(2,1)S(1)} %get-tuple-element.51.o0, bf16[6,64,128]{2,1,0:T(8,128)(2,1)S(1)} %collective-permute-done.14.r1, bf16[6,64,128]{2,1,0:T(8,128)(2,1)S(1)} %collective-permute-done.15.r2, ...), custom_call_target="tpu_custom_call" | custom-call | flops 35000000512 | bytes 3500000 | tf_op jit(solution)/shard_map/out_kernel/pallas_call | solution.py:81
  65.6 1.4 %collective-permute-done.20.theirs = bf16[4,4,64,512]{3,2,1,0:T(8,128)(2,1)S(1)} collective-permute-done((bf16[4,4,64,512]{3,2,1,0:T(8,128)(2,1)S(1)}, bf16[4,4,64,512]{3,2,1,0:T(8,128)(2,1)S(1)}, u32[]{:S(2)}, u32[]{:S(2)}) %collective-permute-start.20) | collective-permute-done | bytes 1048608 | tf_op jit(solution)/shard_map/ppermute | solution.py:38
  67.0 2.1 %weight_kernel.1 = f32[2048,256]{1,0:T(8,128)} custom-call(bf16[4,4,64,512]{3,2,1,0:T(8,128)(2,1)S(1)} %collect_kernel.3.mine, bf16[4,4,64,512]{3,2,1,0:T(8,128)(2,1)S(1)} %collective-permute-done.20.theirs, bf16[512,256]{1,0:T(8,128)(2,1)S(1)} %copy-done.3), custom_call_target="tpu_custom_call" | custom-call | flops 70000001024 | bytes 7000000 | tf_op jit(solution)/shard_map/weight_kernel/pallas_call | solution.py:81
  (30 shorter events, 1.7 us)
Async XLA Ops:
  1.9 6.9 %collective-permute-start = (bf16[8,64,128]{2,1,0:T(8,128)(2,1)S(1)}, bf16[8,64,128]{2,1,0:T(8,128)(2,1)S(1)}, u32[]{:S(2)}, u32[]{:S(2)}) collective-permute-start(bf16[8,64,128]{2,1,0:T(8,128)(2,1)S(1)} %get-tuple-element.32), channel_id=1, source_target_pairs={{0,32},{1,33},{2,34},{3,35},{4,36},{5,37},{6,38},{7,39},{8,40},{9,... | collective-permute-start | bytes 393224 | tf_op jit(solution)/shard_map/ppermute | solution.py:38
  4.0 8.2 %collective-permute-start.1 = (bf16[8,64,128]{2,1,0:T(8,128)(2,1)S(1)}, bf16[8,64,128]{2,1,0:T(8,128)(2,1)S(1)}, u32[]{:S(2)}, u32[]{:S(2)}) collective-permute-start(bf16[8,64,128]{2,1,0:T(8,128)(2,1)S(1)} %get-tuple-element.33), channel_id=1, source_target_pairs={{0,64},{1,65},{2,66},{3,67},{4,68},{5,69},{6,70},{7,71},{8,72},{9,... | collective-permute-start | bytes 393224 | tf_op jit(solution)/shard_map/ppermute | solution.py:38
  6.4 5.7 %collective-permute-start.2 = (bf16[8,64,128]{2,1,0:T(8,128)(2,1)S(1)}, bf16[8,64,128]{2,1,0:T(8,128)(2,1)S(1)}, u32[]{:S(2)}, u32[]{:S(2)}) collective-permute-start(bf16[8,64,128]{2,1,0:T(8,128)(2,1)S(1)} %get-tuple-element.34), channel_id=1, source_target_pairs={{0,96},{1,97},{2,98},{3,99},{4,100},{5,101},{6,102},{7,103},{8,104... | collective-permute-start | bytes 393224 | tf_op jit(solution)/shard_map/ppermute | solution.py:38
  12.1 2.2 %copy-start = (bf16[512,1024]{1,0:T(8,128)(2,1)S(1)}, bf16[512,1024]{1,0:T(8,128)(2,1)}, u32[]{:S(2)}) copy-start(bf16[512,1024]{1,0:T(8,128)(2,1)} %constant.4.clone.high) | copy-start | bytes 3145732
  12.1 2.2 %copy-start.1 = (bf16[512,1024]{1,0:T(8,128)(2,1)S(1)}, bf16[512,1024]{1,0:T(8,128)(2,1)}, u32[]{:S(2)}) copy-start(bf16[512,1024]{1,0:T(8,128)(2,1)} %constant.5.clone.low) | copy-start | bytes 3145732
  12.7 3.9 %copy-start.2 = (bf16[512,256]{1,0:T(8,128)(2,1)}, bf16[512,256]{1,0:T(8,128)(2,1)S(1)}, u32[]{:S(2)}) copy-start(bf16[512,256]{1,0:T(8,128)(2,1)S(1)} %get-tuple-element.37.behind.whole) | copy-start | bytes 786436
  12.7 3.9 %collective-permute-start.3 = (bf16[4,4,64,512]{3,2,1,0:T(8,128)(2,1)S(1)}, bf16[4,4,64,512]{3,2,1,0:T(8,128)(2,1)S(1)}, u32[]{:S(2)}, u32[]{:S(2)}) collective-permute-start(bf16[4,4,64,512]{3,2,1,0:T(8,128)(2,1)S(1)} %get-tuple-element.36), channel_id=1, source_target_pairs={{0,1},{1,0},{2,3},{3,2},{4,5},{5,4},{6,7},{7,6},{8,9},{9,8},{10,11... | collective-permute-start | bytes 3145736 | tf_op jit(solution)/shard_map/ppermute | solution.py:38
  17.1 22.2 %collective-permute-start.4 = (bf16[4,64,512]{2,1,0:T(8,128)(2,1)S(1)}, bf16[4,64,512]{2,1,0:T(8,128)(2,1)S(1)}, u32[]{:S(2)}, u32[]{:S(2)}) collective-permute-start(bf16[4,64,512]{2,1,0:T(8,128)(2,1)S(1)} %get-tuple-element.40), channel_id=1, source_target_pairs={{0,8},{1,9},{2,10},{3,11},{4,12},{5,13},{6,14},{7,15},{8,16},{9,17... | collective-permute-start | bytes 786440 | tf_op jit(solution)/shard_map/ppermute | solution.py:38
  18.8 20.6 %collective-permute-start.5 = (bf16[4,64,512]{2,1,0:T(8,128)(2,1)S(1)}, bf16[4,64,512]{2,1,0:T(8,128)(2,1)S(1)}, u32[]{:S(2)}, u32[]{:S(2)}) collective-permute-start(bf16[4,64,512]{2,1,0:T(8,128)(2,1)S(1)} %get-tuple-element.41), channel_id=1, source_target_pairs={{0,16},{1,17},{2,18},{3,19},{4,20},{5,21},{6,22},{7,23},{8,24},{9,... | collective-permute-start | bytes 786440 | tf_op jit(solution)/shard_map/ppermute | solution.py:38
  22.1 17.3 %collective-permute-start.6 = (bf16[4,64,512]{2,1,0:T(8,128)(2,1)S(1)}, bf16[4,64,512]{2,1,0:T(8,128)(2,1)S(1)}, u32[]{:S(2)}, u32[]{:S(2)}) collective-permute-start(bf16[4,64,512]{2,1,0:T(8,128)(2,1)S(1)} %get-tuple-element.42.behind), channel_id=1, source_target_pairs={{0,24},{1,25},{2,26},{3,27},{4,28},{5,29},{6,30},{7,31},{8,0},{9,1... | collective-permute-start | bytes 786440 | tf_op jit(solution)/shard_map/ppermute | solution.py:38
  22.8 0.7 collective-permute-start.7
  23.5 12.7 %collective-permute-start.8 = (bf16[64,512]{1,0:T(8,128)(2,1)S(1)}, bf16[64,512]{1,0:T(8,128)(2,1)S(1)}, u32[]{:S(2)}, u32[]{:S(2)}) collective-permute-start(bf16[64,512]{1,0:T(8,128)(2,1)S(1)} %relay_kernel.1.b0), channel_id=1, source_target_pairs={{0,8},{1,9},{2,10},{3,11},{4,12},{5,13},{6,14},{7,15},{8,16},{9,17... | collective-permute-start | bytes 196616 | tf_op jit(solution)/shard_map/ppermute | solution.py:38
  29.8 6.4 %collective-permute-start.9 = (bf16[64,512]{1,0:T(8,128)(2,1)S(1)}, bf16[64,512]{1,0:T(8,128)(2,1)S(1)}, u32[]{:S(2)}, u32[]{:S(2)}) collective-permute-start(bf16[64,512]{1,0:T(8,128)(2,1)S(1)} %relay_kernel.1.b0), channel_id=1, source_target_pairs={{0,16},{1,17},{2,18},{3,19},{4,20},{5,21},{6,22},{7,23},{8,24},{9,... | collective-permute-start | bytes 196616 | tf_op jit(solution)/shard_map/ppermute | solution.py:38
  36.2 3.1 %collective-permute-start.10 = (bf16[64,512]{1,0:T(8,128)(2,1)S(1)}, bf16[64,512]{1,0:T(8,128)(2,1)S(1)}, u32[]{:S(2)}, u32[]{:S(2)}) collective-permute-start(bf16[64,512]{1,0:T(8,128)(2,1)S(1)} %relay_kernel.1.b0), channel_id=1, source_target_pairs={{0,24},{1,25},{2,26},{3,27},{4,28},{5,29},{6,30},{7,31},{8,0},{9,1... | collective-permute-start | bytes 196616 | tf_op jit(solution)/shard_map/ppermute | solution.py:38
  39.5 6.2 %collective-permute-start.11 = (bf16[64,512]{1,0:T(8,128)(2,1)S(1)}, bf16[64,512]{1,0:T(8,128)(2,1)S(1)}, u32[]{:S(2)}, u32[]{:S(2)}) collective-permute-start(bf16[64,512]{1,0:T(8,128)(2,1)S(1)} %get-tuple-element.44), channel_id=1, source_target_pairs={{0,2},{1,3},{2,4},{3,5},{4,6},{5,7},{6,0},{7,1},{8,10},{9,11},{10,... | collective-permute-start | bytes 196616 | tf_op jit(solution)/shard_map/ppermute | solution.py:38
  40.9 6.5 %collective-permute-start.12 = (bf16[64,512]{1,0:T(8,128)(2,1)S(1)}, bf16[64,512]{1,0:T(8,128)(2,1)S(1)}, u32[]{:S(2)}, u32[]{:S(2)}) collective-permute-start(bf16[64,512]{1,0:T(8,128)(2,1)S(1)} %get-tuple-element.45), channel_id=1, source_target_pairs={{0,4},{1,5},{2,6},{3,7},{4,0},{5,1},{6,2},{7,3},{8,12},{9,13},{10,... | collective-permute-start | bytes 196616 | tf_op jit(solution)/shard_map/ppermute | solution.py:38
  43.5 3.9 %collective-permute-start.13 = (bf16[64,512]{1,0:T(8,128)(2,1)S(1)}, bf16[64,512]{1,0:T(8,128)(2,1)S(1)}, u32[]{:S(2)}, u32[]{:S(2)}) collective-permute-start(bf16[64,512]{1,0:T(8,128)(2,1)S(1)} %get-tuple-element.46), channel_id=1, source_target_pairs={{0,6},{1,7},{2,0},{3,1},{4,2},{5,3},{6,4},{7,5},{8,14},{9,15},{10,... | collective-permute-start | bytes 196616 | tf_op jit(solution)/shard_map/ppermute | solution.py:38
  44.5 10.0 %collective-permute-start.17 = (bf16[4,64,512]{2,1,0:T(8,128)(2,1)S(1)}, bf16[4,64,512]{2,1,0:T(8,128)(2,1)S(1)}, u32[]{:S(2)}, u32[]{:S(2)}) collective-permute-start(bf16[4,64,512]{2,1,0:T(8,128)(2,1)S(1)} %collect_kernel.2.behind.b0), channel_id=1, source_target_pairs={{0,2},{1,3},{2,4},{3,5},{4,6},{5,7},{6,0},{7,1},{8,10},{9,11},{10,... | collective-permute-start | bytes 786440 | tf_op jit(solution)/shard_map/ppermute | solution.py:38
  44.9 13.0 %collective-permute-start.18 = (bf16[4,64,512]{2,1,0:T(8,128)(2,1)S(1)}, bf16[4,64,512]{2,1,0:T(8,128)(2,1)S(1)}, u32[]{:S(2)}, u32[]{:S(2)}) collective-permute-start(bf16[4,64,512]{2,1,0:T(8,128)(2,1)S(1)} %collect_kernel.2.behind.b0), channel_id=1, source_target_pairs={{0,4},{1,5},{2,6},{3,7},{4,0},{5,1},{6,2},{7,3},{8,12},{9,13},{10,... | collective-permute-start | bytes 786440 | tf_op jit(solution)/shard_map/ppermute | solution.py:38
  45.7 13.1 %collective-permute-start.19 = (bf16[4,64,512]{2,1,0:T(8,128)(2,1)S(1)}, bf16[4,64,512]{2,1,0:T(8,128)(2,1)S(1)}, u32[]{:S(2)}, u32[]{:S(2)}) collective-permute-start(bf16[4,64,512]{2,1,0:T(8,128)(2,1)S(1)} %collect_kernel.2.behind.b0), channel_id=1, source_target_pairs={{0,6},{1,7},{2,0},{3,1},{4,2},{5,3},{6,4},{7,5},{8,14},{9,15},{10,... | collective-permute-start | bytes 786440 | tf_op jit(solution)/shard_map/ppermute | solution.py:38
  49.9 14.8 %collective-permute-start.14 = (bf16[6,64,128]{2,1,0:T(8,128)(2,1)S(1)}, bf16[6,64,128]{2,1,0:T(8,128)(2,1)S(1)}, u32[]{:S(2)}, u32[]{:S(2)}) collective-permute-start(bf16[6,64,128]{2,1,0:T(8,128)(2,1)S(1)} %get-tuple-element.52), channel_id=1, source_target_pairs={{0,32},{1,33},{2,34},{3,35},{4,36},{5,37},{6,38},{7,39},{8,40},{9,... | collective-permute-start | bytes 294920 | tf_op jit(solution)/shard_map/ppermute | solution.py:38
  50.5 14.2 %collective-permute-start.15 = (bf16[6,64,128]{2,1,0:T(8,128)(2,1)S(1)}, bf16[6,64,128]{2,1,0:T(8,128)(2,1)S(1)}, u32[]{:S(2)}, u32[]{:S(2)}) collective-permute-start(bf16[6,64,128]{2,1,0:T(8,128)(2,1)S(1)} %get-tuple-element.53), channel_id=1, source_target_pairs={{0,64},{1,65},{2,66},{3,67},{4,68},{5,69},{6,70},{7,71},{8,72},{9,... | collective-permute-start | bytes 294920 | tf_op jit(solution)/shard_map/ppermute | solution.py:38
  54.5 10.2 %collective-permute-start.16 = (bf16[6,64,128]{2,1,0:T(8,128)(2,1)S(1)}, bf16[6,64,128]{2,1,0:T(8,128)(2,1)S(1)}, u32[]{:S(2)}, u32[]{:S(2)}) collective-permute-start(bf16[6,64,128]{2,1,0:T(8,128)(2,1)S(1)} %get-tuple-element.54), channel_id=1, source_target_pairs={{0,96},{1,97},{2,98},{3,99},{4,100},{5,101},{6,102},{7,103},{8,104... | collective-permute-start | bytes 294920 | tf_op jit(solution)/shard_map/ppermute | solution.py:38
  58.9 8.0 %collective-permute-start.20 = (bf16[4,4,64,512]{3,2,1,0:T(8,128)(2,1)S(1)}, bf16[4,4,64,512]{3,2,1,0:T(8,128)(2,1)S(1)}, u32[]{:S(2)}, u32[]{:S(2)}) collective-permute-start(bf16[4,4,64,512]{3,2,1,0:T(8,128)(2,1)S(1)} %collect_kernel.3.mine), channel_id=1, source_target_pairs={{0,1},{1,0},{2,3},{3,2},{4,5},{5,4},{6,7},{7,6},{8,9},{9,8},{10,11... | collective-permute-start | bytes 3145736 | tf_op jit(solution)/shard_map/ppermute | solution.py:38
  64.7 2.3 %copy-start.3 = (bf16[512,256]{1,0:T(8,128)(2,1)S(1)}, bf16[512,256]{1,0:T(8,128)(2,1)}, u32[]{:S(2)}) copy-start(bf16[512,256]{1,0:T(8,128)(2,1)} %copy-done.2) | copy-start | bytes 786436

commit v4 on v3

--- a/solution.py
+++ b/solution.py
@@ -16,6 +16,9 @@
 NT = (((1,), (1,)), ((), ()))
 VMEM_LIMIT = 20 * 1024 * 1024
 WEIGHT = 3.5e10
+TIMES = dict(
+    pack=2, fetch=2, lift=2, core=2, pre=2, relay=0.3, collect=0.3, sum=0.3, post=3, out=1, weight=2, near=0
+)
 
 
 def coords():
@@ -52,10 +55,6 @@
 
 def other_core(array):
     return move(array, lambda x, z, y, c: (x, z, y, 1 - c))
-
-
-def turned(array):
-    return move(array, lambda x, z, y, c: (z, x, y, c))
 
 
 def wave_table(length):
@@ -69,7 +68,10 @@
     return high, low
 
 
-def call(kernel, out_shape, *args, scratch=(), in_hbm=(), time=2.0):
+def call(
+    kernel, out_shape, *args, scratch=(), in_hbm=(), out_hbm=False, aliases=None, time=2.0
+):
+    out_space = pl.ANY if out_hbm else pltpu.VMEM
     specs, operands = [], []
     for place, arg in enumerate(args):
         if place in in_hbm:
@@ -83,8 +85,9 @@
         out_shape=out_shape,
         name=kernel.__name__,
         in_specs=specs,
-        out_specs=jax.tree.map(lambda _: pl.BlockSpec(memory_space=pltpu.VMEM), out_shape),
+        out_specs=jax.tree.map(lambda _: pl.BlockSpec(memory_space=out_space), out_shape),
         scratch_shapes=list(scratch),
+        input_output_aliases=aliases or {},
         cost_estimate=pl.CostEstimate(
             flops=int(time * WEIGHT), transcendentals=0, bytes_accessed=int(time * 3.5e6)
         ),
@@ -115,7 +118,7 @@
     taps_ref,
     grad_ref,
     held,
-    taps_held,
+    square,
     sems,
 ):
     x = coords()[0]
@@ -124,18 +127,18 @@
         (
             (feat_hbm, feat_ref),
             (filt_hbm, filt_ref),
+            (taps_hbm, taps_ref),
             (grad_hbm, grad_ref),
-            (taps_hbm, taps_ref),
         )
     ):
         copy = pltpu.make_async_copy(src, dst, sems.at[place])
         copy.start()
         copies.append(copy)
+    square[0] = jnp.zeros((128, 256), F32)
     for copy in copies:
         copy.wait()
     for stream in range(4):
-        block = feat_ref[stream] if stream < 3 else filt_ref[...]
-        flipped = block.T
+        flipped = (feat_ref[stream] if stream < 3 else filt_ref[...]).T
         for quarter in range(4):
             held[quarter, stream] = flipped[quarter * 64 : quarter * 64 + 64]
     for by, out in enumerate((p0, p1, p2, p3)):
@@ -145,29 +148,35 @@
                 out[4 + 2 * row + column] = grad_ref[
                     row * 64 : row * 64 + 64, column * 128 : column * 128 + 128
                 ]
-    taps_held[0] = jnp.zeros((128, 256), F32)
     for stream in range(3):
-        taps_held[0, stream * 8 : stream * 8 + TAPS, :] = taps_ref[stream]
-    columns = taps_held[0].T
+        square[0, stream * 8 : stream * 8 + TAPS, :] = taps_ref[stream]
+    columns = square[0].T
     for quarter in range(4):
-        taps_held[1 + quarter, 0:64, 0:128] = columns[quarter * 64 : quarter * 64 + 64]
-    taps_out[...] = taps_held[1 + x, 0:64, 0:128]
-
-
-def fetch_kernel(weight, behind, out, sems):
+        square[1 + quarter, 0:64, 0:128] = columns[quarter * 64 : quarter * 64 + 64]
+    taps_out[...] = square[1 + x, 0:64, 0:128]
+
+
+def fetch_kernel(weight, high_hbm, low_hbm, behind, out, high, low, sems, table_sems):
     x, z, y, c = coords()
     copies = []
     for half in range(2):
         core = c if half == 0 else 1 - c
-        copy = pltpu.make_async_copy(weight.at[:, :, core, x], out.at[half], sems.at[half])
+        for yd in range(NY):
+            copies.append(
+                pltpu.make_async_copy(
+                    weight.at[:, yd, core, x], out.at[half, yd], sems.at[half, yd]
+                )
+            )
+    copies.append(pltpu.make_async_copy(high_hbm, high, table_sems.at[0]))
+    copies.append(pltpu.make_async_copy(low_hbm, low, table_sems.at[1]))
+    for copy in copies:
         copy.start()
-        copies.append(copy)
     for copy in copies:
         copy.wait()
 
 
 def lift_kernel(p0, r1, r2, r3, rows, whole_out, send_out, gathered):
-    x, z, y, c = coords()
+    x = coords()[0]
     for by, block in enumerate((p0, r1, r2, r3)):
         slot = lax.rem(x + 4 - by, 4)
         for row in range(2):
@@ -177,30 +186,30 @@
                 ] = block[4 + 2 * row + column]
     whole = gathered[...].reshape(512, 256)
     whole_out[...] = whole
-    for zd in range(NZ):
+    for yd in range(NY):
         part = lax.dot_general(
-            rows[1, zd].reshape(256, 256), whole, NT, preferred_element_type=F32
+            rows[1, yd].reshape(256, 256), whole, NT, preferred_element_type=F32
         )
-        send_out[zd] = part.astype(BF16).reshape(NY, 64, 512)
+        send_out[yd] = part.astype(BF16).reshape(NZ, 64, 512)
 
 
 def sum_core_kernel(recv, whole, rows, behind, own_out, s1, s2, s3):
-    x, z, y, c = coords()
-    for by, out in enumerate((own_out, s1, s2, s3)):
-        zd = lax.rem(z + by, 4)
-        part = lax.dot_general(
-            rows[0, zd].reshape(256, 256), whole[...], NT, preferred_element_type=F32
-        )
-        total = part.reshape(NY, 64, 512) + recv[zd].astype(F32)
-        out[...] = total.astype(out.dtype)
-
-
-def sum_z_kernel(own, r1, r2, r3, behind, own_out, s1, s2, s3):
     y = coords()[2]
     for by, out in enumerate((own_out, s1, s2, s3)):
         yd = lax.rem(y + by, 4)
+        part = lax.dot_general(
+            rows[0, yd].reshape(256, 256), whole[...], NT, preferred_element_type=F32
+        )
+        total = part.reshape(NZ, 64, 512) + recv[yd].astype(F32)
+        out[...] = total.astype(out.dtype)
+
+
+def sum_y_kernel(own, r1, r2, r3, own_out, s1, s2, s3):
+    z = coords()[1]
+    for by, out in enumerate((own_out, s1, s2, s3)):
+        zd = lax.rem(z + by, 4)
         total = (
-            own[yd] + r1[yd].astype(F32) + (r2[yd].astype(F32) + r3[yd].astype(F32))
+            own[zd] + r1[zd].astype(F32) + (r2[zd].astype(F32) + r3[zd].astype(F32))
         )
         out[...] = total.astype(out.dtype)
 
@@ -324,8 +333,17 @@
         taps_out[stream] = rows[stream * 8 : stream * 8 + TAPS]
 
 
-def relay_kernel(block, behind, out):
-    out[...] = block[...]
+def pair_kernel(b0, b1, out):
+    out[0] = b0[...]
+    out[1] = b1[...]
+
+
+def route_kernel(near, far, o0, o1, o2, o3, held):
+    x, z = coords()[:2]
+    for back in range(4):
+        held[lax.rem(z + 4 - back, 4)] = (near if back < 2 else far)[back % 2]
+    for by, out in enumerate((o0, o1, o2, o3)):
+        out[...] = held[lax.rem(x + by, 4)]
 
 
 def collect_kernel(b0, b1, b2, b3, out):
@@ -333,19 +351,30 @@
         out[place] = block[...]
 
 
-def weight_kernel(mine, theirs, whole, out):
+def weight_half(blocks, whole, out, parts, sems, core):
     x, z, y, c = coords()
-    for half, blocks in enumerate((mine, theirs)):
-        core = c if half == 0 else 1 - c
-        for along in range(4):
-            yd = lax.rem(y + 4 - along, 4)
-            part = jnp.dot(
-                blocks[along].reshape(256, 512), whole[...], preferred_element_type=F32
-            )
-            for across in range(4):
-                src = lax.rem(z + 4 - across, 4)
-                start = pl.multiple_of(yd * 512 + core * 256 + src * 64, 64)
-                out[pl.ds(start, 64), :] = part[across * 64 : across * 64 + 64]
+    stores = []
+    for along in range(4):
+        yd = lax.rem(y + 4 - along, 4)
+        part = jnp.dot(
+            blocks[along].reshape(256, 512), whole[...], preferred_element_type=F32
+        )
+        for across in range(4):
+            src = lax.rem(x + 4 - across, 4)
+            parts[along, src] = part[across * 64 : across * 64 + 64]
+        store = pltpu.make_async_copy(parts.at[along], out.at[yd, core], sems.at[along])
+        store.start()
+        stores.append(store)
+    for store in stores:
+        store.wait()
+
+
+def near_kernel(blocks, whole, out, parts, sems):
+    weight_half(blocks, whole, out, parts, sems, coords()[3])
+
+
+def far_kernel(blocks, whole, held, out, parts, sems):
+    weight_half(blocks, whole, out, parts, sems, 1 - coords()[3])
 
 
 def local(high, low, features, short_kernel, long_filter, out_weight, grad_out):
@@ -368,22 +397,27 @@
             pltpu.VMEM((5, 128, 256), F32),
             pltpu.SemaphoreType.DMA((4,)),
         ],
+        time=TIMES["pack"],
     )
     got = [pay[0]] + [along_x(pay[k], k) for k in (1, 2, 3)]
-    rows = call(
+    rows, high, low = call(
         fetch_kernel,
-        kept((2, NZ, NY, 64, 256), BF16),
+        [kept((2, NY, NZ, 64, 256), BF16)] + [kept((512, 1024), BF16)] * 2,
         weight,
+        high,
+        low,
         taps,
-        in_hbm=(0,),
-        scratch=[pltpu.SemaphoreType.DMA((2,))],
+        in_hbm=(0, 1, 2),
+        scratch=[pltpu.SemaphoreType.DMA((2, NY)), pltpu.SemaphoreType.DMA((2,))],
+        time=TIMES["fetch"],
     )
     whole, send = call(
         lift_kernel,
-        [kept((512, 256), BF16), kept((NZ, NY, 64, 512), BF16)],
+        [kept((512, 256), BF16), kept((NY, NZ, 64, 512), BF16)],
         *got,
         rows,
         scratch=[pltpu.VMEM((4, 128, 256), BF16)],
+        time=TIMES["lift"],
     )
     recv = other_core(send)
     mixed, conv, long, spec, feats = call(
@@ -401,41 +435,52 @@
         low,
         whole,
         scratch=[pltpu.VMEM((4, 4, 64, 128), BF16)],
+        time=TIMES["pre"],
     )
     own, *sends = call(
         sum_core_kernel,
-        [kept((NY, 64, 512), F32)] + [kept((NY, 64, 512), BF16)] * 3,
+        [kept((NZ, 64, 512), F32)] + [kept((NZ, 64, 512), BF16)] * 3,
         recv,
         whole,
         rows,
         mixed,
-    )
-    recvs = [along_z(sends[k - 1], k) for k in (1, 2, 3)]
-    moved = call(relay_kernel, kept((64, 512), BF16), turned(mixed), sends[2], time=0.0)
+        time=TIMES["core"],
+    )
+    recvs = [along_y(sends[k - 1], k) for k in (1, 2, 3)]
+    pair = call(
+        pair_kernel, kept((2, 64, 512), BF16), mixed, along_z(mixed, 1), time=TIMES["relay"]
+    )
+    routed = call(
+        route_kernel,
+        [kept((64, 512), BF16)] * 4,
+        pair,
+        along_z(pair, 2),
+        scratch=[pltpu.VMEM((4, 64, 512), BF16)],
+        time=TIMES["relay"],
+    )
     column = call(
         collect_kernel,
         kept((4, 64, 512), BF16),
-        moved,
-        *[along_z(moved, k) for k in (1, 2, 3)],
-        time=0.0,
+        routed[0],
+        *[along_x(routed[k], k) for k in (1, 2, 3)],
+        time=TIMES["collect"],
     )
     mine = call(
         collect_kernel,
         kept((4, 4, 64, 512), BF16),
         column,
         *[along_y(column, k) for k in (1, 2, 3)],
-        time=0.0,
+        time=TIMES["collect"],
     )
     theirs = other_core(mine)
     own, *sends = call(
-        sum_z_kernel,
+        sum_y_kernel,
         [kept((64, 512), F32)] + [kept((64, 512), BF16)] * 3,
         own,
         *recvs,
-        column,
-        time=0.3,
-    )
-    recvs = [along_y(sends[k - 1], k) for k in (1, 2, 3)]
+        time=TIMES["sum"],
+    )
+    recvs = [along_z(sends[k - 1], k) for k in (1, 2, 3)]
     outs = call(
         post_kernel,
         [kept((6, 64, 128), BF16)] * 4,
@@ -449,7 +494,7 @@
         high,
         low,
         scratch=[pltpu.VMEM((4, 6, 64, 128), BF16)],
-        time=3.0,
+        time=TIMES["post"],
     )
     backs = [outs[0]] + [along_x(outs[k], k) for k in (1, 2, 3)]
     grad_features, grad_kernel, grad_filter = call(
@@ -457,9 +502,30 @@
         [shape((3, 128, 256), BF16), shape((3, TAPS, 256), F32), shape((128, 256), F32)],
         *backs,
         scratch=[pltpu.VMEM((4, 6, 64, 128), BF16)],
-        time=1.0,
-    )
-    grad_weight = call(weight_kernel, shape((2048, 256), F32), mine, theirs, whole)
+        time=TIMES["out"],
+    )
+    space = [pltpu.VMEM((NY, 4, 64, 256), F32), pltpu.SemaphoreType.DMA((NY,))]
+    grad_weight = call(
+        near_kernel,
+        pltpu.HBM((NY, NC, 4, 64, 256), F32),
+        mine,
+        whole,
+        out_hbm=True,
+        scratch=space,
+        time=TIMES["near"],
+    )
+    grad_weight = call(
+        far_kernel,
+        shape((NY, NC, 4, 64, 256), F32),
+        theirs,
+        whole,
+        grad_weight,
+        in_hbm=(2,),
+        out_hbm=True,
+        aliases={2: 0},
+        scratch=space,
+        time=TIMES["weight"],
+    ).reshape(2048, 256)
     return grad_features, grad_kernel, grad_filter, grad_weight
 
 

time: 69.3 us -> 61.5 us (0.89)
  waiting for transfers between devices: 14.5 us -> 9.28 us
  starting transfers between devices: 42.9 us -> 39 us
  Pallas kernels: 10.8 us -> 12.2 us
    ppermute x21 -> x22, waiting for transfers between devices: 14.5 us -> 9.28 us  [move(): return lax.ppermute(array, ('ctx', 'ch'), pairs)]
    ppermute x21 -> x22, starting transfers between devices: 42.9 us -> 39 us  [move(): return lax.ppermute(array, ('ctx', 'ch'), pairs)]
    pallas_call x12 -> x14, Pallas kernels: 10.8 us -> 12.2 us  [call(): pl.pallas_call(kernel, out_shape=out_shape, name=kernel.__name__, in_spec...]
  transfers between devices with their start and end apart: 21 -> 22, of which waited for: 7 -> 6; matrix products, arithmetic and copies ran while one was open for 0% -> 0% of each run, Pallas kernels for 9% -> 12%
where the time goes in v4:
time: 61.5 us; the launch traced here: 61.3 us
  starting transfers between devices  39 us (63%)
  Pallas kernels  12.2 us (20%)
  waiting for transfers between devices  9.28 us (15%)
  between operations  0.76 us (1%)
    ppermute x22, starting transfers between devices, move(): return lax.ppermute(array, ('ctx', 'ch'), pairs)  39 us
    pallas_call x14, Pallas kernels, call(): pl.pallas_call(kernel, out_shape=out_shape, name=kernel.__name__, in_spec...  12.2 us
    ppermute x22, waiting for transfers between devices, move(): return lax.ppermute(array, ('ctx', 'ch'), pairs)  9.28 us
  transfers between devices with their start and end apart: 22, of which 6 were waited for; matrix products, arithmetic and copies ran while one was open for 0% of the time, Pallas kernels for 12%

profile of v4, /device:TPU:1, one launch (start us, length us, event | category | flops | bytes accessed | tf_op | source)
XLA Modules:
  0.0 61.3 jit_solution(17402390437632620367)
XLA Ops:
  0.6 1.2 %pack_kernel.1 = (bf16[8,64,128]{2,1,0:T(8,128)(2,1)S(1)}, bf16[8,64,128]{2,1,0:T(8,128)(2,1)S(1)}, bf16[8,64,128]{2,1,0:T(8,128)(2,1)S(1)}, bf16[8,64,128]{2,1,0:T(8,128)(2,1)S(1)}, f32[64,128]{1,0:T(8,128)S(1)}) custom-call(bf16[3,128,256]{2,1,0:T(8,128)(2,1)} %feat_hbm.1, bf16[128,256]{1,0:T(8,128)(2,1)} %filt_hbm.1, f32[3,7,256]{2,1,0:T(8,128)} %taps_hbm.1, ...), custom_call_target="tpu_custom_call" | custom-call | flops 70000001024 | bytes 7000000 | tf_op jit(solution)/shard_map/pack_kernel/pallas_call | solution.py:83
  1.9 2.1 %collective-permute-start = (bf16[8,64,128]{2,1,0:T(8,128)(2,1)S(1)}, bf16[8,64,128]{2,1,0:T(8,128)(2,1)S(1)}, u32[]{:S(2)}, u32[]{:S(2)}) collective-permute-start(bf16[8,64,128]{2,1,0:T(8,128)(2,1)S(1)} %get-tuple-element.39), channel_id=1, source_target_pairs={{0,32},{1,33},{2,34},{3,35},{4,36},{5,37},{6,38},{7,39},{8,40},{9,... | collective-permute-start | bytes 393224 | tf_op jit(solution)/shard_map/ppermute | solution.py:41
  4.0 2.5 %collective-permute-start.1 = (bf16[8,64,128]{2,1,0:T(8,128)(2,1)S(1)}, bf16[8,64,128]{2,1,0:T(8,128)(2,1)S(1)}, u32[]{:S(2)}, u32[]{:S(2)}) collective-permute-start(bf16[8,64,128]{2,1,0:T(8,128)(2,1)S(1)} %get-tuple-element.40), channel_id=1, source_target_pairs={{0,64},{1,65},{2,66},{3,67},{4,68},{5,69},{6,70},{7,71},{8,72},{9,... | collective-permute-start | bytes 393224 | tf_op jit(solution)/shard_map/ppermute | solution.py:41
  6.5 1.1 %collective-permute-start.2 = (bf16[8,64,128]{2,1,0:T(8,128)(2,1)S(1)}, bf16[8,64,128]{2,1,0:T(8,128)(2,1)S(1)}, u32[]{:S(2)}, u32[]{:S(2)}) collective-permute-start(bf16[8,64,128]{2,1,0:T(8,128)(2,1)S(1)} %get-tuple-element.41), channel_id=1, source_target_pairs={{0,96},{1,97},{2,98},{3,99},{4,100},{5,101},{6,102},{7,103},{8,104... | collective-permute-start | bytes 393224 | tf_op jit(solution)/shard_map/ppermute | solution.py:41
  7.6 2.1 %fetch_kernel.1 = (bf16[2,4,4,64,256]{4,3,2,1,0:T(8,128)(2,1)S(1)}, bf16[512,1024]{1,0:T(8,128)(2,1)S(1)}, bf16[512,1024]{1,0:T(8,128)(2,1)S(1)}) custom-call(bf16[4,4,2,4,64,256]{5,4,3,2,1,0:T(8,128)(2,1)} %bitcast.3, bf16[512,1024]{1,0:T(8,128)(2,1)} %constant.4.clone.high_hbm, bf16[512,1024]{1,0:T(8,128)(2,1)} %constant.5.clone.low_hbm, ...), custom_call_target="tpu_custom_call" | custom-call | flops 70000001024 | bytes 7000000 | tf_op jit(solution)/shard_map/fetch_kernel/pallas_call | solution.py:83
  9.7 2.5 %collective-permute-done.1.r2 = bf16[8,64,128]{2,1,0:T(8,128)(2,1)S(1)} collective-permute-done((bf16[8,64,128]{2,1,0:T(8,128)(2,1)S(1)}, bf16[8,64,128]{2,1,0:T(8,128)(2,1)S(1)}, u32[]{:S(2)}, u32[]{:S(2)}) %collective-permute-start.1) | collective-permute-done | bytes 131104 | tf_op jit(solution)/shard_map/ppermute | solution.py:41
  12.7 1.7 %pre_kernel.1 = (bf16[64,512]{1,0:T(8,128)(2,1)S(1)}, f32[3,64,512]{2,1,0:T(8,128)S(1)}, f32[64,512]{1,0:T(8,128)S(1)}, f32[128,1024]{1,0:T(8,128)S(1)}, bf16[3,64,512]{2,1,0:T(8,128)(2,1)S(1)}) custom-call(bf16[8,64,128]{2,1,0:T(8,128)(2,1)S(1)} %get-tuple-element.38.p0, bf16[8,64,128]{2,1,0:T(8,128)(2,1)S(1)} %collective-permute-done.r1, ...), custom_call_target="tpu_custom_call" | custom-call | flops 70000001024 | bytes 7000000 | tf_op jit(solution)/shard_map/pre_kernel/pallas_call | solution.py:83
  14.4 1.7 %collective-permute-start.13 = (bf16[64,512]{1,0:T(8,128)(2,1)S(1)}, bf16[64,512]{1,0:T(8,128)(2,1)S(1)}, u32[]{:S(2)}, u32[]{:S(2)}) collective-permute-start(bf16[64,512]{1,0:T(8,128)(2,1)S(1)} %get-tuple-element.48.behind.b0), channel_id=1, source_target_pairs={{0,8},{1,9},{2,10},{3,11},{4,12},{5,13},{6,14},{7,15},{8,16},{9,17... | collective-permute-start | bytes 196616 | tf_op jit(solution)/shard_map/ppermute | solution.py:41
  16.1 1.8 %collective-permute-start.3 = (bf16[4,4,64,512]{3,2,1,0:T(8,128)(2,1)S(1)}, bf16[4,4,64,512]{3,2,1,0:T(8,128)(2,1)S(1)}, u32[]{:S(2)}, u32[]{:S(2)}) collective-permute-start(bf16[4,4,64,512]{3,2,1,0:T(8,128)(2,1)S(1)} %get-tuple-element.44), channel_id=1, source_target_pairs={{0,1},{1,0},{2,3},{3,2},{4,5},{5,4},{6,7},{7,6},{8,9},{9,8},{10,11... | collective-permute-start | bytes 3145736 | tf_op jit(solution)/shard_map/ppermute | solution.py:41
  17.9 2.0 %collective-permute-done.13.b1 = bf16[64,512]{1,0:T(8,128)(2,1)S(1)} collective-permute-done((bf16[64,512]{1,0:T(8,128)(2,1)S(1)}, bf16[64,512]{1,0:T(8,128)(2,1)S(1)}, u32[]{:S(2)}, u32[]{:S(2)}) %collective-permute-start.13) | collective-permute-done | bytes 65568 | tf_op jit(solution)/shard_map/ppermute | solution.py:41
  19.9 1.4 %collective-permute-start.14 = (bf16[2,64,512]{2,1,0:T(8,128)(2,1)S(1)}, bf16[2,64,512]{2,1,0:T(8,128)(2,1)S(1)}, u32[]{:S(2)}, u32[]{:S(2)}) collective-permute-start(bf16[2,64,512]{2,1,0:T(8,128)(2,1)S(1)} %pair_kernel.1.near), channel_id=1, source_target_pairs={{0,16},{1,17},{2,18},{3,19},{4,20},{5,21},{6,22},{7,23},{8,24},{9,... | collective-permute-start | bytes 393224 | tf_op jit(solution)/shard_map/ppermute | solution.py:41
  21.8 1.4 %collective-permute-start.4 = (bf16[4,64,512]{2,1,0:T(8,128)(2,1)S(1)}, bf16[4,64,512]{2,1,0:T(8,128)(2,1)S(1)}, u32[]{:S(2)}, u32[]{:S(2)}) collective-permute-start(bf16[4,64,512]{2,1,0:T(8,128)(2,1)S(1)} %get-tuple-element.50), channel_id=1, source_target_pairs={{0,2},{1,3},{2,4},{3,5},{4,6},{5,7},{6,0},{7,1},{8,10},{9,11},{10,... | collective-permute-start | bytes 786440 | tf_op jit(solution)/shard_map/ppermute | solution.py:41
  23.1 2.6 %collective-permute-start.5 = (bf16[4,64,512]{2,1,0:T(8,128)(2,1)S(1)}, bf16[4,64,512]{2,1,0:T(8,128)(2,1)S(1)}, u32[]{:S(2)}, u32[]{:S(2)}) collective-permute-start(bf16[4,64,512]{2,1,0:T(8,128)(2,1)S(1)} %get-tuple-element.51), channel_id=1, source_target_pairs={{0,4},{1,5},{2,6},{3,7},{4,0},{5,1},{6,2},{7,3},{8,12},{9,13},{10,... | collective-permute-start | bytes 786440 | tf_op jit(solution)/shard_map/ppermute | solution.py:41
  25.8 1.1 %collective-permute-start.6 = (bf16[4,64,512]{2,1,0:T(8,128)(2,1)S(1)}, bf16[4,64,512]{2,1,0:T(8,128)(2,1)S(1)}, u32[]{:S(2)}, u32[]{:S(2)}) collective-permute-start(bf16[4,64,512]{2,1,0:T(8,128)(2,1)S(1)} %get-tuple-element.52), channel_id=1, source_target_pairs={{0,6},{1,7},{2,0},{3,1},{4,2},{5,3},{6,4},{7,5},{8,14},{9,15},{10,... | collective-permute-start | bytes 786440 | tf_op jit(solution)/shard_map/ppermute | solution.py:41
  26.9 1.2 %collective-permute-start.15 = (bf16[64,512]{1,0:T(8,128)(2,1)S(1)}, bf16[64,512]{1,0:T(8,128)(2,1)S(1)}, u32[]{:S(2)}, u32[]{:S(2)}) collective-permute-start(bf16[64,512]{1,0:T(8,128)(2,1)S(1)} %get-tuple-element.69), channel_id=1, source_target_pairs={{0,32},{1,33},{2,34},{3,35},{4,36},{5,37},{6,38},{7,39},{8,40},{9,... | collective-permute-start | bytes 196616 | tf_op jit(solution)/shard_map/ppermute | solution.py:41
  28.1 2.2 %collective-permute-start.16 = (bf16[64,512]{1,0:T(8,128)(2,1)S(1)}, bf16[64,512]{1,0:T(8,128)(2,1)S(1)}, u32[]{:S(2)}, u32[]{:S(2)}) collective-permute-start(bf16[64,512]{1,0:T(8,128)(2,1)S(1)} %get-tuple-element.70), channel_id=1, source_target_pairs={{0,64},{1,65},{2,66},{3,67},{4,68},{5,69},{6,70},{7,71},{8,72},{9,... | collective-permute-start | bytes 196616 | tf_op jit(solution)/shard_map/ppermute | solution.py:41
  30.3 1.1 %collective-permute-start.17 = (bf16[64,512]{1,0:T(8,128)(2,1)S(1)}, bf16[64,512]{1,0:T(8,128)(2,1)S(1)}, u32[]{:S(2)}, u32[]{:S(2)}) collective-permute-start(bf16[64,512]{1,0:T(8,128)(2,1)S(1)} %get-tuple-element.71), channel_id=1, source_target_pairs={{0,96},{1,97},{2,98},{3,99},{4,100},{5,101},{6,102},{7,103},{8,104... | collective-permute-start | bytes 196616 | tf_op jit(solution)/shard_map/ppermute | solution.py:41
  31.4 3.1 %collective-permute-done.5.r2 = bf16[4,64,512]{2,1,0:T(8,128)(2,1)S(1)} collective-permute-done((bf16[4,64,512]{2,1,0:T(8,128)(2,1)S(1)}, bf16[4,64,512]{2,1,0:T(8,128)(2,1)S(1)}, u32[]{:S(2)}, u32[]{:S(2)}) %collective-permute-start.5) | collective-permute-done | bytes 262176 | tf_op jit(solution)/shard_map/ppermute | solution.py:41
  34.7 0.7 %collective-permute-start.7 = (bf16[64,512]{1,0:T(8,128)(2,1)S(1)}, bf16[64,512]{1,0:T(8,128)(2,1)S(1)}, u32[]{:S(2)}, u32[]{:S(2)}) collective-permute-start(bf16[64,512]{1,0:T(8,128)(2,1)S(1)} %get-tuple-element.54), channel_id=1, source_target_pairs={{0,8},{1,9},{2,10},{3,11},{4,12},{5,13},{6,14},{7,15},{8,16},{9,17... | collective-permute-start | bytes 196616 | tf_op jit(solution)/shard_map/ppermute | solution.py:41
  35.4 2.6 %collective-permute-start.8 = (bf16[64,512]{1,0:T(8,128)(2,1)S(1)}, bf16[64,512]{1,0:T(8,128)(2,1)S(1)}, u32[]{:S(2)}, u32[]{:S(2)}) collective-permute-start(bf16[64,512]{1,0:T(8,128)(2,1)S(1)} %get-tuple-element.55), channel_id=1, source_target_pairs={{0,16},{1,17},{2,18},{3,19},{4,20},{5,21},{6,22},{7,23},{8,24},{9,... | collective-permute-start | bytes 196616 | tf_op jit(solution)/shard_map/ppermute | solution.py:41
  38.1 2.0 %collective-permute-start.9 = (bf16[64,512]{1,0:T(8,128)(2,1)S(1)}, bf16[64,512]{1,0:T(8,128)(2,1)S(1)}, u32[]{:S(2)}, u32[]{:S(2)}) collective-permute-start(bf16[64,512]{1,0:T(8,128)(2,1)S(1)} %get-tuple-element.56), channel_id=1, source_target_pairs={{0,24},{1,25},{2,26},{3,27},{4,28},{5,29},{6,30},{7,31},{8,0},{9,1... | collective-permute-start | bytes 196616 | tf_op jit(solution)/shard_map/ppermute | solution.py:41
  40.1 2.8 %collective-permute-start.18 = (bf16[4,64,512]{2,1,0:T(8,128)(2,1)S(1)}, bf16[4,64,512]{2,1,0:T(8,128)(2,1)S(1)}, u32[]{:S(2)}, u32[]{:S(2)}) collective-permute-start(bf16[4,64,512]{2,1,0:T(8,128)(2,1)S(1)} %collect_kernel.2.b0), channel_id=1, source_target_pairs={{0,2},{1,3},{2,4},{3,5},{4,6},{5,7},{6,0},{7,1},{8,10},{9,11},{10,... | collective-permute-start | bytes 786440 | tf_op jit(solution)/shard_map/ppermute | solution.py:41
  42.9 1.8 %collective-permute-start.19 = (bf16[4,64,512]{2,1,0:T(8,128)(2,1)S(1)}, bf16[4,64,512]{2,1,0:T(8,128)(2,1)S(1)}, u32[]{:S(2)}, u32[]{:S(2)}) collective-permute-start(bf16[4,64,512]{2,1,0:T(8,128)(2,1)S(1)} %collect_kernel.2.b0), channel_id=1, source_target_pairs={{0,4},{1,5},{2,6},{3,7},{4,0},{5,1},{6,2},{7,3},{8,12},{9,13},{10,... | collective-permute-start | bytes 786440 | tf_op jit(solution)/shard_map/ppermute | solution.py:41
  45.4 2.5 %post_kernel.1 = (bf16[6,64,128]{2,1,0:T(8,128)(2,1)S(1)}, bf16[6,64,128]{2,1,0:T(8,128)(2,1)S(1)}, bf16[6,64,128]{2,1,0:T(8,128)(2,1)S(1)}, bf16[6,64,128]{2,1,0:T(8,128)(2,1)S(1)}) custom-call(f32[64,512]{1,0:T(8,128)S(1)} %get-tuple-element.53.own, bf16[64,512]{1,0:T(8,128)(2,1)S(1)} %collective-permute-done.7.r1, ...), custom_call_target="tpu_custom_call" | custom-call | flops 105000001536 | bytes 10500000 | tf_op jit(solution)/shard_map/post_kernel/pallas_call | solution.py:83
  47.9 1.1 %collective-permute-start.10 = (bf16[6,64,128]{2,1,0:T(8,128)(2,1)S(1)}, bf16[6,64,128]{2,1,0:T(8,128)(2,1)S(1)}, u32[]{:S(2)}, u32[]{:S(2)}) collective-permute-start(bf16[6,64,128]{2,1,0:T(8,128)(2,1)S(1)} %get-tuple-element.62), channel_id=1, source_target_pairs={{0,32},{1,33},{2,34},{3,35},{4,36},{5,37},{6,38},{7,39},{8,40},{9,... | collective-permute-start | bytes 294920 | tf_op jit(solution)/shard_map/ppermute | solution.py:41
  49.0 2.1 %collective-permute-start.11 = (bf16[6,64,128]{2,1,0:T(8,128)(2,1)S(1)}, bf16[6,64,128]{2,1,0:T(8,128)(2,1)S(1)}, u32[]{:S(2)}, u32[]{:S(2)}) collective-permute-start(bf16[6,64,128]{2,1,0:T(8,128)(2,1)S(1)} %get-tuple-element.63), channel_id=1, source_target_pairs={{0,64},{1,65},{2,66},{3,67},{4,68},{5,69},{6,70},{7,71},{8,72},{9,... | collective-permute-start | bytes 294920 | tf_op jit(solution)/shard_map/ppermute | solution.py:41
  51.2 1.3 %collective-permute-start.12 = (bf16[6,64,128]{2,1,0:T(8,128)(2,1)S(1)}, bf16[6,64,128]{2,1,0:T(8,128)(2,1)S(1)}, u32[]{:S(2)}, u32[]{:S(2)}) collective-permute-start(bf16[6,64,128]{2,1,0:T(8,128)(2,1)S(1)} %get-tuple-element.64), channel_id=1, source_target_pairs={{0,96},{1,97},{2,98},{3,99},{4,100},{5,101},{6,102},{7,103},{8,104... | collective-permute-start | bytes 294920 | tf_op jit(solution)/shard_map/ppermute | solution.py:41
  52.4 1.5 %collective-permute-done.19.b2 = bf16[4,64,512]{2,1,0:T(8,128)(2,1)S(1)} collective-permute-done((bf16[4,64,512]{2,1,0:T(8,128)(2,1)S(1)}, bf16[4,64,512]{2,1,0:T(8,128)(2,1)S(1)}, u32[]{:S(2)}, u32[]{:S(2)}) %collective-permute-start.19) | collective-permute-done | bytes 262176 | tf_op jit(solution)/shard_map/ppermute | solution.py:41
  54.0 3.7 %collective-permute-start.21 = (bf16[4,4,64,512]{3,2,1,0:T(8,128)(2,1)S(1)}, bf16[4,4,64,512]{3,2,1,0:T(8,128)(2,1)S(1)}, u32[]{:S(2)}, u32[]{:S(2)}) collective-permute-start(bf16[4,4,64,512]{3,2,1,0:T(8,128)(2,1)S(1)} %collect_kernel.3.blocks), channel_id=1, source_target_pairs={{0,1},{1,0},{2,3},{3,2},{4,5},{5,4},{6,7},{7,6},{8,9},{9,8},{10,11... | collective-permute-start | bytes 3145736 | tf_op jit(solution)/shard_map/ppermute | solution.py:41
  57.7 1.3 %near_kernel.1.held = f32[4,2,4,64,256]{4,3,2,1,0:T(8,128)} custom-call(bf16[4,4,64,512]{3,2,1,0:T(8,128)(2,1)S(1)} %collect_kernel.3.blocks, bf16[512,256]{1,0:T(8,128)(2,1)S(1)} %get-tuple-element.45.behind.whole), custom_call_target="tpu_custom_call" | custom-call | tf_op jit(solution)/shard_map/near_kernel/pallas_call | solution.py:83
  59.1 0.9 %out_kernel.1 = (bf16[3,128,256]{2,1,0:T(8,128)(2,1)}, f32[3,7,256]{2,1,0:T(8,128)}, f32[128,256]{1,0:T(8,128)}) custom-call(bf16[6,64,128]{2,1,0:T(8,128)(2,1)S(1)} %get-tuple-element.61.o0, bf16[6,64,128]{2,1,0:T(8,128)(2,1)S(1)} %collective-permute-done.10.r1, bf16[6,64,128]{2,1,0:T(8,128)(2,1)S(1)} %collective-permute-done.11.r2, ...), custom_call_target="tpu_custom_call" | custom-call | flops 35000000512 | bytes 3500000 | tf_op jit(solution)/shard_map/out_kernel/pallas_call | solution.py:83
  60.0 1.3 %far_kernel.1 = f32[4,2,4,64,256]{4,3,2,1,0:T(8,128)} custom-call(bf16[4,4,64,512]{3,2,1,0:T(8,128)(2,1)S(1)} %collective-permute-done.21.blocks, bf16[512,256]{1,0:T(8,128)(2,1)S(1)} %get-tuple-element.45.behind.whole, f32[4,2,4,64,256]{4,3,2,1,0:T(8,128)} %near_kernel.1.held), custom_call_target="tpu_custom_call", output_to_operand_aliasing={{}: (2, {})} | custom-call | flops 70000001024 | bytes 7000000 | tf_op jit(solution)/shard_map/far_kernel/pallas_call | solution.py:83
  (26 shorter events, 2.1 us)
Async XLA Ops:
  1.9 7.8 %collective-permute-start = (bf16[8,64,128]{2,1,0:T(8,128)(2,1)S(1)}, bf16[8,64,128]{2,1,0:T(8,128)(2,1)S(1)}, u32[]{:S(2)}, u32[]{:S(2)}) collective-permute-start(bf16[8,64,128]{2,1,0:T(8,128)(2,1)S(1)} %get-tuple-element.39), channel_id=1, source_target_pairs={{0,32},{1,33},{2,34},{3,35},{4,36},{5,37},{6,38},{7,39},{8,40},{9,... | collective-permute-start | bytes 393224 | tf_op jit(solution)/shard_map/ppermute | solution.py:41
  4.0 8.2 %collective-permute-start.1 = (bf16[8,64,128]{2,1,0:T(8,128)(2,1)S(1)}, bf16[8,64,128]{2,1,0:T(8,128)(2,1)S(1)}, u32[]{:S(2)}, u32[]{:S(2)}) collective-permute-start(bf16[8,64,128]{2,1,0:T(8,128)(2,1)S(1)} %get-tuple-element.40), channel_id=1, source_target_pairs={{0,64},{1,65},{2,66},{3,67},{4,68},{5,69},{6,70},{7,71},{8,72},{9,... | collective-permute-start | bytes 393224 | tf_op jit(solution)/shard_map/ppermute | solution.py:41
  6.5 5.7 %collective-permute-start.2 = (bf16[8,64,128]{2,1,0:T(8,128)(2,1)S(1)}, bf16[8,64,128]{2,1,0:T(8,128)(2,1)S(1)}, u32[]{:S(2)}, u32[]{:S(2)}) collective-permute-start(bf16[8,64,128]{2,1,0:T(8,128)(2,1)S(1)} %get-tuple-element.41), channel_id=1, source_target_pairs={{0,96},{1,97},{2,98},{3,99},{4,100},{5,101},{6,102},{7,103},{8,104... | collective-permute-start | bytes 393224 | tf_op jit(solution)/shard_map/ppermute | solution.py:41
  14.4 5.5 %collective-permute-start.13 = (bf16[64,512]{1,0:T(8,128)(2,1)S(1)}, bf16[64,512]{1,0:T(8,128)(2,1)S(1)}, u32[]{:S(2)}, u32[]{:S(2)}) collective-permute-start(bf16[64,512]{1,0:T(8,128)(2,1)S(1)} %get-tuple-element.48.behind.b0), channel_id=1, source_target_pairs={{0,8},{1,9},{2,10},{3,11},{4,12},{5,13},{6,14},{7,15},{8,16},{9,17... | collective-permute-start | bytes 196616 | tf_op jit(solution)/shard_map/ppermute | solution.py:41
  16.1 5.2 %collective-permute-start.3 = (bf16[4,4,64,512]{3,2,1,0:T(8,128)(2,1)S(1)}, bf16[4,4,64,512]{3,2,1,0:T(8,128)(2,1)S(1)}, u32[]{:S(2)}, u32[]{:S(2)}) collective-permute-start(bf16[4,4,64,512]{3,2,1,0:T(8,128)(2,1)S(1)} %get-tuple-element.44), channel_id=1, source_target_pairs={{0,1},{1,0},{2,3},{3,2},{4,5},{5,4},{6,7},{7,6},{8,9},{9,8},{10,11... | collective-permute-start | bytes 3145736 | tf_op jit(solution)/shard_map/ppermute | solution.py:41
  19.9 7.0 %collective-permute-start.14 = (bf16[2,64,512]{2,1,0:T(8,128)(2,1)S(1)}, bf16[2,64,512]{2,1,0:T(8,128)(2,1)S(1)}, u32[]{:S(2)}, u32[]{:S(2)}) collective-permute-start(bf16[2,64,512]{2,1,0:T(8,128)(2,1)S(1)} %pair_kernel.1.near), channel_id=1, source_target_pairs={{0,16},{1,17},{2,18},{3,19},{4,20},{5,21},{6,22},{7,23},{8,24},{9,... | collective-permute-start | bytes 393224 | tf_op jit(solution)/shard_map/ppermute | solution.py:41
  21.8 8.5 %collective-permute-start.4 = (bf16[4,64,512]{2,1,0:T(8,128)(2,1)S(1)}, bf16[4,64,512]{2,1,0:T(8,128)(2,1)S(1)}, u32[]{:S(2)}, u32[]{:S(2)}) collective-permute-start(bf16[4,64,512]{2,1,0:T(8,128)(2,1)S(1)} %get-tuple-element.50), channel_id=1, source_target_pairs={{0,2},{1,3},{2,4},{3,5},{4,6},{5,7},{6,0},{7,1},{8,10},{9,11},{10,... | collective-permute-start | bytes 786440 | tf_op jit(solution)/shard_map/ppermute | solution.py:41
  23.1 11.4 %collective-permute-start.5 = (bf16[4,64,512]{2,1,0:T(8,128)(2,1)S(1)}, bf16[4,64,512]{2,1,0:T(8,128)(2,1)S(1)}, u32[]{:S(2)}, u32[]{:S(2)}) collective-permute-start(bf16[4,64,512]{2,1,0:T(8,128)(2,1)S(1)} %get-tuple-element.51), channel_id=1, source_target_pairs={{0,4},{1,5},{2,6},{3,7},{4,0},{5,1},{6,2},{7,3},{8,12},{9,13},{10,... | collective-permute-start | bytes 786440 | tf_op jit(solution)/shard_map/ppermute | solution.py:41
  25.8 8.9 %collective-permute-start.6 = (bf16[4,64,512]{2,1,0:T(8,128)(2,1)S(1)}, bf16[4,64,512]{2,1,0:T(8,128)(2,1)S(1)}, u32[]{:S(2)}, u32[]{:S(2)}) collective-permute-start(bf16[4,64,512]{2,1,0:T(8,128)(2,1)S(1)} %get-tuple-element.52), channel_id=1, source_target_pairs={{0,6},{1,7},{2,0},{3,1},{4,2},{5,3},{6,4},{7,5},{8,14},{9,15},{10,... | collective-permute-start | bytes 786440 | tf_op jit(solution)/shard_map/ppermute | solution.py:41
  26.9 11.2 %collective-permute-start.15 = (bf16[64,512]{1,0:T(8,128)(2,1)S(1)}, bf16[64,512]{1,0:T(8,128)(2,1)S(1)}, u32[]{:S(2)}, u32[]{:S(2)}) collective-permute-start(bf16[64,512]{1,0:T(8,128)(2,1)S(1)} %get-tuple-element.69), channel_id=1, source_target_pairs={{0,32},{1,33},{2,34},{3,35},{4,36},{5,37},{6,38},{7,39},{8,40},{9,... | collective-permute-start | bytes 196616 | tf_op jit(solution)/shard_map/ppermute | solution.py:41
  28.1 11.9 %collective-permute-start.16 = (bf16[64,512]{1,0:T(8,128)(2,1)S(1)}, bf16[64,512]{1,0:T(8,128)(2,1)S(1)}, u32[]{:S(2)}, u32[]{:S(2)}) collective-permute-start(bf16[64,512]{1,0:T(8,128)(2,1)S(1)} %get-tuple-element.70), channel_id=1, source_target_pairs={{0,64},{1,65},{2,66},{3,67},{4,68},{5,69},{6,70},{7,71},{8,72},{9,... | collective-permute-start | bytes 196616 | tf_op jit(solution)/shard_map/ppermute | solution.py:41
  30.3 9.7 %collective-permute-start.17 = (bf16[64,512]{1,0:T(8,128)(2,1)S(1)}, bf16[64,512]{1,0:T(8,128)(2,1)S(1)}, u32[]{:S(2)}, u32[]{:S(2)}) collective-permute-start(bf16[64,512]{1,0:T(8,128)(2,1)S(1)} %get-tuple-element.71), channel_id=1, source_target_pairs={{0,96},{1,97},{2,98},{3,99},{4,100},{5,101},{6,102},{7,103},{8,104... | collective-permute-start | bytes 196616 | tf_op jit(solution)/shard_map/ppermute | solution.py:41
  34.7 10.0 %collective-permute-start.7 = (bf16[64,512]{1,0:T(8,128)(2,1)S(1)}, bf16[64,512]{1,0:T(8,128)(2,1)S(1)}, u32[]{:S(2)}, u32[]{:S(2)}) collective-permute-start(bf16[64,512]{1,0:T(8,128)(2,1)S(1)} %get-tuple-element.54), channel_id=1, source_target_pairs={{0,8},{1,9},{2,10},{3,11},{4,12},{5,13},{6,14},{7,15},{8,16},{9,17... | collective-permute-start | bytes 196616 | tf_op jit(solution)/shard_map/ppermute | solution.py:41
  35.4 10.0 %collective-permute-start.8 = (bf16[64,512]{1,0:T(8,128)(2,1)S(1)}, bf16[64,512]{1,0:T(8,128)(2,1)S(1)}, u32[]{:S(2)}, u32[]{:S(2)}) collective-permute-start(bf16[64,512]{1,0:T(8,128)(2,1)S(1)} %get-tuple-element.55), channel_id=1, source_target_pairs={{0,16},{1,17},{2,18},{3,19},{4,20},{5,21},{6,22},{7,23},{8,24},{9,... | collective-permute-start | bytes 196616 | tf_op jit(solution)/shard_map/ppermute | solution.py:41
  38.1 7.3 %collective-permute-start.9 = (bf16[64,512]{1,0:T(8,128)(2,1)S(1)}, bf16[64,512]{1,0:T(8,128)(2,1)S(1)}, u32[]{:S(2)}, u32[]{:S(2)}) collective-permute-start(bf16[64,512]{1,0:T(8,128)(2,1)S(1)} %get-tuple-element.56), channel_id=1, source_target_pairs={{0,24},{1,25},{2,26},{3,27},{4,28},{5,29},{6,30},{7,31},{8,0},{9,1... | collective-permute-start | bytes 196616 | tf_op jit(solution)/shard_map/ppermute | solution.py:41
  40.1 11.1 %collective-permute-start.18 = (bf16[4,64,512]{2,1,0:T(8,128)(2,1)S(1)}, bf16[4,64,512]{2,1,0:T(8,128)(2,1)S(1)}, u32[]{:S(2)}, u32[]{:S(2)}) collective-permute-start(bf16[4,64,512]{2,1,0:T(8,128)(2,1)S(1)} %collect_kernel.2.b0), channel_id=1, source_target_pairs={{0,2},{1,3},{2,4},{3,5},{4,6},{5,7},{6,0},{7,1},{8,10},{9,11},{10,... | collective-permute-start | bytes 786440 | tf_op jit(solution)/shard_map/ppermute | solution.py:41
  42.9 11.1 %collective-permute-start.19 = (bf16[4,64,512]{2,1,0:T(8,128)(2,1)S(1)}, bf16[4,64,512]{2,1,0:T(8,128)(2,1)S(1)}, u32[]{:S(2)}, u32[]{:S(2)}) collective-permute-start(bf16[4,64,512]{2,1,0:T(8,128)(2,1)S(1)} %collect_kernel.2.b0), channel_id=1, source_target_pairs={{0,4},{1,5},{2,6},{3,7},{4,0},{5,1},{6,2},{7,3},{8,12},{9,13},{10,... | collective-permute-start | bytes 786440 | tf_op jit(solution)/shard_map/ppermute | solution.py:41
  44.7 9.3 %collective-permute-start.20 = (bf16[4,64,512]{2,1,0:T(8,128)(2,1)S(1)}, bf16[4,64,512]{2,1,0:T(8,128)(2,1)S(1)}, u32[]{:S(2)}, u32[]{:S(2)}) collective-permute-start(bf16[4,64,512]{2,1,0:T(8,128)(2,1)S(1)} %collect_kernel.2.b0), channel_id=1, source_target_pairs={{0,6},{1,7},{2,0},{3,1},{4,2},{5,3},{6,4},{7,5},{8,14},{9,15},{10,... | collective-permute-start | bytes 786440 | tf_op jit(solution)/shard_map/ppermute | solution.py:41
  47.9 11.1 %collective-permute-start.10 = (bf16[6,64,128]{2,1,0:T(8,128)(2,1)S(1)}, bf16[6,64,128]{2,1,0:T(8,128)(2,1)S(1)}, u32[]{:S(2)}, u32[]{:S(2)}) collective-permute-start(bf16[6,64,128]{2,1,0:T(8,128)(2,1)S(1)} %get-tuple-element.62), channel_id=1, source_target_pairs={{0,32},{1,33},{2,34},{3,35},{4,36},{5,37},{6,38},{7,39},{8,40},{9,... | collective-permute-start | bytes 294920 | tf_op jit(solution)/shard_map/ppermute | solution.py:41
  49.0 10.0 %collective-permute-start.11 = (bf16[6,64,128]{2,1,0:T(8,128)(2,1)S(1)}, bf16[6,64,128]{2,1,0:T(8,128)(2,1)S(1)}, u32[]{:S(2)}, u32[]{:S(2)}) collective-permute-start(bf16[6,64,128]{2,1,0:T(8,128)(2,1)S(1)} %get-tuple-element.63), channel_id=1, source_target_pairs={{0,64},{1,65},{2,66},{3,67},{4,68},{5,69},{6,70},{7,71},{8,72},{9,... | collective-permute-start | bytes 294920 | tf_op jit(solution)/shard_map/ppermute | solution.py:41
  51.2 7.9 %collective-permute-start.12 = (bf16[6,64,128]{2,1,0:T(8,128)(2,1)S(1)}, bf16[6,64,128]{2,1,0:T(8,128)(2,1)S(1)}, u32[]{:S(2)}, u32[]{:S(2)}) collective-permute-start(bf16[6,64,128]{2,1,0:T(8,128)(2,1)S(1)} %get-tuple-element.64), channel_id=1, source_target_pairs={{0,96},{1,97},{2,98},{3,99},{4,100},{5,101},{6,102},{7,103},{8,104... | collective-permute-start | bytes 294920 | tf_op jit(solution)/shard_map/ppermute | solution.py:41
  54.0 6.0 %collective-permute-start.21 = (bf16[4,4,64,512]{3,2,1,0:T(8,128)(2,1)S(1)}, bf16[4,4,64,512]{3,2,1,0:T(8,128)(2,1)S(1)}, u32[]{:S(2)}, u32[]{:S(2)}) collective-permute-start(bf16[4,4,64,512]{3,2,1,0:T(8,128)(2,1)S(1)} %collect_kernel.3.blocks), channel_id=1, source_target_pairs={{0,1},{1,0},{2,3},{3,2},{4,5},{5,4},{6,7},{7,6},{8,9},{9,8},{10,11... | collective-permute-start | bytes 3145736 | tf_op jit(solution)/shard_map/ppermute | solution.py:41

commit v5 on v4

--- a/solution.py
+++ b/solution.py
@@ -17,7 +17,7 @@
 VMEM_LIMIT = 20 * 1024 * 1024
 WEIGHT = 3.5e10
 TIMES = dict(
-    pack=2, fetch=2, lift=2, core=2, pre=2, relay=0.3, collect=0.3, sum=0.3, post=3, out=1, weight=2, near=0
+    pack=2, fetch=2, lift=2, core=2, pre=2, relay=0, collect=0, sum=0.3, post=3, out=1, weight=2, near=0, pair=0, gate=0.3
 )
 
 
@@ -333,7 +333,11 @@
         taps_out[stream] = rows[stream * 8 : stream * 8 + TAPS]
 
 
-def pair_kernel(b0, b1, out):
+def gate_kernel(block, out):
+    out[...] = block[0, 0:8, 0:128]
+
+
+def pair_kernel(b0, b1, behind, out):
     out[0] = b0[...]
     out[1] = b1[...]
 
@@ -447,8 +451,14 @@
         time=TIMES["core"],
     )
     recvs = [along_y(sends[k - 1], k) for k in (1, 2, 3)]
+    gate = call(gate_kernel, kept((8, 128), BF16), sends[2], time=TIMES["gate"])
     pair = call(
-        pair_kernel, kept((2, 64, 512), BF16), mixed, along_z(mixed, 1), time=TIMES["relay"]
+        pair_kernel,
+        kept((2, 64, 512), BF16),
+        mixed,
+        along_z(mixed, 1),
+        gate,
+        time=TIMES["pair"],
     )
     routed = call(
         route_kernel,

time: 61.5 us -> 60.1 us (0.977)
  waiting for transfers between devices: 9.28 us -> 8.41 us
    ppermute x22, waiting for transfers between devices: 9.28 us -> 8.41 us  [move(): return lax.ppermute(array, ('ctx', 'ch'), pairs)]
    pallas_call x14 -> x15, Pallas kernels: 12.2 us -> 12.2 us  [call(): pl.pallas_call(kernel, out_shape=out_shape, name=kernel.__name__, in_spec...]
  transfers between devices with their start and end apart: 22 -> 22, of which waited for: 6 -> 3; matrix products, arithmetic and copies ran while one was open for 0% -> 0% of each run, Pallas kernels for 12% -> 15%
where the time goes in v5:
time: 60.1 us; the launch traced here: 59.9 us
  starting transfers between devices  38.4 us (64%)
  Pallas kernels  12.2 us (20%)
  waiting for transfers between devices  8.41 us (14%)
  between operations  0.76 us (1%)
    ppermute x22, starting transfers between devices, move(): return lax.ppermute(array, ('ctx', 'ch'), pairs)  38.4 us
    pallas_call x15, Pallas kernels, call(): pl.pallas_call(kernel, out_shape=out_shape, name=kernel.__name__, in_spec...  12.2 us
    ppermute x22, waiting for transfers between devices, move(): return lax.ppermute(array, ('ctx', 'ch'), pairs)  8.41 us
  transfers between devices with their start and end apart: 22, of which 3 were waited for; matrix products, arithmetic and copies ran while one was open for 0% of the time, Pallas kernels for 15%

profile of v5, /device:TPU:1, one launch (start us, length us, event | category | flops | bytes accessed | tf_op | source)
XLA Modules:
  0.0 59.9 jit_solution(7800640505934926908)
XLA Ops:
  0.6 1.2 %pack_kernel.1 = (bf16[8,64,128]{2,1,0:T(8,128)(2,1)S(1)}, bf16[8,64,128]{2,1,0:T(8,128)(2,1)S(1)}, bf16[8,64,128]{2,1,0:T(8,128)(2,1)S(1)}, bf16[8,64,128]{2,1,0:T(8,128)(2,1)S(1)}, f32[64,128]{1,0:T(8,128)S(1)}) custom-call(bf16[3,128,256]{2,1,0:T(8,128)(2,1)} %feat_hbm.1, bf16[128,256]{1,0:T(8,128)(2,1)} %filt_hbm.1, f32[3,7,256]{2,1,0:T(8,128)} %taps_hbm.1, ...), custom_call_target="tpu_custom_call" | custom-call | flops 70000001024 | bytes 7000000 | tf_op jit(solution)/shard_map/pack_kernel/pallas_call | solution.py:83
  1.9 2.1 %collective-permute-start = (bf16[8,64,128]{2,1,0:T(8,128)(2,1)S(1)}, bf16[8,64,128]{2,1,0:T(8,128)(2,1)S(1)}, u32[]{:S(2)}, u32[]{:S(2)}) collective-permute-start(bf16[8,64,128]{2,1,0:T(8,128)(2,1)S(1)} %get-tuple-element.39), channel_id=1, source_target_pairs={{0,32},{1,33},{2,34},{3,35},{4,36},{5,37},{6,38},{7,39},{8,40},{9,... | collective-permute-start | bytes 393224 | tf_op jit(solution)/shard_map/ppermute | solution.py:41
  4.0 2.5 %collective-permute-start.1 = (bf16[8,64,128]{2,1,0:T(8,128)(2,1)S(1)}, bf16[8,64,128]{2,1,0:T(8,128)(2,1)S(1)}, u32[]{:S(2)}, u32[]{:S(2)}) collective-permute-start(bf16[8,64,128]{2,1,0:T(8,128)(2,1)S(1)} %get-tuple-element.40), channel_id=1, source_target_pairs={{0,64},{1,65},{2,66},{3,67},{4,68},{5,69},{6,70},{7,71},{8,72},{9,... | collective-permute-start | bytes 393224 | tf_op jit(solution)/shard_map/ppermute | solution.py:41
  6.5 1.1 %collective-permute-start.2 = (bf16[8,64,128]{2,1,0:T(8,128)(2,1)S(1)}, bf16[8,64,128]{2,1,0:T(8,128)(2,1)S(1)}, u32[]{:S(2)}, u32[]{:S(2)}) collective-permute-start(bf16[8,64,128]{2,1,0:T(8,128)(2,1)S(1)} %get-tuple-element.41), channel_id=1, source_target_pairs={{0,96},{1,97},{2,98},{3,99},{4,100},{5,101},{6,102},{7,103},{8,104... | collective-permute-start | bytes 393224 | tf_op jit(solution)/shard_map/ppermute | solution.py:41
  7.6 2.1 %fetch_kernel.1 = (bf16[2,4,4,64,256]{4,3,2,1,0:T(8,128)(2,1)S(1)}, bf16[512,1024]{1,0:T(8,128)(2,1)S(1)}, bf16[512,1024]{1,0:T(8,128)(2,1)S(1)}) custom-call(bf16[4,4,2,4,64,256]{5,4,3,2,1,0:T(8,128)(2,1)} %bitcast.3, bf16[512,1024]{1,0:T(8,128)(2,1)} %constant.4.clone.high_hbm, bf16[512,1024]{1,0:T(8,128)(2,1)} %constant.5.clone.low_hbm, ...), custom_call_target="tpu_custom_call" | custom-call | flops 70000001024 | bytes 7000000 | tf_op jit(solution)/shard_map/fetch_kernel/pallas_call | solution.py:83
  9.7 2.5 %collective-permute-done.1.r2 = bf16[8,64,128]{2,1,0:T(8,128)(2,1)S(1)} collective-permute-done((bf16[8,64,128]{2,1,0:T(8,128)(2,1)S(1)}, bf16[8,64,128]{2,1,0:T(8,128)(2,1)S(1)}, u32[]{:S(2)}, u32[]{:S(2)}) %collective-permute-start.1) | collective-permute-done | bytes 131104 | tf_op jit(solution)/shard_map/ppermute | solution.py:41
  12.2 0.5 lift_kernel.1
  12.7 1.6 %collective-permute-start.3 = (bf16[4,4,64,512]{3,2,1,0:T(8,128)(2,1)S(1)}, bf16[4,4,64,512]{3,2,1,0:T(8,128)(2,1)S(1)}, u32[]{:S(2)}, u32[]{:S(2)}) collective-permute-start(bf16[4,4,64,512]{3,2,1,0:T(8,128)(2,1)S(1)} %get-tuple-element.44), channel_id=1, source_target_pairs={{0,1},{1,0},{2,3},{3,2},{4,5},{5,4},{6,7},{7,6},{8,9},{9,8},{10,11... | collective-permute-start | bytes 3145736 | tf_op jit(solution)/shard_map/ppermute | solution.py:41
  14.3 1.6 %pre_kernel.1 = (bf16[64,512]{1,0:T(8,128)(2,1)S(1)}, f32[3,64,512]{2,1,0:T(8,128)S(1)}, f32[64,512]{1,0:T(8,128)S(1)}, f32[128,1024]{1,0:T(8,128)S(1)}, bf16[3,64,512]{2,1,0:T(8,128)(2,1)S(1)}) custom-call(bf16[8,64,128]{2,1,0:T(8,128)(2,1)S(1)} %get-tuple-element.38.p0, bf16[8,64,128]{2,1,0:T(8,128)(2,1)S(1)} %collective-permute-done.r1, ...), custom_call_target="tpu_custom_call" | custom-call | flops 70000001024 | bytes 7000000 | tf_op jit(solution)/shard_map/pre_kernel/pallas_call | solution.py:83
  16.0 1.7 %collective-permute-start.13 = (bf16[64,512]{1,0:T(8,128)(2,1)S(1)}, bf16[64,512]{1,0:T(8,128)(2,1)S(1)}, u32[]{:S(2)}, u32[]{:S(2)}) collective-permute-start(bf16[64,512]{1,0:T(8,128)(2,1)S(1)} %get-tuple-element.48.behind.b0), channel_id=1, source_target_pairs={{0,8},{1,9},{2,10},{3,11},{4,12},{5,13},{6,14},{7,15},{8,16},{9,17... | collective-permute-start | bytes 196616 | tf_op jit(solution)/shard_map/ppermute | solution.py:41
  18.2 1.4 %collective-permute-start.4 = (bf16[4,64,512]{2,1,0:T(8,128)(2,1)S(1)}, bf16[4,64,512]{2,1,0:T(8,128)(2,1)S(1)}, u32[]{:S(2)}, u32[]{:S(2)}) collective-permute-start(bf16[4,64,512]{2,1,0:T(8,128)(2,1)S(1)} %get-tuple-element.50), channel_id=1, source_target_pairs={{0,2},{1,3},{2,4},{3,5},{4,6},{5,7},{6,0},{7,1},{8,10},{9,11},{10,... | collective-permute-start | bytes 786440 | tf_op jit(solution)/shard_map/ppermute | solution.py:41
  19.5 2.6 %collective-permute-start.5 = (bf16[4,64,512]{2,1,0:T(8,128)(2,1)S(1)}, bf16[4,64,512]{2,1,0:T(8,128)(2,1)S(1)}, u32[]{:S(2)}, u32[]{:S(2)}) collective-permute-start(bf16[4,64,512]{2,1,0:T(8,128)(2,1)S(1)} %get-tuple-element.51), channel_id=1, source_target_pairs={{0,4},{1,5},{2,6},{3,7},{4,0},{5,1},{6,2},{7,3},{8,12},{9,13},{10,... | collective-permute-start | bytes 786440 | tf_op jit(solution)/shard_map/ppermute | solution.py:41
  22.2 1.1 %collective-permute-start.6 = (bf16[4,64,512]{2,1,0:T(8,128)(2,1)S(1)}, bf16[4,64,512]{2,1,0:T(8,128)(2,1)S(1)}, u32[]{:S(2)}, u32[]{:S(2)}) collective-permute-start(bf16[4,64,512]{2,1,0:T(8,128)(2,1)S(1)} %get-tuple-element.52.block), channel_id=1, source_target_pairs={{0,6},{1,7},{2,0},{3,1},{4,2},{5,3},{6,4},{7,5},{8,14},{9,15},{10,... | collective-permute-start | bytes 786440 | tf_op jit(solution)/shard_map/ppermute | solution.py:41
  23.3 3.4 %collective-permute-start.14 = (bf16[2,64,512]{2,1,0:T(8,128)(2,1)S(1)}, bf16[2,64,512]{2,1,0:T(8,128)(2,1)S(1)}, u32[]{:S(2)}, u32[]{:S(2)}) collective-permute-start(bf16[2,64,512]{2,1,0:T(8,128)(2,1)S(1)} %pair_kernel.1.near), channel_id=1, source_target_pairs={{0,16},{1,17},{2,18},{3,19},{4,20},{5,21},{6,22},{7,23},{8,24},{9,... | collective-permute-start | bytes 393224 | tf_op jit(solution)/shard_map/ppermute | solution.py:41
  26.6 2.7 %collective-permute-done.14.far = bf16[2,64,512]{2,1,0:T(8,128)(2,1)S(1)} collective-permute-done((bf16[2,64,512]{2,1,0:T(8,128)(2,1)S(1)}, bf16[2,64,512]{2,1,0:T(8,128)(2,1)S(1)}, u32[]{:S(2)}, u32[]{:S(2)}) %collective-permute-start.14) | collective-permute-done | bytes 131104 | tf_op jit(solution)/shard_map/ppermute | solution.py:41
  29.4 1.1 %collective-permute-start.15 = (bf16[64,512]{1,0:T(8,128)(2,1)S(1)}, bf16[64,512]{1,0:T(8,128)(2,1)S(1)}, u32[]{:S(2)}, u32[]{:S(2)}) collective-permute-start(bf16[64,512]{1,0:T(8,128)(2,1)S(1)} %get-tuple-element.69), channel_id=1, source_target_pairs={{0,32},{1,33},{2,34},{3,35},{4,36},{5,37},{6,38},{7,39},{8,40},{9,... | collective-permute-start | bytes 196616 | tf_op jit(solution)/shard_map/ppermute | solution.py:41
  30.5 2.1 %collective-permute-start.16 = (bf16[64,512]{1,0:T(8,128)(2,1)S(1)}, bf16[64,512]{1,0:T(8,128)(2,1)S(1)}, u32[]{:S(2)}, u32[]{:S(2)}) collective-permute-start(bf16[64,512]{1,0:T(8,128)(2,1)S(1)} %get-tuple-element.70), channel_id=1, source_target_pairs={{0,64},{1,65},{2,66},{3,67},{4,68},{5,69},{6,70},{7,71},{8,72},{9,... | collective-permute-start | bytes 196616 | tf_op jit(solution)/shard_map/ppermute | solution.py:41
  32.6 1.3 %collective-permute-start.17 = (bf16[64,512]{1,0:T(8,128)(2,1)S(1)}, bf16[64,512]{1,0:T(8,128)(2,1)S(1)}, u32[]{:S(2)}, u32[]{:S(2)}) collective-permute-start(bf16[64,512]{1,0:T(8,128)(2,1)S(1)} %get-tuple-element.71), channel_id=1, source_target_pairs={{0,96},{1,97},{2,98},{3,99},{4,100},{5,101},{6,102},{7,103},{8,104... | collective-permute-start | bytes 196616 | tf_op jit(solution)/shard_map/ppermute | solution.py:41
  34.0 1.7 %collective-permute-start.7 = (bf16[64,512]{1,0:T(8,128)(2,1)S(1)}, bf16[64,512]{1,0:T(8,128)(2,1)S(1)}, u32[]{:S(2)}, u32[]{:S(2)}) collective-permute-start(bf16[64,512]{1,0:T(8,128)(2,1)S(1)} %get-tuple-element.54), channel_id=1, source_target_pairs={{0,8},{1,9},{2,10},{3,11},{4,12},{5,13},{6,14},{7,15},{8,16},{9,17... | collective-permute-start | bytes 196616 | tf_op jit(solution)/shard_map/ppermute | solution.py:41
  35.8 2.1 %collective-permute-start.8 = (bf16[64,512]{1,0:T(8,128)(2,1)S(1)}, bf16[64,512]{1,0:T(8,128)(2,1)S(1)}, u32[]{:S(2)}, u32[]{:S(2)}) collective-permute-start(bf16[64,512]{1,0:T(8,128)(2,1)S(1)} %get-tuple-element.55), channel_id=1, source_target_pairs={{0,16},{1,17},{2,18},{3,19},{4,20},{5,21},{6,22},{7,23},{8,24},{9,... | collective-permute-start | bytes 196616 | tf_op jit(solution)/shard_map/ppermute | solution.py:41
  37.9 1.6 %collective-permute-start.9 = (bf16[64,512]{1,0:T(8,128)(2,1)S(1)}, bf16[64,512]{1,0:T(8,128)(2,1)S(1)}, u32[]{:S(2)}, u32[]{:S(2)}) collective-permute-start(bf16[64,512]{1,0:T(8,128)(2,1)S(1)} %get-tuple-element.56), channel_id=1, source_target_pairs={{0,24},{1,25},{2,26},{3,27},{4,28},{5,29},{6,30},{7,31},{8,0},{9,1... | collective-permute-start | bytes 196616 | tf_op jit(solution)/shard_map/ppermute | solution.py:41
  39.5 0.9 %collective-permute-start.18 = (bf16[4,64,512]{2,1,0:T(8,128)(2,1)S(1)}, bf16[4,64,512]{2,1,0:T(8,128)(2,1)S(1)}, u32[]{:S(2)}, u32[]{:S(2)}) collective-permute-start(bf16[4,64,512]{2,1,0:T(8,128)(2,1)S(1)} %collect_kernel.2.b0), channel_id=1, source_target_pairs={{0,2},{1,3},{2,4},{3,5},{4,6},{5,7},{6,0},{7,1},{8,10},{9,11},{10,... | collective-permute-start | bytes 786440 | tf_op jit(solution)/shard_map/ppermute | solution.py:41
  40.4 2.8 %collective-permute-start.19 = (bf16[4,64,512]{2,1,0:T(8,128)(2,1)S(1)}, bf16[4,64,512]{2,1,0:T(8,128)(2,1)S(1)}, u32[]{:S(2)}, u32[]{:S(2)}) collective-permute-start(bf16[4,64,512]{2,1,0:T(8,128)(2,1)S(1)} %collect_kernel.2.b0), channel_id=1, source_target_pairs={{0,4},{1,5},{2,6},{3,7},{4,0},{5,1},{6,2},{7,3},{8,12},{9,13},{10,... | collective-permute-start | bytes 786440 | tf_op jit(solution)/shard_map/ppermute | solution.py:41
  43.7 2.5 %post_kernel.1 = (bf16[6,64,128]{2,1,0:T(8,128)(2,1)S(1)}, bf16[6,64,128]{2,1,0:T(8,128)(2,1)S(1)}, bf16[6,64,128]{2,1,0:T(8,128)(2,1)S(1)}, bf16[6,64,128]{2,1,0:T(8,128)(2,1)S(1)}) custom-call(f32[64,512]{1,0:T(8,128)S(1)} %get-tuple-element.53.own, bf16[64,512]{1,0:T(8,128)(2,1)S(1)} %collective-permute-done.7.r1, ...), custom_call_target="tpu_custom_call" | custom-call | flops 105000001536 | bytes 10500000 | tf_op jit(solution)/shard_map/post_kernel/pallas_call | solution.py:83
  46.2 1.1 %collective-permute-start.10 = (bf16[6,64,128]{2,1,0:T(8,128)(2,1)S(1)}, bf16[6,64,128]{2,1,0:T(8,128)(2,1)S(1)}, u32[]{:S(2)}, u32[]{:S(2)}) collective-permute-start(bf16[6,64,128]{2,1,0:T(8,128)(2,1)S(1)} %get-tuple-element.62), channel_id=1, source_target_pairs={{0,32},{1,33},{2,34},{3,35},{4,36},{5,37},{6,38},{7,39},{8,40},{9,... | collective-permute-start | bytes 294920 | tf_op jit(solution)/shard_map/ppermute | solution.py:41
  47.4 2.1 %collective-permute-start.11 = (bf16[6,64,128]{2,1,0:T(8,128)(2,1)S(1)}, bf16[6,64,128]{2,1,0:T(8,128)(2,1)S(1)}, u32[]{:S(2)}, u32[]{:S(2)}) collective-permute-start(bf16[6,64,128]{2,1,0:T(8,128)(2,1)S(1)} %get-tuple-element.63), channel_id=1, source_target_pairs={{0,64},{1,65},{2,66},{3,67},{4,68},{5,69},{6,70},{7,71},{8,72},{9,... | collective-permute-start | bytes 294920 | tf_op jit(solution)/shard_map/ppermute | solution.py:41
  49.5 1.3 %collective-permute-start.12 = (bf16[6,64,128]{2,1,0:T(8,128)(2,1)S(1)}, bf16[6,64,128]{2,1,0:T(8,128)(2,1)S(1)}, u32[]{:S(2)}, u32[]{:S(2)}) collective-permute-start(bf16[6,64,128]{2,1,0:T(8,128)(2,1)S(1)} %get-tuple-element.64), channel_id=1, source_target_pairs={{0,96},{1,97},{2,98},{3,99},{4,100},{5,101},{6,102},{7,103},{8,104... | collective-permute-start | bytes 294920 | tf_op jit(solution)/shard_map/ppermute | solution.py:41
  50.7 3.1 %collective-permute-done.19.b2 = bf16[4,64,512]{2,1,0:T(8,128)(2,1)S(1)} collective-permute-done((bf16[4,64,512]{2,1,0:T(8,128)(2,1)S(1)}, bf16[4,64,512]{2,1,0:T(8,128)(2,1)S(1)}, u32[]{:S(2)}, u32[]{:S(2)}) %collective-permute-start.19) | collective-permute-done | bytes 262176 | tf_op jit(solution)/shard_map/ppermute | solution.py:41
  54.0 2.3 %collective-permute-start.21 = (bf16[4,4,64,512]{3,2,1,0:T(8,128)(2,1)S(1)}, bf16[4,4,64,512]{3,2,1,0:T(8,128)(2,1)S(1)}, u32[]{:S(2)}, u32[]{:S(2)}) collective-permute-start(bf16[4,4,64,512]{3,2,1,0:T(8,128)(2,1)S(1)} %collect_kernel.3.blocks), channel_id=1, source_target_pairs={{0,1},{1,0},{2,3},{3,2},{4,5},{5,4},{6,7},{7,6},{8,9},{9,8},{10,11... | collective-permute-start | bytes 3145736 | tf_op jit(solution)/shard_map/ppermute | solution.py:41
  56.3 0.9 %out_kernel.1 = (bf16[3,128,256]{2,1,0:T(8,128)(2,1)}, f32[3,7,256]{2,1,0:T(8,128)}, f32[128,256]{1,0:T(8,128)}) custom-call(bf16[6,64,128]{2,1,0:T(8,128)(2,1)S(1)} %get-tuple-element.61.o0, bf16[6,64,128]{2,1,0:T(8,128)(2,1)S(1)} %collective-permute-done.10.r1, bf16[6,64,128]{2,1,0:T(8,128)(2,1)S(1)} %collective-permute-done.11.r2, ...), custom_call_target="tpu_custom_call" | custom-call | flops 35000000512 | bytes 3500000 | tf_op jit(solution)/shard_map/out_kernel/pallas_call | solution.py:83
  57.3 1.3 %near_kernel.1.held = f32[4,2,4,64,256]{4,3,2,1,0:T(8,128)} custom-call(bf16[4,4,64,512]{3,2,1,0:T(8,128)(2,1)S(1)} %collect_kernel.3.blocks, bf16[512,256]{1,0:T(8,128)(2,1)S(1)} %copy-done.1), custom_call_target="tpu_custom_call" | custom-call | tf_op jit(solution)/shard_map/near_kernel/pallas_call | solution.py:83
  58.6 1.3 %far_kernel.1 = f32[4,2,4,64,256]{4,3,2,1,0:T(8,128)} custom-call(bf16[4,4,64,512]{3,2,1,0:T(8,128)(2,1)S(1)} %collective-permute-done.21.blocks, bf16[512,256]{1,0:T(8,128)(2,1)S(1)} %copy-done.1, f32[4,2,4,64,256]{4,3,2,1,0:T(8,128)} %near_kernel.1.held), custom_call_target="tpu_custom_call", output_to_operand_aliasing={{}: (2, {})} | custom-call | flops 70000001024 | bytes 7000000 | tf_op jit(solution)/shard_map/far_kernel/pallas_call | solution.py:83
  (31 shorter events, 1.3 us)
Async XLA Ops:
  1.9 7.8 %collective-permute-start = (bf16[8,64,128]{2,1,0:T(8,128)(2,1)S(1)}, bf16[8,64,128]{2,1,0:T(8,128)(2,1)S(1)}, u32[]{:S(2)}, u32[]{:S(2)}) collective-permute-start(bf16[8,64,128]{2,1,0:T(8,128)(2,1)S(1)} %get-tuple-element.39), channel_id=1, source_target_pairs={{0,32},{1,33},{2,34},{3,35},{4,36},{5,37},{6,38},{7,39},{8,40},{9,... | collective-permute-start | bytes 393224 | tf_op jit(solution)/shard_map/ppermute | solution.py:41
  4.0 8.2 %collective-permute-start.1 = (bf16[8,64,128]{2,1,0:T(8,128)(2,1)S(1)}, bf16[8,64,128]{2,1,0:T(8,128)(2,1)S(1)}, u32[]{:S(2)}, u32[]{:S(2)}) collective-permute-start(bf16[8,64,128]{2,1,0:T(8,128)(2,1)S(1)} %get-tuple-element.40), channel_id=1, source_target_pairs={{0,64},{1,65},{2,66},{3,67},{4,68},{5,69},{6,70},{7,71},{8,72},{9,... | collective-permute-start | bytes 393224 | tf_op jit(solution)/shard_map/ppermute | solution.py:41
  6.5 5.7 %collective-permute-start.2 = (bf16[8,64,128]{2,1,0:T(8,128)(2,1)S(1)}, bf16[8,64,128]{2,1,0:T(8,128)(2,1)S(1)}, u32[]{:S(2)}, u32[]{:S(2)}) collective-permute-start(bf16[8,64,128]{2,1,0:T(8,128)(2,1)S(1)} %get-tuple-element.41), channel_id=1, source_target_pairs={{0,96},{1,97},{2,98},{3,99},{4,100},{5,101},{6,102},{7,103},{8,104... | collective-permute-start | bytes 393224 | tf_op jit(solution)/shard_map/ppermute | solution.py:41
  12.7 5.0 %copy-start = (bf16[512,256]{1,0:T(8,128)(2,1)}, bf16[512,256]{1,0:T(8,128)(2,1)S(1)}, u32[]{:S(2)}) copy-start(bf16[512,256]{1,0:T(8,128)(2,1)S(1)} %get-tuple-element.45.behind.whole) | copy-start | bytes 786436
  12.7 5.0 %collective-permute-start.3 = (bf16[4,4,64,512]{3,2,1,0:T(8,128)(2,1)S(1)}, bf16[4,4,64,512]{3,2,1,0:T(8,128)(2,1)S(1)}, u32[]{:S(2)}, u32[]{:S(2)}) collective-permute-start(bf16[4,4,64,512]{3,2,1,0:T(8,128)(2,1)S(1)} %get-tuple-element.44), channel_id=1, source_target_pairs={{0,1},{1,0},{2,3},{3,2},{4,5},{5,4},{6,7},{7,6},{8,9},{9,8},{10,11... | collective-permute-start | bytes 3145736 | tf_op jit(solution)/shard_map/ppermute | solution.py:41
  16.0 7.2 %collective-permute-start.13 = (bf16[64,512]{1,0:T(8,128)(2,1)S(1)}, bf16[64,512]{1,0:T(8,128)(2,1)S(1)}, u32[]{:S(2)}, u32[]{:S(2)}) collective-permute-start(bf16[64,512]{1,0:T(8,128)(2,1)S(1)} %get-tuple-element.48.behind.b0), channel_id=1, source_target_pairs={{0,8},{1,9},{2,10},{3,11},{4,12},{5,13},{6,14},{7,15},{8,16},{9,17... | collective-permute-start | bytes 196616 | tf_op jit(solution)/shard_map/ppermute | solution.py:41
  18.2 14.4 %collective-permute-start.4 = (bf16[4,64,512]{2,1,0:T(8,128)(2,1)S(1)}, bf16[4,64,512]{2,1,0:T(8,128)(2,1)S(1)}, u32[]{:S(2)}, u32[]{:S(2)}) collective-permute-start(bf16[4,64,512]{2,1,0:T(8,128)(2,1)S(1)} %get-tuple-element.50), channel_id=1, source_target_pairs={{0,2},{1,3},{2,4},{3,5},{4,6},{5,7},{6,0},{7,1},{8,10},{9,11},{10,... | collective-permute-start | bytes 786440 | tf_op jit(solution)/shard_map/ppermute | solution.py:41
  19.5 14.4 %collective-permute-start.5 = (bf16[4,64,512]{2,1,0:T(8,128)(2,1)S(1)}, bf16[4,64,512]{2,1,0:T(8,128)(2,1)S(1)}, u32[]{:S(2)}, u32[]{:S(2)}) collective-permute-start(bf16[4,64,512]{2,1,0:T(8,128)(2,1)S(1)} %get-tuple-element.51), channel_id=1, source_target_pairs={{0,4},{1,5},{2,6},{3,7},{4,0},{5,1},{6,2},{7,3},{8,12},{9,13},{10,... | collective-permute-start | bytes 786440 | tf_op jit(solution)/shard_map/ppermute | solution.py:41
  22.2 11.8 %collective-permute-start.6 = (bf16[4,64,512]{2,1,0:T(8,128)(2,1)S(1)}, bf16[4,64,512]{2,1,0:T(8,128)(2,1)S(1)}, u32[]{:S(2)}, u32[]{:S(2)}) collective-permute-start(bf16[4,64,512]{2,1,0:T(8,128)(2,1)S(1)} %get-tuple-element.52.block), channel_id=1, source_target_pairs={{0,6},{1,7},{2,0},{3,1},{4,2},{5,3},{6,4},{7,5},{8,14},{9,15},{10,... | collective-permute-start | bytes 786440 | tf_op jit(solution)/shard_map/ppermute | solution.py:41
  23.3 6.1 %collective-permute-start.14 = (bf16[2,64,512]{2,1,0:T(8,128)(2,1)S(1)}, bf16[2,64,512]{2,1,0:T(8,128)(2,1)S(1)}, u32[]{:S(2)}, u32[]{:S(2)}) collective-permute-start(bf16[2,64,512]{2,1,0:T(8,128)(2,1)S(1)} %pair_kernel.1.near), channel_id=1, source_target_pairs={{0,16},{1,17},{2,18},{3,19},{4,20},{5,21},{6,22},{7,23},{8,24},{9,... | collective-permute-start | bytes 393224 | tf_op jit(solution)/shard_map/ppermute | solution.py:41
  29.4 8.5 %collective-permute-start.15 = (bf16[64,512]{1,0:T(8,128)(2,1)S(1)}, bf16[64,512]{1,0:T(8,128)(2,1)S(1)}, u32[]{:S(2)}, u32[]{:S(2)}) collective-permute-start(bf16[64,512]{1,0:T(8,128)(2,1)S(1)} %get-tuple-element.69), channel_id=1, source_target_pairs={{0,32},{1,33},{2,34},{3,35},{4,36},{5,37},{6,38},{7,39},{8,40},{9,... | collective-permute-start | bytes 196616 | tf_op jit(solution)/shard_map/ppermute | solution.py:41
  30.5 9.0 %collective-permute-start.16 = (bf16[64,512]{1,0:T(8,128)(2,1)S(1)}, bf16[64,512]{1,0:T(8,128)(2,1)S(1)}, u32[]{:S(2)}, u32[]{:S(2)}) collective-permute-start(bf16[64,512]{1,0:T(8,128)(2,1)S(1)} %get-tuple-element.70), channel_id=1, source_target_pairs={{0,64},{1,65},{2,66},{3,67},{4,68},{5,69},{6,70},{7,71},{8,72},{9,... | collective-permute-start | bytes 196616 | tf_op jit(solution)/shard_map/ppermute | solution.py:41
  32.6 6.9 %collective-permute-start.17 = (bf16[64,512]{1,0:T(8,128)(2,1)S(1)}, bf16[64,512]{1,0:T(8,128)(2,1)S(1)}, u32[]{:S(2)}, u32[]{:S(2)}) collective-permute-start(bf16[64,512]{1,0:T(8,128)(2,1)S(1)} %get-tuple-element.71), channel_id=1, source_target_pairs={{0,96},{1,97},{2,98},{3,99},{4,100},{5,101},{6,102},{7,103},{8,104... | collective-permute-start | bytes 196616 | tf_op jit(solution)/shard_map/ppermute | solution.py:41
  34.0 9.2 %collective-permute-start.7 = (bf16[64,512]{1,0:T(8,128)(2,1)S(1)}, bf16[64,512]{1,0:T(8,128)(2,1)S(1)}, u32[]{:S(2)}, u32[]{:S(2)}) collective-permute-start(bf16[64,512]{1,0:T(8,128)(2,1)S(1)} %get-tuple-element.54), channel_id=1, source_target_pairs={{0,8},{1,9},{2,10},{3,11},{4,12},{5,13},{6,14},{7,15},{8,16},{9,17... | collective-permute-start | bytes 196616 | tf_op jit(solution)/shard_map/ppermute | solution.py:41
  35.8 7.9 %collective-permute-start.8 = (bf16[64,512]{1,0:T(8,128)(2,1)S(1)}, bf16[64,512]{1,0:T(8,128)(2,1)S(1)}, u32[]{:S(2)}, u32[]{:S(2)}) collective-permute-start(bf16[64,512]{1,0:T(8,128)(2,1)S(1)} %get-tuple-element.55), channel_id=1, source_target_pairs={{0,16},{1,17},{2,18},{3,19},{4,20},{5,21},{6,22},{7,23},{8,24},{9,... | collective-permute-start | bytes 196616 | tf_op jit(solution)/shard_map/ppermute | solution.py:41
  37.9 5.8 %collective-permute-start.9 = (bf16[64,512]{1,0:T(8,128)(2,1)S(1)}, bf16[64,512]{1,0:T(8,128)(2,1)S(1)}, u32[]{:S(2)}, u32[]{:S(2)}) collective-permute-start(bf16[64,512]{1,0:T(8,128)(2,1)S(1)} %get-tuple-element.56), channel_id=1, source_target_pairs={{0,24},{1,25},{2,26},{3,27},{4,28},{5,29},{6,30},{7,31},{8,0},{9,1... | collective-permute-start | bytes 196616 | tf_op jit(solution)/shard_map/ppermute | solution.py:41
  39.5 9.9 %collective-permute-start.18 = (bf16[4,64,512]{2,1,0:T(8,128)(2,1)S(1)}, bf16[4,64,512]{2,1,0:T(8,128)(2,1)S(1)}, u32[]{:S(2)}, u32[]{:S(2)}) collective-permute-start(bf16[4,64,512]{2,1,0:T(8,128)(2,1)S(1)} %collect_kernel.2.b0), channel_id=1, source_target_pairs={{0,2},{1,3},{2,4},{3,5},{4,6},{5,7},{6,0},{7,1},{8,10},{9,11},{10,... | collective-permute-start | bytes 786440 | tf_op jit(solution)/shard_map/ppermute | solution.py:41
  40.4 13.4 %collective-permute-start.19 = (bf16[4,64,512]{2,1,0:T(8,128)(2,1)S(1)}, bf16[4,64,512]{2,1,0:T(8,128)(2,1)S(1)}, u32[]{:S(2)}, u32[]{:S(2)}) collective-permute-start(bf16[4,64,512]{2,1,0:T(8,128)(2,1)S(1)} %collect_kernel.2.b0), channel_id=1, source_target_pairs={{0,4},{1,5},{2,6},{3,7},{4,0},{5,1},{6,2},{7,3},{8,12},{9,13},{10,... | collective-permute-start | bytes 786440 | tf_op jit(solution)/shard_map/ppermute | solution.py:41
  43.3 10.6 %collective-permute-start.20 = (bf16[4,64,512]{2,1,0:T(8,128)(2,1)S(1)}, bf16[4,64,512]{2,1,0:T(8,128)(2,1)S(1)}, u32[]{:S(2)}, u32[]{:S(2)}) collective-permute-start(bf16[4,64,512]{2,1,0:T(8,128)(2,1)S(1)} %collect_kernel.2.b0), channel_id=1, source_target_pairs={{0,6},{1,7},{2,0},{3,1},{4,2},{5,3},{6,4},{7,5},{8,14},{9,15},{10,... | collective-permute-start | bytes 786440 | tf_op jit(solution)/shard_map/ppermute | solution.py:41
  46.2 10.1 %collective-permute-start.10 = (bf16[6,64,128]{2,1,0:T(8,128)(2,1)S(1)}, bf16[6,64,128]{2,1,0:T(8,128)(2,1)S(1)}, u32[]{:S(2)}, u32[]{:S(2)}) collective-permute-start(bf16[6,64,128]{2,1,0:T(8,128)(2,1)S(1)} %get-tuple-element.62), channel_id=1, source_target_pairs={{0,32},{1,33},{2,34},{3,35},{4,36},{5,37},{6,38},{7,39},{8,40},{9,... | collective-permute-start | bytes 294920 | tf_op jit(solution)/shard_map/ppermute | solution.py:41
  47.4 9.0 %collective-permute-start.11 = (bf16[6,64,128]{2,1,0:T(8,128)(2,1)S(1)}, bf16[6,64,128]{2,1,0:T(8,128)(2,1)S(1)}, u32[]{:S(2)}, u32[]{:S(2)}) collective-permute-start(bf16[6,64,128]{2,1,0:T(8,128)(2,1)S(1)} %get-tuple-element.63), channel_id=1, source_target_pairs={{0,64},{1,65},{2,66},{3,67},{4,68},{5,69},{6,70},{7,71},{8,72},{9,... | collective-permute-start | bytes 294920 | tf_op jit(solution)/shard_map/ppermute | solution.py:41
  49.5 6.8 %collective-permute-start.12 = (bf16[6,64,128]{2,1,0:T(8,128)(2,1)S(1)}, bf16[6,64,128]{2,1,0:T(8,128)(2,1)S(1)}, u32[]{:S(2)}, u32[]{:S(2)}) collective-permute-start(bf16[6,64,128]{2,1,0:T(8,128)(2,1)S(1)} %get-tuple-element.64), channel_id=1, source_target_pairs={{0,96},{1,97},{2,98},{3,99},{4,100},{5,101},{6,102},{7,103},{8,104... | collective-permute-start | bytes 294920 | tf_op jit(solution)/shard_map/ppermute | solution.py:41
  54.0 4.6 %collective-permute-start.21 = (bf16[4,4,64,512]{3,2,1,0:T(8,128)(2,1)S(1)}, bf16[4,4,64,512]{3,2,1,0:T(8,128)(2,1)S(1)}, u32[]{:S(2)}, u32[]{:S(2)}) collective-permute-start(bf16[4,4,64,512]{3,2,1,0:T(8,128)(2,1)S(1)} %collect_kernel.3.blocks), channel_id=1, source_target_pairs={{0,1},{1,0},{2,3},{3,2},{4,5},{5,4},{6,7},{7,6},{8,9},{9,8},{10,11... | collective-permute-start | bytes 3145736 | tf_op jit(solution)/shard_map/ppermute | solution.py:41
  56.3 1.0 %copy-start.1 = (bf16[512,256]{1,0:T(8,128)(2,1)S(1)}, bf16[512,256]{1,0:T(8,128)(2,1)}, u32[]{:S(2)}) copy-start(bf16[512,256]{1,0:T(8,128)(2,1)} %copy-done) | copy-start | bytes 786436

commit v6 on v5

--- a/solution.py
+++ b/solution.py
@@ -345,7 +345,7 @@
 def route_kernel(near, far, o0, o1, o2, o3, held):
     x, z = coords()[:2]
     for back in range(4):
-        held[lax.rem(z + 4 - back, 4)] = (near if back < 2 else far)[back % 2]
+        held[lax.rem(z + 4 - back, 4)] = (far if back % 2 else near)[back // 2]
     for by, out in enumerate((o0, o1, o2, o3)):
         out[...] = held[lax.rem(x + by, 4)]
 
@@ -456,7 +456,7 @@
         pair_kernel,
         kept((2, 64, 512), BF16),
         mixed,
-        along_z(mixed, 1),
+        along_z(mixed, 2),
         gate,
         time=TIMES["pair"],
     )
@@ -464,7 +464,7 @@
         route_kernel,
         [kept((64, 512), BF16)] * 4,
         pair,
-        along_z(pair, 2),
+        along_z(pair, 1),
         scratch=[pltpu.VMEM((4, 64, 512), BF16)],
         time=TIMES["relay"],
     )

time: 60.1 us -> 59.9 us (level)
  starting transfers between devices: 38.4 us -> 35.4 us
  waiting for transfers between devices: 8.41 us -> 11.3 us
    ppermute x22, starting transfers between devices: 38.4 us -> 35.4 us  [move(): return lax.ppermute(array, ('ctx', 'ch'), pairs)]
    ppermute x22, waiting for transfers between devices: 8.41 us -> 11.3 us  [move(): return lax.ppermute(array, ('ctx', 'ch'), pairs)]
  transfers between devices with their start and end apart: 22 -> 22, of which waited for: 3 -> 4; matrix products, arithmetic and copies ran while one was open for 0% -> 0% of each run, Pallas kernels for 15% -> 15%
where the time goes in v6:
time: 59.9 us; the launch traced here: 59.7 us
  starting transfers between devices  35.4 us (59%)
  Pallas kernels  12.2 us (20%)
  waiting for transfers between devices  11.3 us (19%)
  between operations  0.76 us (1%)
    ppermute x22, starting transfers between devices, move(): return lax.ppermute(array, ('ctx', 'ch'), pairs)  35.4 us
    pallas_call x15, Pallas kernels, call(): pl.pallas_call(kernel, out_shape=out_shape, name=kernel.__name__, in_spec...  12.2 us
    ppermute x22, waiting for transfers between devices, move(): return lax.ppermute(array, ('ctx', 'ch'), pairs)  11.3 us
  transfers between devices with their start and end apart: 22, of which 4 were waited for; matrix products, arithmetic and copies ran while one was open for 0% of the time, Pallas kernels for 15%

profile of v6, /device:TPU:1, one launch (start us, length us, event | category | flops | bytes accessed | tf_op | source)
XLA Modules:
  0.0 59.7 jit_solution(16146056576227018151)
XLA Ops:
  0.6 1.2 %pack_kernel.1 = (bf16[8,64,128]{2,1,0:T(8,128)(2,1)S(1)}, bf16[8,64,128]{2,1,0:T(8,128)(2,1)S(1)}, bf16[8,64,128]{2,1,0:T(8,128)(2,1)S(1)}, bf16[8,64,128]{2,1,0:T(8,128)(2,1)S(1)}, f32[64,128]{1,0:T(8,128)S(1)}) custom-call(bf16[3,128,256]{2,1,0:T(8,128)(2,1)} %feat_hbm.1, bf16[128,256]{1,0:T(8,128)(2,1)} %filt_hbm.1, f32[3,7,256]{2,1,0:T(8,128)} %taps_hbm.1, ...), custom_call_target="tpu_custom_call" | custom-call | flops 70000001024 | bytes 7000000 | tf_op jit(solution)/shard_map/pack_kernel/pallas_call | solution.py:83
  1.9 2.1 %collective-permute-start = (bf16[8,64,128]{2,1,0:T(8,128)(2,1)S(1)}, bf16[8,64,128]{2,1,0:T(8,128)(2,1)S(1)}, u32[]{:S(2)}, u32[]{:S(2)}) collective-permute-start(bf16[8,64,128]{2,1,0:T(8,128)(2,1)S(1)} %get-tuple-element.39), channel_id=1, source_target_pairs={{0,32},{1,33},{2,34},{3,35},{4,36},{5,37},{6,38},{7,39},{8,40},{9,... | collective-permute-start | bytes 393224 | tf_op jit(solution)/shard_map/ppermute | solution.py:41
  4.0 2.5 %collective-permute-start.1 = (bf16[8,64,128]{2,1,0:T(8,128)(2,1)S(1)}, bf16[8,64,128]{2,1,0:T(8,128)(2,1)S(1)}, u32[]{:S(2)}, u32[]{:S(2)}) collective-permute-start(bf16[8,64,128]{2,1,0:T(8,128)(2,1)S(1)} %get-tuple-element.40), channel_id=1, source_target_pairs={{0,64},{1,65},{2,66},{3,67},{4,68},{5,69},{6,70},{7,71},{8,72},{9,... | collective-permute-start | bytes 393224 | tf_op jit(solution)/shard_map/ppermute | solution.py:41
  6.5 1.1 %collective-permute-start.2 = (bf16[8,64,128]{2,1,0:T(8,128)(2,1)S(1)}, bf16[8,64,128]{2,1,0:T(8,128)(2,1)S(1)}, u32[]{:S(2)}, u32[]{:S(2)}) collective-permute-start(bf16[8,64,128]{2,1,0:T(8,128)(2,1)S(1)} %get-tuple-element.41), channel_id=1, source_target_pairs={{0,96},{1,97},{2,98},{3,99},{4,100},{5,101},{6,102},{7,103},{8,104... | collective-permute-start | bytes 393224 | tf_op jit(solution)/shard_map/ppermute | solution.py:41
  7.6 2.1 %fetch_kernel.1 = (bf16[2,4,4,64,256]{4,3,2,1,0:T(8,128)(2,1)S(1)}, bf16[512,1024]{1,0:T(8,128)(2,1)S(1)}, bf16[512,1024]{1,0:T(8,128)(2,1)S(1)}) custom-call(bf16[4,4,2,4,64,256]{5,4,3,2,1,0:T(8,128)(2,1)} %bitcast.3, bf16[512,1024]{1,0:T(8,128)(2,1)} %constant.4.clone.high_hbm, bf16[512,1024]{1,0:T(8,128)(2,1)} %constant.5.clone.low_hbm, ...), custom_call_target="tpu_custom_call" | custom-call | flops 70000001024 | bytes 7000000 | tf_op jit(solution)/shard_map/fetch_kernel/pallas_call | solution.py:83
  9.7 2.5 %collective-permute-done.1.r2 = bf16[8,64,128]{2,1,0:T(8,128)(2,1)S(1)} collective-permute-done((bf16[8,64,128]{2,1,0:T(8,128)(2,1)S(1)}, bf16[8,64,128]{2,1,0:T(8,128)(2,1)S(1)}, u32[]{:S(2)}, u32[]{:S(2)}) %collective-permute-start.1) | collective-permute-done | bytes 131104 | tf_op jit(solution)/shard_map/ppermute | solution.py:41
  12.7 1.6 %collective-permute-start.3 = (bf16[4,4,64,512]{3,2,1,0:T(8,128)(2,1)S(1)}, bf16[4,4,64,512]{3,2,1,0:T(8,128)(2,1)S(1)}, u32[]{:S(2)}, u32[]{:S(2)}) collective-permute-start(bf16[4,4,64,512]{3,2,1,0:T(8,128)(2,1)S(1)} %get-tuple-element.44), channel_id=1, source_target_pairs={{0,1},{1,0},{2,3},{3,2},{4,5},{5,4},{6,7},{7,6},{8,9},{9,8},{10,11... | collective-permute-start | bytes 3145736 | tf_op jit(solution)/shard_map/ppermute | solution.py:41
  14.3 1.6 %pre_kernel.1 = (bf16[64,512]{1,0:T(8,128)(2,1)S(1)}, f32[3,64,512]{2,1,0:T(8,128)S(1)}, f32[64,512]{1,0:T(8,128)S(1)}, f32[128,1024]{1,0:T(8,128)S(1)}, bf16[3,64,512]{2,1,0:T(8,128)(2,1)S(1)}) custom-call(bf16[8,64,128]{2,1,0:T(8,128)(2,1)S(1)} %get-tuple-element.38.p0, bf16[8,64,128]{2,1,0:T(8,128)(2,1)S(1)} %collective-permute-done.r1, ...), custom_call_target="tpu_custom_call" | custom-call | flops 70000001024 | bytes 7000000 | tf_op jit(solution)/shard_map/pre_kernel/pallas_call | solution.py:83
  16.0 3.7 %collective-permute-start.13 = (bf16[64,512]{1,0:T(8,128)(2,1)S(1)}, bf16[64,512]{1,0:T(8,128)(2,1)S(1)}, u32[]{:S(2)}, u32[]{:S(2)}) collective-permute-start(bf16[64,512]{1,0:T(8,128)(2,1)S(1)} %get-tuple-element.48.behind.b0), channel_id=1, source_target_pairs={{0,16},{1,17},{2,18},{3,19},{4,20},{5,21},{6,22},{7,23},{8,24},{9,... | collective-permute-start | bytes 196616 | tf_op jit(solution)/shard_map/ppermute | solution.py:41
  20.2 1.4 %collective-permute-start.4 = (bf16[4,64,512]{2,1,0:T(8,128)(2,1)S(1)}, bf16[4,64,512]{2,1,0:T(8,128)(2,1)S(1)}, u32[]{:S(2)}, u32[]{:S(2)}) collective-permute-start(bf16[4,64,512]{2,1,0:T(8,128)(2,1)S(1)} %get-tuple-element.50), channel_id=1, source_target_pairs={{0,2},{1,3},{2,4},{3,5},{4,6},{5,7},{6,0},{7,1},{8,10},{9,11},{10,... | collective-permute-start | bytes 786440 | tf_op jit(solution)/shard_map/ppermute | solution.py:41
  21.5 2.6 %collective-permute-start.5 = (bf16[4,64,512]{2,1,0:T(8,128)(2,1)S(1)}, bf16[4,64,512]{2,1,0:T(8,128)(2,1)S(1)}, u32[]{:S(2)}, u32[]{:S(2)}) collective-permute-start(bf16[4,64,512]{2,1,0:T(8,128)(2,1)S(1)} %get-tuple-element.51), channel_id=1, source_target_pairs={{0,4},{1,5},{2,6},{3,7},{4,0},{5,1},{6,2},{7,3},{8,12},{9,13},{10,... | collective-permute-start | bytes 786440 | tf_op jit(solution)/shard_map/ppermute | solution.py:41
  24.1 1.1 %collective-permute-start.6 = (bf16[4,64,512]{2,1,0:T(8,128)(2,1)S(1)}, bf16[4,64,512]{2,1,0:T(8,128)(2,1)S(1)}, u32[]{:S(2)}, u32[]{:S(2)}) collective-permute-start(bf16[4,64,512]{2,1,0:T(8,128)(2,1)S(1)} %get-tuple-element.52.block), channel_id=1, source_target_pairs={{0,6},{1,7},{2,0},{3,1},{4,2},{5,3},{6,4},{7,5},{8,14},{9,15},{10,... | collective-permute-start | bytes 786440 | tf_op jit(solution)/shard_map/ppermute | solution.py:41
  25.2 0.8 %collective-permute-start.14 = (bf16[2,64,512]{2,1,0:T(8,128)(2,1)S(1)}, bf16[2,64,512]{2,1,0:T(8,128)(2,1)S(1)}, u32[]{:S(2)}, u32[]{:S(2)}) collective-permute-start(bf16[2,64,512]{2,1,0:T(8,128)(2,1)S(1)} %pair_kernel.1.near), channel_id=1, source_target_pairs={{0,8},{1,9},{2,10},{3,11},{4,12},{5,13},{6,14},{7,15},{8,16},{9,17... | collective-permute-start | bytes 393224 | tf_op jit(solution)/shard_map/ppermute | solution.py:41
  26.0 4.3 %collective-permute-done.14.far = bf16[2,64,512]{2,1,0:T(8,128)(2,1)S(1)} collective-permute-done((bf16[2,64,512]{2,1,0:T(8,128)(2,1)S(1)}, bf16[2,64,512]{2,1,0:T(8,128)(2,1)S(1)}, u32[]{:S(2)}, u32[]{:S(2)}) %collective-permute-start.14) | collective-permute-done | bytes 131104 | tf_op jit(solution)/shard_map/ppermute | solution.py:41
  30.4 1.1 %collective-permute-start.15 = (bf16[64,512]{1,0:T(8,128)(2,1)S(1)}, bf16[64,512]{1,0:T(8,128)(2,1)S(1)}, u32[]{:S(2)}, u32[]{:S(2)}) collective-permute-start(bf16[64,512]{1,0:T(8,128)(2,1)S(1)} %get-tuple-element.69), channel_id=1, source_target_pairs={{0,32},{1,33},{2,34},{3,35},{4,36},{5,37},{6,38},{7,39},{8,40},{9,... | collective-permute-start | bytes 196616 | tf_op jit(solution)/shard_map/ppermute | solution.py:41
  31.5 2.1 %collective-permute-start.16 = (bf16[64,512]{1,0:T(8,128)(2,1)S(1)}, bf16[64,512]{1,0:T(8,128)(2,1)S(1)}, u32[]{:S(2)}, u32[]{:S(2)}) collective-permute-start(bf16[64,512]{1,0:T(8,128)(2,1)S(1)} %get-tuple-element.70), channel_id=1, source_target_pairs={{0,64},{1,65},{2,66},{3,67},{4,68},{5,69},{6,70},{7,71},{8,72},{9,... | collective-permute-start | bytes 196616 | tf_op jit(solution)/shard_map/ppermute | solution.py:41
  33.6 1.3 %collective-permute-start.17 = (bf16[64,512]{1,0:T(8,128)(2,1)S(1)}, bf16[64,512]{1,0:T(8,128)(2,1)S(1)}, u32[]{:S(2)}, u32[]{:S(2)}) collective-permute-start(bf16[64,512]{1,0:T(8,128)(2,1)S(1)} %get-tuple-element.71), channel_id=1, source_target_pairs={{0,96},{1,97},{2,98},{3,99},{4,100},{5,101},{6,102},{7,103},{8,104... | collective-permute-start | bytes 196616 | tf_op jit(solution)/shard_map/ppermute | solution.py:41
  34.9 1.0 %collective-permute-done.5.r2 = bf16[4,64,512]{2,1,0:T(8,128)(2,1)S(1)} collective-permute-done((bf16[4,64,512]{2,1,0:T(8,128)(2,1)S(1)}, bf16[4,64,512]{2,1,0:T(8,128)(2,1)S(1)}, u32[]{:S(2)}, u32[]{:S(2)}) %collective-permute-start.5) | collective-permute-done | bytes 262176 | tf_op jit(solution)/shard_map/ppermute | solution.py:41
  36.0 0.8 %collective-permute-start.7 = (bf16[64,512]{1,0:T(8,128)(2,1)S(1)}, bf16[64,512]{1,0:T(8,128)(2,1)S(1)}, u32[]{:S(2)}, u32[]{:S(2)}) collective-permute-start(bf16[64,512]{1,0:T(8,128)(2,1)S(1)} %get-tuple-element.54), channel_id=1, source_target_pairs={{0,8},{1,9},{2,10},{3,11},{4,12},{5,13},{6,14},{7,15},{8,16},{9,17... | collective-permute-start | bytes 196616 | tf_op jit(solution)/shard_map/ppermute | solution.py:41
  36.8 1.1 %collective-permute-start.8 = (bf16[64,512]{1,0:T(8,128)(2,1)S(1)}, bf16[64,512]{1,0:T(8,128)(2,1)S(1)}, u32[]{:S(2)}, u32[]{:S(2)}) collective-permute-start(bf16[64,512]{1,0:T(8,128)(2,1)S(1)} %get-tuple-element.55), channel_id=1, source_target_pairs={{0,16},{1,17},{2,18},{3,19},{4,20},{5,21},{6,22},{7,23},{8,24},{9,... | collective-permute-start | bytes 196616 | tf_op jit(solution)/shard_map/ppermute | solution.py:41
  37.9 1.4 %collective-permute-start.9 = (bf16[64,512]{1,0:T(8,128)(2,1)S(1)}, bf16[64,512]{1,0:T(8,128)(2,1)S(1)}, u32[]{:S(2)}, u32[]{:S(2)}) collective-permute-start(bf16[64,512]{1,0:T(8,128)(2,1)S(1)} %get-tuple-element.56), channel_id=1, source_target_pairs={{0,24},{1,25},{2,26},{3,27},{4,28},{5,29},{6,30},{7,31},{8,0},{9,1... | collective-permute-start | bytes 196616 | tf_op jit(solution)/shard_map/ppermute | solution.py:41
  39.3 0.9 %collective-permute-start.18 = (bf16[4,64,512]{2,1,0:T(8,128)(2,1)S(1)}, bf16[4,64,512]{2,1,0:T(8,128)(2,1)S(1)}, u32[]{:S(2)}, u32[]{:S(2)}) collective-permute-start(bf16[4,64,512]{2,1,0:T(8,128)(2,1)S(1)} %collect_kernel.2.b0), channel_id=1, source_target_pairs={{0,2},{1,3},{2,4},{3,5},{4,6},{5,7},{6,0},{7,1},{8,10},{9,11},{10,... | collective-permute-start | bytes 786440 | tf_op jit(solution)/shard_map/ppermute | solution.py:41
  40.3 2.8 %collective-permute-start.19 = (bf16[4,64,512]{2,1,0:T(8,128)(2,1)S(1)}, bf16[4,64,512]{2,1,0:T(8,128)(2,1)S(1)}, u32[]{:S(2)}, u32[]{:S(2)}) collective-permute-start(bf16[4,64,512]{2,1,0:T(8,128)(2,1)S(1)} %collect_kernel.2.b0), channel_id=1, source_target_pairs={{0,4},{1,5},{2,6},{3,7},{4,0},{5,1},{6,2},{7,3},{8,12},{9,13},{10,... | collective-permute-start | bytes 786440 | tf_op jit(solution)/shard_map/ppermute | solution.py:41
  43.5 2.5 %post_kernel.1 = (bf16[6,64,128]{2,1,0:T(8,128)(2,1)S(1)}, bf16[6,64,128]{2,1,0:T(8,128)(2,1)S(1)}, bf16[6,64,128]{2,1,0:T(8,128)(2,1)S(1)}, bf16[6,64,128]{2,1,0:T(8,128)(2,1)S(1)}) custom-call(f32[64,512]{1,0:T(8,128)S(1)} %get-tuple-element.53.own, bf16[64,512]{1,0:T(8,128)(2,1)S(1)} %collective-permute-done.7.r1, ...), custom_call_target="tpu_custom_call" | custom-call | flops 105000001536 | bytes 10500000 | tf_op jit(solution)/shard_map/post_kernel/pallas_call | solution.py:83
  46.1 1.1 %collective-permute-start.10 = (bf16[6,64,128]{2,1,0:T(8,128)(2,1)S(1)}, bf16[6,64,128]{2,1,0:T(8,128)(2,1)S(1)}, u32[]{:S(2)}, u32[]{:S(2)}) collective-permute-start(bf16[6,64,128]{2,1,0:T(8,128)(2,1)S(1)} %get-tuple-element.62), channel_id=1, source_target_pairs={{0,32},{1,33},{2,34},{3,35},{4,36},{5,37},{6,38},{7,39},{8,40},{9,... | collective-permute-start | bytes 294920 | tf_op jit(solution)/shard_map/ppermute | solution.py:41
  47.2 2.1 %collective-permute-start.11 = (bf16[6,64,128]{2,1,0:T(8,128)(2,1)S(1)}, bf16[6,64,128]{2,1,0:T(8,128)(2,1)S(1)}, u32[]{:S(2)}, u32[]{:S(2)}) collective-permute-start(bf16[6,64,128]{2,1,0:T(8,128)(2,1)S(1)} %get-tuple-element.63), channel_id=1, source_target_pairs={{0,64},{1,65},{2,66},{3,67},{4,68},{5,69},{6,70},{7,71},{8,72},{9,... | collective-permute-start | bytes 294920 | tf_op jit(solution)/shard_map/ppermute | solution.py:41
  49.3 1.3 %collective-permute-start.12 = (bf16[6,64,128]{2,1,0:T(8,128)(2,1)S(1)}, bf16[6,64,128]{2,1,0:T(8,128)(2,1)S(1)}, u32[]{:S(2)}, u32[]{:S(2)}) collective-permute-start(bf16[6,64,128]{2,1,0:T(8,128)(2,1)S(1)} %get-tuple-element.64), channel_id=1, source_target_pairs={{0,96},{1,97},{2,98},{3,99},{4,100},{5,101},{6,102},{7,103},{8,104... | collective-permute-start | bytes 294920 | tf_op jit(solution)/shard_map/ppermute | solution.py:41
  50.6 3.4 %collective-permute-done.19.b2 = bf16[4,64,512]{2,1,0:T(8,128)(2,1)S(1)} collective-permute-done((bf16[4,64,512]{2,1,0:T(8,128)(2,1)S(1)}, bf16[4,64,512]{2,1,0:T(8,128)(2,1)S(1)}, u32[]{:S(2)}, u32[]{:S(2)}) %collective-permute-start.19) | collective-permute-done | bytes 262176 | tf_op jit(solution)/shard_map/ppermute | solution.py:41
  54.1 2.1 %collective-permute-start.21 = (bf16[4,4,64,512]{3,2,1,0:T(8,128)(2,1)S(1)}, bf16[4,4,64,512]{3,2,1,0:T(8,128)(2,1)S(1)}, u32[]{:S(2)}, u32[]{:S(2)}) collective-permute-start(bf16[4,4,64,512]{3,2,1,0:T(8,128)(2,1)S(1)} %collect_kernel.3.blocks), channel_id=1, source_target_pairs={{0,1},{1,0},{2,3},{3,2},{4,5},{5,4},{6,7},{7,6},{8,9},{9,8},{10,11... | collective-permute-start | bytes 3145736 | tf_op jit(solution)/shard_map/ppermute | solution.py:41
  56.1 0.9 %out_kernel.1 = (bf16[3,128,256]{2,1,0:T(8,128)(2,1)}, f32[3,7,256]{2,1,0:T(8,128)}, f32[128,256]{1,0:T(8,128)}) custom-call(bf16[6,64,128]{2,1,0:T(8,128)(2,1)S(1)} %get-tuple-element.61.o0, bf16[6,64,128]{2,1,0:T(8,128)(2,1)S(1)} %collective-permute-done.10.r1, bf16[6,64,128]{2,1,0:T(8,128)(2,1)S(1)} %collective-permute-done.11.r2, ...), custom_call_target="tpu_custom_call" | custom-call | flops 35000000512 | bytes 3500000 | tf_op jit(solution)/shard_map/out_kernel/pallas_call | solution.py:83
  57.1 1.3 %near_kernel.1.held = f32[4,2,4,64,256]{4,3,2,1,0:T(8,128)} custom-call(bf16[4,4,64,512]{3,2,1,0:T(8,128)(2,1)S(1)} %collect_kernel.3.blocks, bf16[512,256]{1,0:T(8,128)(2,1)S(1)} %copy-done.1), custom_call_target="tpu_custom_call" | custom-call | tf_op jit(solution)/shard_map/near_kernel/pallas_call | solution.py:83
  58.4 1.3 %far_kernel.1 = f32[4,2,4,64,256]{4,3,2,1,0:T(8,128)} custom-call(bf16[4,4,64,512]{3,2,1,0:T(8,128)(2,1)S(1)} %collective-permute-done.21.blocks, bf16[512,256]{1,0:T(8,128)(2,1)S(1)} %copy-done.1, f32[4,2,4,64,256]{4,3,2,1,0:T(8,128)} %near_kernel.1.held), custom_call_target="tpu_custom_call", output_to_operand_aliasing={{}: (2, {})} | custom-call | flops 70000001024 | bytes 7000000 | tf_op jit(solution)/shard_map/far_kernel/pallas_call | solution.py:83
  (31 shorter events, 1.8 us)
Async XLA Ops:
  1.9 7.8 %collective-permute-start = (bf16[8,64,128]{2,1,0:T(8,128)(2,1)S(1)}, bf16[8,64,128]{2,1,0:T(8,128)(2,1)S(1)}, u32[]{:S(2)}, u32[]{:S(2)}) collective-permute-start(bf16[8,64,128]{2,1,0:T(8,128)(2,1)S(1)} %get-tuple-element.39), channel_id=1, source_target_pairs={{0,32},{1,33},{2,34},{3,35},{4,36},{5,37},{6,38},{7,39},{8,40},{9,... | collective-permute-start | bytes 393224 | tf_op jit(solution)/shard_map/ppermute | solution.py:41
  4.0 8.2 %collective-permute-start.1 = (bf16[8,64,128]{2,1,0:T(8,128)(2,1)S(1)}, bf16[8,64,128]{2,1,0:T(8,128)(2,1)S(1)}, u32[]{:S(2)}, u32[]{:S(2)}) collective-permute-start(bf16[8,64,128]{2,1,0:T(8,128)(2,1)S(1)} %get-tuple-element.40), channel_id=1, source_target_pairs={{0,64},{1,65},{2,66},{3,67},{4,68},{5,69},{6,70},{7,71},{8,72},{9,... | collective-permute-start | bytes 393224 | tf_op jit(solution)/shard_map/ppermute | solution.py:41
  6.5 5.7 %collective-permute-start.2 = (bf16[8,64,128]{2,1,0:T(8,128)(2,1)S(1)}, bf16[8,64,128]{2,1,0:T(8,128)(2,1)S(1)}, u32[]{:S(2)}, u32[]{:S(2)}) collective-permute-start(bf16[8,64,128]{2,1,0:T(8,128)(2,1)S(1)} %get-tuple-element.41), channel_id=1, source_target_pairs={{0,96},{1,97},{2,98},{3,99},{4,100},{5,101},{6,102},{7,103},{8,104... | collective-permute-start | bytes 393224 | tf_op jit(solution)/shard_map/ppermute | solution.py:41
  12.7 7.0 %copy-start = (bf16[512,256]{1,0:T(8,128)(2,1)}, bf16[512,256]{1,0:T(8,128)(2,1)S(1)}, u32[]{:S(2)}) copy-start(bf16[512,256]{1,0:T(8,128)(2,1)S(1)} %get-tuple-element.45.behind.whole) | copy-start | bytes 786436
  12.7 7.0 %collective-permute-start.3 = (bf16[4,4,64,512]{3,2,1,0:T(8,128)(2,1)S(1)}, bf16[4,4,64,512]{3,2,1,0:T(8,128)(2,1)S(1)}, u32[]{:S(2)}, u32[]{:S(2)}) collective-permute-start(bf16[4,4,64,512]{3,2,1,0:T(8,128)(2,1)S(1)} %get-tuple-element.44), channel_id=1, source_target_pairs={{0,1},{1,0},{2,3},{3,2},{4,5},{5,4},{6,7},{7,6},{8,9},{9,8},{10,11... | collective-permute-start | bytes 3145736 | tf_op jit(solution)/shard_map/ppermute | solution.py:41
  16.0 9.2 %collective-permute-start.13 = (bf16[64,512]{1,0:T(8,128)(2,1)S(1)}, bf16[64,512]{1,0:T(8,128)(2,1)S(1)}, u32[]{:S(2)}, u32[]{:S(2)}) collective-permute-start(bf16[64,512]{1,0:T(8,128)(2,1)S(1)} %get-tuple-element.48.behind.b0), channel_id=1, source_target_pairs={{0,16},{1,17},{2,18},{3,19},{4,20},{5,21},{6,22},{7,23},{8,24},{9,... | collective-permute-start | bytes 196616 | tf_op jit(solution)/shard_map/ppermute | solution.py:41
  20.2 13.5 %collective-permute-start.4 = (bf16[4,64,512]{2,1,0:T(8,128)(2,1)S(1)}, bf16[4,64,512]{2,1,0:T(8,128)(2,1)S(1)}, u32[]{:S(2)}, u32[]{:S(2)}) collective-permute-start(bf16[4,64,512]{2,1,0:T(8,128)(2,1)S(1)} %get-tuple-element.50), channel_id=1, source_target_pairs={{0,2},{1,3},{2,4},{3,5},{4,6},{5,7},{6,0},{7,1},{8,10},{9,11},{10,... | collective-permute-start | bytes 786440 | tf_op jit(solution)/shard_map/ppermute | solution.py:41
  21.5 14.4 %collective-permute-start.5 = (bf16[4,64,512]{2,1,0:T(8,128)(2,1)S(1)}, bf16[4,64,512]{2,1,0:T(8,128)(2,1)S(1)}, u32[]{:S(2)}, u32[]{:S(2)}) collective-permute-start(bf16[4,64,512]{2,1,0:T(8,128)(2,1)S(1)} %get-tuple-element.51), channel_id=1, source_target_pairs={{0,4},{1,5},{2,6},{3,7},{4,0},{5,1},{6,2},{7,3},{8,12},{9,13},{10,... | collective-permute-start | bytes 786440 | tf_op jit(solution)/shard_map/ppermute | solution.py:41
  24.1 11.8 %collective-permute-start.6 = (bf16[4,64,512]{2,1,0:T(8,128)(2,1)S(1)}, bf16[4,64,512]{2,1,0:T(8,128)(2,1)S(1)}, u32[]{:S(2)}, u32[]{:S(2)}) collective-permute-start(bf16[4,64,512]{2,1,0:T(8,128)(2,1)S(1)} %get-tuple-element.52.block), channel_id=1, source_target_pairs={{0,6},{1,7},{2,0},{3,1},{4,2},{5,3},{6,4},{7,5},{8,14},{9,15},{10,... | collective-permute-start | bytes 786440 | tf_op jit(solution)/shard_map/ppermute | solution.py:41
  25.2 5.1 %collective-permute-start.14 = (bf16[2,64,512]{2,1,0:T(8,128)(2,1)S(1)}, bf16[2,64,512]{2,1,0:T(8,128)(2,1)S(1)}, u32[]{:S(2)}, u32[]{:S(2)}) collective-permute-start(bf16[2,64,512]{2,1,0:T(8,128)(2,1)S(1)} %pair_kernel.1.near), channel_id=1, source_target_pairs={{0,8},{1,9},{2,10},{3,11},{4,12},{5,13},{6,14},{7,15},{8,16},{9,17... | collective-permute-start | bytes 393224 | tf_op jit(solution)/shard_map/ppermute | solution.py:41
  30.4 7.5 %collective-permute-start.15 = (bf16[64,512]{1,0:T(8,128)(2,1)S(1)}, bf16[64,512]{1,0:T(8,128)(2,1)S(1)}, u32[]{:S(2)}, u32[]{:S(2)}) collective-permute-start(bf16[64,512]{1,0:T(8,128)(2,1)S(1)} %get-tuple-element.69), channel_id=1, source_target_pairs={{0,32},{1,33},{2,34},{3,35},{4,36},{5,37},{6,38},{7,39},{8,40},{9,... | collective-permute-start | bytes 196616 | tf_op jit(solution)/shard_map/ppermute | solution.py:41
  31.5 7.8 %collective-permute-start.16 = (bf16[64,512]{1,0:T(8,128)(2,1)S(1)}, bf16[64,512]{1,0:T(8,128)(2,1)S(1)}, u32[]{:S(2)}, u32[]{:S(2)}) collective-permute-start(bf16[64,512]{1,0:T(8,128)(2,1)S(1)} %get-tuple-element.70), channel_id=1, source_target_pairs={{0,64},{1,65},{2,66},{3,67},{4,68},{5,69},{6,70},{7,71},{8,72},{9,... | collective-permute-start | bytes 196616 | tf_op jit(solution)/shard_map/ppermute | solution.py:41
  33.6 5.7 %collective-permute-start.17 = (bf16[64,512]{1,0:T(8,128)(2,1)S(1)}, bf16[64,512]{1,0:T(8,128)(2,1)S(1)}, u32[]{:S(2)}, u32[]{:S(2)}) collective-permute-start(bf16[64,512]{1,0:T(8,128)(2,1)S(1)} %get-tuple-element.71), channel_id=1, source_target_pairs={{0,96},{1,97},{2,98},{3,99},{4,100},{5,101},{6,102},{7,103},{8,104... | collective-permute-start | bytes 196616 | tf_op jit(solution)/shard_map/ppermute | solution.py:41
  36.0 7.1 %collective-permute-start.7 = (bf16[64,512]{1,0:T(8,128)(2,1)S(1)}, bf16[64,512]{1,0:T(8,128)(2,1)S(1)}, u32[]{:S(2)}, u32[]{:S(2)}) collective-permute-start(bf16[64,512]{1,0:T(8,128)(2,1)S(1)} %get-tuple-element.54), channel_id=1, source_target_pairs={{0,8},{1,9},{2,10},{3,11},{4,12},{5,13},{6,14},{7,15},{8,16},{9,17... | collective-permute-start | bytes 196616 | tf_op jit(solution)/shard_map/ppermute | solution.py:41
  36.8 6.7 %collective-permute-start.8 = (bf16[64,512]{1,0:T(8,128)(2,1)S(1)}, bf16[64,512]{1,0:T(8,128)(2,1)S(1)}, u32[]{:S(2)}, u32[]{:S(2)}) collective-permute-start(bf16[64,512]{1,0:T(8,128)(2,1)S(1)} %get-tuple-element.55), channel_id=1, source_target_pairs={{0,16},{1,17},{2,18},{3,19},{4,20},{5,21},{6,22},{7,23},{8,24},{9,... | collective-permute-start | bytes 196616 | tf_op jit(solution)/shard_map/ppermute | solution.py:41
  37.9 5.6 %collective-permute-start.9 = (bf16[64,512]{1,0:T(8,128)(2,1)S(1)}, bf16[64,512]{1,0:T(8,128)(2,1)S(1)}, u32[]{:S(2)}, u32[]{:S(2)}) collective-permute-start(bf16[64,512]{1,0:T(8,128)(2,1)S(1)} %get-tuple-element.56), channel_id=1, source_target_pairs={{0,24},{1,25},{2,26},{3,27},{4,28},{5,29},{6,30},{7,31},{8,0},{9,1... | collective-permute-start | bytes 196616 | tf_op jit(solution)/shard_map/ppermute | solution.py:41
  39.3 10.0 %collective-permute-start.18 = (bf16[4,64,512]{2,1,0:T(8,128)(2,1)S(1)}, bf16[4,64,512]{2,1,0:T(8,128)(2,1)S(1)}, u32[]{:S(2)}, u32[]{:S(2)}) collective-permute-start(bf16[4,64,512]{2,1,0:T(8,128)(2,1)S(1)} %collect_kernel.2.b0), channel_id=1, source_target_pairs={{0,2},{1,3},{2,4},{3,5},{4,6},{5,7},{6,0},{7,1},{8,10},{9,11},{10,... | collective-permute-start | bytes 786440 | tf_op jit(solution)/shard_map/ppermute | solution.py:41
  40.3 13.7 %collective-permute-start.19 = (bf16[4,64,512]{2,1,0:T(8,128)(2,1)S(1)}, bf16[4,64,512]{2,1,0:T(8,128)(2,1)S(1)}, u32[]{:S(2)}, u32[]{:S(2)}) collective-permute-start(bf16[4,64,512]{2,1,0:T(8,128)(2,1)S(1)} %collect_kernel.2.b0), channel_id=1, source_target_pairs={{0,4},{1,5},{2,6},{3,7},{4,0},{5,1},{6,2},{7,3},{8,12},{9,13},{10,... | collective-permute-start | bytes 786440 | tf_op jit(solution)/shard_map/ppermute | solution.py:41
  43.1 10.9 %collective-permute-start.20 = (bf16[4,64,512]{2,1,0:T(8,128)(2,1)S(1)}, bf16[4,64,512]{2,1,0:T(8,128)(2,1)S(1)}, u32[]{:S(2)}, u32[]{:S(2)}) collective-permute-start(bf16[4,64,512]{2,1,0:T(8,128)(2,1)S(1)} %collect_kernel.2.b0), channel_id=1, source_target_pairs={{0,6},{1,7},{2,0},{3,1},{4,2},{5,3},{6,4},{7,5},{8,14},{9,15},{10,... | collective-permute-start | bytes 786440 | tf_op jit(solution)/shard_map/ppermute | solution.py:41
  46.1 10.1 %collective-permute-start.10 = (bf16[6,64,128]{2,1,0:T(8,128)(2,1)S(1)}, bf16[6,64,128]{2,1,0:T(8,128)(2,1)S(1)}, u32[]{:S(2)}, u32[]{:S(2)}) collective-permute-start(bf16[6,64,128]{2,1,0:T(8,128)(2,1)S(1)} %get-tuple-element.62), channel_id=1, source_target_pairs={{0,32},{1,33},{2,34},{3,35},{4,36},{5,37},{6,38},{7,39},{8,40},{9,... | collective-permute-start | bytes 294920 | tf_op jit(solution)/shard_map/ppermute | solution.py:41
  47.2 9.0 %collective-permute-start.11 = (bf16[6,64,128]{2,1,0:T(8,128)(2,1)S(1)}, bf16[6,64,128]{2,1,0:T(8,128)(2,1)S(1)}, u32[]{:S(2)}, u32[]{:S(2)}) collective-permute-start(bf16[6,64,128]{2,1,0:T(8,128)(2,1)S(1)} %get-tuple-element.63), channel_id=1, source_target_pairs={{0,64},{1,65},{2,66},{3,67},{4,68},{5,69},{6,70},{7,71},{8,72},{9,... | collective-permute-start | bytes 294920 | tf_op jit(solution)/shard_map/ppermute | solution.py:41
  49.3 6.8 %collective-permute-start.12 = (bf16[6,64,128]{2,1,0:T(8,128)(2,1)S(1)}, bf16[6,64,128]{2,1,0:T(8,128)(2,1)S(1)}, u32[]{:S(2)}, u32[]{:S(2)}) collective-permute-start(bf16[6,64,128]{2,1,0:T(8,128)(2,1)S(1)} %get-tuple-element.64), channel_id=1, source_target_pairs={{0,96},{1,97},{2,98},{3,99},{4,100},{5,101},{6,102},{7,103},{8,104... | collective-permute-start | bytes 294920 | tf_op jit(solution)/shard_map/ppermute | solution.py:41
  54.1 4.3 %collective-permute-start.21 = (bf16[4,4,64,512]{3,2,1,0:T(8,128)(2,1)S(1)}, bf16[4,4,64,512]{3,2,1,0:T(8,128)(2,1)S(1)}, u32[]{:S(2)}, u32[]{:S(2)}) collective-permute-start(bf16[4,4,64,512]{3,2,1,0:T(8,128)(2,1)S(1)} %collect_kernel.3.blocks), channel_id=1, source_target_pairs={{0,1},{1,0},{2,3},{3,2},{4,5},{5,4},{6,7},{7,6},{8,9},{9,8},{10,11... | collective-permute-start | bytes 3145736 | tf_op jit(solution)/shard_map/ppermute | solution.py:41
  56.1 1.0 %copy-start.1 = (bf16[512,256]{1,0:T(8,128)(2,1)S(1)}, bf16[512,256]{1,0:T(8,128)(2,1)}, u32[]{:S(2)}) copy-start(bf16[512,256]{1,0:T(8,128)(2,1)} %copy-done) | copy-start | bytes 786436

commit v7 on v6

--- a/solution.py
+++ b/solution.py
@@ -106,19 +106,15 @@
 def pack_kernel(
     feat_hbm,
     filt_hbm,
-    taps_hbm,
     grad_hbm,
     p0,
     p1,
     p2,
     p3,
-    taps_out,
     feat_ref,
     filt_ref,
-    taps_ref,
     grad_ref,
     held,
-    square,
     sems,
 ):
     x = coords()[0]
@@ -127,14 +123,12 @@
         (
             (feat_hbm, feat_ref),
             (filt_hbm, filt_ref),
-            (taps_hbm, taps_ref),
             (grad_hbm, grad_ref),
         )
     ):
         copy = pltpu.make_async_copy(src, dst, sems.at[place])
         copy.start()
         copies.append(copy)
-    square[0] = jnp.zeros((128, 256), F32)
     for copy in copies:
         copy.wait()
     for stream in range(4):
@@ -148,15 +142,22 @@
                 out[4 + 2 * row + column] = grad_ref[
                     row * 64 : row * 64 + 64, column * 128 : column * 128 + 128
                 ]
-    for stream in range(3):
-        square[0, stream * 8 : stream * 8 + TAPS, :] = taps_ref[stream]
-    columns = square[0].T
-    for quarter in range(4):
-        square[1 + quarter, 0:64, 0:128] = columns[quarter * 64 : quarter * 64 + 64]
-    taps_out[...] = square[1 + x, 0:64, 0:128]
-
-
-def fetch_kernel(weight, high_hbm, low_hbm, behind, out, high, low, sems, table_sems):
+
+
+def fetch_kernel(
+    weight,
+    high_hbm,
+    low_hbm,
+    taps_ref,
+    behind,
+    out,
+    high,
+    low,
+    taps_out,
+    square,
+    sems,
+    table_sems,
+):
     x, z, y, c = coords()
     copies = []
     for half in range(2):
@@ -171,6 +172,13 @@
     copies.append(pltpu.make_async_copy(low_hbm, low, table_sems.at[1]))
     for copy in copies:
         copy.start()
+    square[0] = jnp.zeros((128, 256), F32)
+    for stream in range(3):
+        square[0, stream * 8 : stream * 8 + TAPS, :] = taps_ref[stream]
+    columns = square[0].T
+    for quarter in range(4):
+        square[1 + quarter, 0:64, 0:128] = columns[quarter * 64 : quarter * 64 + 64]
+    taps_out[...] = square[1 + x, 0:64, 0:128]
     for copy in copies:
         copy.wait()
 
@@ -384,35 +392,35 @@
 def local(high, low, features, short_kernel, long_filter, out_weight, grad_out):
     high, low = jnp.asarray(high), jnp.asarray(low)
     weight = out_weight.reshape(NZ, NY, NC, NX, 64, 256)
-    *pay, taps = call(
+    pay = call(
         pack_kernel,
-        [kept((8, 64, 128), BF16)] * 4 + [kept((64, 128), F32)],
+        [kept((8, 64, 128), BF16)] * 4,
         features,
         long_filter,
-        short_kernel,
         grad_out,
-        in_hbm=(0, 1, 2, 3),
+        in_hbm=(0, 1, 2),
         scratch=[
             pltpu.VMEM((3, 128, 256), BF16),
             pltpu.VMEM((128, 256), BF16),
-            pltpu.VMEM((3, TAPS, 256), F32),
             pltpu.VMEM((128, 256), BF16),
             pltpu.VMEM((4, 4, 64, 128), BF16),
-            pltpu.VMEM((5, 128, 256), F32),
-            pltpu.SemaphoreType.DMA((4,)),
+            pltpu.SemaphoreType.DMA((3,)),
         ],
         time=TIMES["pack"],
     )
     got = [pay[0]] + [along_x(pay[k], k) for k in (1, 2, 3)]
-    rows, high, low = call(
+    rows, high, low, taps = call(
         fetch_kernel,
-        [kept((2, NY, NZ, 64, 256), BF16)] + [kept((512, 1024), BF16)] * 2,
+        [kept((2, NY, NZ, 64, 256), BF16)]
+        + [kept((512, 1024), BF16)] * 2
+        + [kept((64, 128), F32)],
         weight,
         high,
         low,
-        taps,
+        short_kernel,
+        pay[0],
         in_hbm=(0, 1, 2),
-        scratch=[pltpu.SemaphoreType.DMA((2, NY)), pltpu.SemaphoreType.DMA((2,))],
+        scratch=[pltpu.VMEM((5, 128, 256), F32), pltpu.SemaphoreType.DMA((2, NY)), pltpu.SemaphoreType.DMA((2,))],
         time=TIMES["fetch"],
     )
     whole, send = call(

time: 59.9 us -> 59.8 us (level)
  no operation moved by 1% of the time
where the time goes in v7:
time: 59.8 us; the launch traced here: 59.6 us
  starting transfers between devices  35.4 us (59%)
  Pallas kernels  12.2 us (20%)
  waiting for transfers between devices  11.2 us (19%)
  between operations  0.76 us (1%)
    ppermute x22, starting transfers between devices, move(): return lax.ppermute(array, ('ctx', 'ch'), pairs)  35.4 us
    pallas_call x15, Pallas kernels, call(): pl.pallas_call(kernel, out_shape=out_shape, name=kernel.__name__, in_spec...  12.2 us
    ppermute x22, waiting for transfers between devices, move(): return lax.ppermute(array, ('ctx', 'ch'), pairs)  11.2 us
  transfers between devices with their start and end apart: 22, of which 4 were waited for; matrix products, arithmetic and copies ran while one was open for 0% of the time, Pallas kernels for 15%

profile of v7, /device:TPU:1, one launch (start us, length us, event | category | flops | bytes accessed | tf_op | source)
XLA Modules:
  0.0 59.6 jit_solution(8825497066430446407)
XLA Ops:
  0.6 1.2 %pack_kernel.1 = (bf16[8,64,128]{2,1,0:T(8,128)(2,1)S(1)}, bf16[8,64,128]{2,1,0:T(8,128)(2,1)S(1)}, bf16[8,64,128]{2,1,0:T(8,128)(2,1)S(1)}, bf16[8,64,128]{2,1,0:T(8,128)(2,1)S(1)}) custom-call(bf16[3,128,256]{2,1,0:T(8,128)(2,1)} %feat_hbm.1, bf16[128,256]{1,0:T(8,128)(2,1)} %filt_hbm.1, bf16[128,256]{1,0:T(8,128)(2,1)} %grad_hbm.1), custom_call_target="tpu_custom_call" | custom-call | flops 70000001024 | bytes 7000000 | tf_op jit(solution)/shard_map/pack_kernel/pallas_call | solution.py:83
  1.8 2.1 %collective-permute-start = (bf16[8,64,128]{2,1,0:T(8,128)(2,1)S(1)}, bf16[8,64,128]{2,1,0:T(8,128)(2,1)S(1)}, u32[]{:S(2)}, u32[]{:S(2)}) collective-permute-start(bf16[8,64,128]{2,1,0:T(8,128)(2,1)S(1)} %get-tuple-element.39), channel_id=1, source_target_pairs={{0,32},{1,33},{2,34},{3,35},{4,36},{5,37},{6,38},{7,39},{8,40},{9,... | collective-permute-start | bytes 393224 | tf_op jit(solution)/shard_map/ppermute | solution.py:41
  3.9 2.4 %collective-permute-start.1 = (bf16[8,64,128]{2,1,0:T(8,128)(2,1)S(1)}, bf16[8,64,128]{2,1,0:T(8,128)(2,1)S(1)}, u32[]{:S(2)}, u32[]{:S(2)}) collective-permute-start(bf16[8,64,128]{2,1,0:T(8,128)(2,1)S(1)} %get-tuple-element.40), channel_id=1, source_target_pairs={{0,64},{1,65},{2,66},{3,67},{4,68},{5,69},{6,70},{7,71},{8,72},{9,... | collective-permute-start | bytes 393224 | tf_op jit(solution)/shard_map/ppermute | solution.py:41
  6.4 1.2 %collective-permute-start.2 = (bf16[8,64,128]{2,1,0:T(8,128)(2,1)S(1)}, bf16[8,64,128]{2,1,0:T(8,128)(2,1)S(1)}, u32[]{:S(2)}, u32[]{:S(2)}) collective-permute-start(bf16[8,64,128]{2,1,0:T(8,128)(2,1)S(1)} %get-tuple-element.41), channel_id=1, source_target_pairs={{0,96},{1,97},{2,98},{3,99},{4,100},{5,101},{6,102},{7,103},{8,104... | collective-permute-start | bytes 393224 | tf_op jit(solution)/shard_map/ppermute | solution.py:41
  7.5 2.1 %fetch_kernel.1 = (bf16[2,4,4,64,256]{4,3,2,1,0:T(8,128)(2,1)S(1)}, bf16[512,1024]{1,0:T(8,128)(2,1)S(1)}, bf16[512,1024]{1,0:T(8,128)(2,1)S(1)}, f32[64,128]{1,0:T(8,128)S(1)}) custom-call(bf16[4,4,2,4,64,256]{5,4,3,2,1,0:T(8,128)(2,1)} %bitcast.3, bf16[512,1024]{1,0:T(8,128)(2,1)} %constant.4.clone.high_hbm, bf16[512,1024]{1,0:T(8,128)(2,1)} %constant.5.clone.low_hbm, ...), custom_call_target="tpu_custom_call" | custom-call | flops 70000001024 | bytes 7000000 | tf_op jit(solution)/shard_map/fetch_kernel/pallas_call | solution.py:83
  9.6 2.5 %collective-permute-done.1.r2 = bf16[8,64,128]{2,1,0:T(8,128)(2,1)S(1)} collective-permute-done((bf16[8,64,128]{2,1,0:T(8,128)(2,1)S(1)}, bf16[8,64,128]{2,1,0:T(8,128)(2,1)S(1)}, u32[]{:S(2)}, u32[]{:S(2)}) %collective-permute-start.1) | collective-permute-done | bytes 131104 | tf_op jit(solution)/shard_map/ppermute | solution.py:41
  12.6 1.6 %collective-permute-start.3 = (bf16[4,4,64,512]{3,2,1,0:T(8,128)(2,1)S(1)}, bf16[4,4,64,512]{3,2,1,0:T(8,128)(2,1)S(1)}, u32[]{:S(2)}, u32[]{:S(2)}) collective-permute-start(bf16[4,4,64,512]{3,2,1,0:T(8,128)(2,1)S(1)} %get-tuple-element.43), channel_id=1, source_target_pairs={{0,1},{1,0},{2,3},{3,2},{4,5},{5,4},{6,7},{7,6},{8,9},{9,8},{10,11... | collective-permute-start | bytes 3145736 | tf_op jit(solution)/shard_map/ppermute | solution.py:41
  14.3 1.7 %pre_kernel.1 = (bf16[64,512]{1,0:T(8,128)(2,1)S(1)}, f32[3,64,512]{2,1,0:T(8,128)S(1)}, f32[64,512]{1,0:T(8,128)S(1)}, f32[128,1024]{1,0:T(8,128)S(1)}, bf16[3,64,512]{2,1,0:T(8,128)(2,1)S(1)}) custom-call(bf16[8,64,128]{2,1,0:T(8,128)(2,1)S(1)} %get-tuple-element.38.behind.p0, bf16[8,64,128]{2,1,0:T(8,128)(2,1)S(1)} %collective-permute-done.r1, ...), custom_call_target="tpu_custom_call" | custom-call | flops 70000001024 | bytes 7000000 | tf_op jit(solution)/shard_map/pre_kernel/pallas_call | solution.py:83
  15.9 3.7 %collective-permute-start.13 = (bf16[64,512]{1,0:T(8,128)(2,1)S(1)}, bf16[64,512]{1,0:T(8,128)(2,1)S(1)}, u32[]{:S(2)}, u32[]{:S(2)}) collective-permute-start(bf16[64,512]{1,0:T(8,128)(2,1)S(1)} %get-tuple-element.48.behind.b0), channel_id=1, source_target_pairs={{0,16},{1,17},{2,18},{3,19},{4,20},{5,21},{6,22},{7,23},{8,24},{9,... | collective-permute-start | bytes 196616 | tf_op jit(solution)/shard_map/ppermute | solution.py:41
  20.1 1.4 %collective-permute-start.4 = (bf16[4,64,512]{2,1,0:T(8,128)(2,1)S(1)}, bf16[4,64,512]{2,1,0:T(8,128)(2,1)S(1)}, u32[]{:S(2)}, u32[]{:S(2)}) collective-permute-start(bf16[4,64,512]{2,1,0:T(8,128)(2,1)S(1)} %get-tuple-element.50), channel_id=1, source_target_pairs={{0,2},{1,3},{2,4},{3,5},{4,6},{5,7},{6,0},{7,1},{8,10},{9,11},{10,... | collective-permute-start | bytes 786440 | tf_op jit(solution)/shard_map/ppermute | solution.py:41
  21.5 2.6 %collective-permute-start.5 = (bf16[4,64,512]{2,1,0:T(8,128)(2,1)S(1)}, bf16[4,64,512]{2,1,0:T(8,128)(2,1)S(1)}, u32[]{:S(2)}, u32[]{:S(2)}) collective-permute-start(bf16[4,64,512]{2,1,0:T(8,128)(2,1)S(1)} %get-tuple-element.51), channel_id=1, source_target_pairs={{0,4},{1,5},{2,6},{3,7},{4,0},{5,1},{6,2},{7,3},{8,12},{9,13},{10,... | collective-permute-start | bytes 786440 | tf_op jit(solution)/shard_map/ppermute | solution.py:41
  24.1 1.1 %collective-permute-start.6 = (bf16[4,64,512]{2,1,0:T(8,128)(2,1)S(1)}, bf16[4,64,512]{2,1,0:T(8,128)(2,1)S(1)}, u32[]{:S(2)}, u32[]{:S(2)}) collective-permute-start(bf16[4,64,512]{2,1,0:T(8,128)(2,1)S(1)} %get-tuple-element.52.block), channel_id=1, source_target_pairs={{0,6},{1,7},{2,0},{3,1},{4,2},{5,3},{6,4},{7,5},{8,14},{9,15},{10,... | collective-permute-start | bytes 786440 | tf_op jit(solution)/shard_map/ppermute | solution.py:41
  25.2 0.8 %collective-permute-start.14 = (bf16[2,64,512]{2,1,0:T(8,128)(2,1)S(1)}, bf16[2,64,512]{2,1,0:T(8,128)(2,1)S(1)}, u32[]{:S(2)}, u32[]{:S(2)}) collective-permute-start(bf16[2,64,512]{2,1,0:T(8,128)(2,1)S(1)} %pair_kernel.1.near), channel_id=1, source_target_pairs={{0,8},{1,9},{2,10},{3,11},{4,12},{5,13},{6,14},{7,15},{8,16},{9,17... | collective-permute-start | bytes 393224 | tf_op jit(solution)/shard_map/ppermute | solution.py:41
  26.0 4.3 %collective-permute-done.14.far = bf16[2,64,512]{2,1,0:T(8,128)(2,1)S(1)} collective-permute-done((bf16[2,64,512]{2,1,0:T(8,128)(2,1)S(1)}, bf16[2,64,512]{2,1,0:T(8,128)(2,1)S(1)}, u32[]{:S(2)}, u32[]{:S(2)}) %collective-permute-start.14) | collective-permute-done | bytes 131104 | tf_op jit(solution)/shard_map/ppermute | solution.py:41
  30.3 1.1 %collective-permute-start.15 = (bf16[64,512]{1,0:T(8,128)(2,1)S(1)}, bf16[64,512]{1,0:T(8,128)(2,1)S(1)}, u32[]{:S(2)}, u32[]{:S(2)}) collective-permute-start(bf16[64,512]{1,0:T(8,128)(2,1)S(1)} %get-tuple-element.69), channel_id=1, source_target_pairs={{0,32},{1,33},{2,34},{3,35},{4,36},{5,37},{6,38},{7,39},{8,40},{9,... | collective-permute-start | bytes 196616 | tf_op jit(solution)/shard_map/ppermute | solution.py:41
  31.5 2.1 %collective-permute-start.16 = (bf16[64,512]{1,0:T(8,128)(2,1)S(1)}, bf16[64,512]{1,0:T(8,128)(2,1)S(1)}, u32[]{:S(2)}, u32[]{:S(2)}) collective-permute-start(bf16[64,512]{1,0:T(8,128)(2,1)S(1)} %get-tuple-element.70), channel_id=1, source_target_pairs={{0,64},{1,65},{2,66},{3,67},{4,68},{5,69},{6,70},{7,71},{8,72},{9,... | collective-permute-start | bytes 196616 | tf_op jit(solution)/shard_map/ppermute | solution.py:41
  33.6 1.3 %collective-permute-start.17 = (bf16[64,512]{1,0:T(8,128)(2,1)S(1)}, bf16[64,512]{1,0:T(8,128)(2,1)S(1)}, u32[]{:S(2)}, u32[]{:S(2)}) collective-permute-start(bf16[64,512]{1,0:T(8,128)(2,1)S(1)} %get-tuple-element.71), channel_id=1, source_target_pairs={{0,96},{1,97},{2,98},{3,99},{4,100},{5,101},{6,102},{7,103},{8,104... | collective-permute-start | bytes 196616 | tf_op jit(solution)/shard_map/ppermute | solution.py:41
  34.9 1.0 %collective-permute-done.5.r2 = bf16[4,64,512]{2,1,0:T(8,128)(2,1)S(1)} collective-permute-done((bf16[4,64,512]{2,1,0:T(8,128)(2,1)S(1)}, bf16[4,64,512]{2,1,0:T(8,128)(2,1)S(1)}, u32[]{:S(2)}, u32[]{:S(2)}) %collective-permute-start.5) | collective-permute-done | bytes 262176 | tf_op jit(solution)/shard_map/ppermute | solution.py:41
  36.0 0.8 %collective-permute-start.7 = (bf16[64,512]{1,0:T(8,128)(2,1)S(1)}, bf16[64,512]{1,0:T(8,128)(2,1)S(1)}, u32[]{:S(2)}, u32[]{:S(2)}) collective-permute-start(bf16[64,512]{1,0:T(8,128)(2,1)S(1)} %get-tuple-element.54), channel_id=1, source_target_pairs={{0,8},{1,9},{2,10},{3,11},{4,12},{5,13},{6,14},{7,15},{8,16},{9,17... | collective-permute-start | bytes 196616 | tf_op jit(solution)/shard_map/ppermute | solution.py:41
  36.8 1.1 %collective-permute-start.8 = (bf16[64,512]{1,0:T(8,128)(2,1)S(1)}, bf16[64,512]{1,0:T(8,128)(2,1)S(1)}, u32[]{:S(2)}, u32[]{:S(2)}) collective-permute-start(bf16[64,512]{1,0:T(8,128)(2,1)S(1)} %get-tuple-element.55), channel_id=1, source_target_pairs={{0,16},{1,17},{2,18},{3,19},{4,20},{5,21},{6,22},{7,23},{8,24},{9,... | collective-permute-start | bytes 196616 | tf_op jit(solution)/shard_map/ppermute | solution.py:41
  37.8 1.4 %collective-permute-start.9 = (bf16[64,512]{1,0:T(8,128)(2,1)S(1)}, bf16[64,512]{1,0:T(8,128)(2,1)S(1)}, u32[]{:S(2)}, u32[]{:S(2)}) collective-permute-start(bf16[64,512]{1,0:T(8,128)(2,1)S(1)} %get-tuple-element.56), channel_id=1, source_target_pairs={{0,24},{1,25},{2,26},{3,27},{4,28},{5,29},{6,30},{7,31},{8,0},{9,1... | collective-permute-start | bytes 196616 | tf_op jit(solution)/shard_map/ppermute | solution.py:41
  39.3 0.9 %collective-permute-start.18 = (bf16[4,64,512]{2,1,0:T(8,128)(2,1)S(1)}, bf16[4,64,512]{2,1,0:T(8,128)(2,1)S(1)}, u32[]{:S(2)}, u32[]{:S(2)}) collective-permute-start(bf16[4,64,512]{2,1,0:T(8,128)(2,1)S(1)} %collect_kernel.2.b0), channel_id=1, source_target_pairs={{0,2},{1,3},{2,4},{3,5},{4,6},{5,7},{6,0},{7,1},{8,10},{9,11},{10,... | collective-permute-start | bytes 786440 | tf_op jit(solution)/shard_map/ppermute | solution.py:41
  40.2 2.8 %collective-permute-start.19 = (bf16[4,64,512]{2,1,0:T(8,128)(2,1)S(1)}, bf16[4,64,512]{2,1,0:T(8,128)(2,1)S(1)}, u32[]{:S(2)}, u32[]{:S(2)}) collective-permute-start(bf16[4,64,512]{2,1,0:T(8,128)(2,1)S(1)} %collect_kernel.2.b0), channel_id=1, source_target_pairs={{0,4},{1,5},{2,6},{3,7},{4,0},{5,1},{6,2},{7,3},{8,12},{9,13},{10,... | collective-permute-start | bytes 786440 | tf_op jit(solution)/shard_map/ppermute | solution.py:41
  43.5 2.5 %post_kernel.1 = (bf16[6,64,128]{2,1,0:T(8,128)(2,1)S(1)}, bf16[6,64,128]{2,1,0:T(8,128)(2,1)S(1)}, bf16[6,64,128]{2,1,0:T(8,128)(2,1)S(1)}, bf16[6,64,128]{2,1,0:T(8,128)(2,1)S(1)}) custom-call(f32[64,512]{1,0:T(8,128)S(1)} %get-tuple-element.53.own, bf16[64,512]{1,0:T(8,128)(2,1)S(1)} %collective-permute-done.7.r1, ...), custom_call_target="tpu_custom_call" | custom-call | flops 105000001536 | bytes 10500000 | tf_op jit(solution)/shard_map/post_kernel/pallas_call | solution.py:83
  46.0 1.1 %collective-permute-start.10 = (bf16[6,64,128]{2,1,0:T(8,128)(2,1)S(1)}, bf16[6,64,128]{2,1,0:T(8,128)(2,1)S(1)}, u32[]{:S(2)}, u32[]{:S(2)}) collective-permute-start(bf16[6,64,128]{2,1,0:T(8,128)(2,1)S(1)} %get-tuple-element.62), channel_id=1, source_target_pairs={{0,32},{1,33},{2,34},{3,35},{4,36},{5,37},{6,38},{7,39},{8,40},{9,... | collective-permute-start | bytes 294920 | tf_op jit(solution)/shard_map/ppermute | solution.py:41
  47.1 2.1 %collective-permute-start.11 = (bf16[6,64,128]{2,1,0:T(8,128)(2,1)S(1)}, bf16[6,64,128]{2,1,0:T(8,128)(2,1)S(1)}, u32[]{:S(2)}, u32[]{:S(2)}) collective-permute-start(bf16[6,64,128]{2,1,0:T(8,128)(2,1)S(1)} %get-tuple-element.63), channel_id=1, source_target_pairs={{0,64},{1,65},{2,66},{3,67},{4,68},{5,69},{6,70},{7,71},{8,72},{9,... | collective-permute-start | bytes 294920 | tf_op jit(solution)/shard_map/ppermute | solution.py:41
  49.3 1.3 %collective-permute-start.12 = (bf16[6,64,128]{2,1,0:T(8,128)(2,1)S(1)}, bf16[6,64,128]{2,1,0:T(8,128)(2,1)S(1)}, u32[]{:S(2)}, u32[]{:S(2)}) collective-permute-start(bf16[6,64,128]{2,1,0:T(8,128)(2,1)S(1)} %get-tuple-element.64), channel_id=1, source_target_pairs={{0,96},{1,97},{2,98},{3,99},{4,100},{5,101},{6,102},{7,103},{8,104... | collective-permute-start | bytes 294920 | tf_op jit(solution)/shard_map/ppermute | solution.py:41
  50.5 3.4 %collective-permute-done.19.b2 = bf16[4,64,512]{2,1,0:T(8,128)(2,1)S(1)} collective-permute-done((bf16[4,64,512]{2,1,0:T(8,128)(2,1)S(1)}, bf16[4,64,512]{2,1,0:T(8,128)(2,1)S(1)}, u32[]{:S(2)}, u32[]{:S(2)}) %collective-permute-start.19) | collective-permute-done | bytes 262176 | tf_op jit(solution)/shard_map/ppermute | solution.py:41
  54.0 2.1 %collective-permute-start.21 = (bf16[4,4,64,512]{3,2,1,0:T(8,128)(2,1)S(1)}, bf16[4,4,64,512]{3,2,1,0:T(8,128)(2,1)S(1)}, u32[]{:S(2)}, u32[]{:S(2)}) collective-permute-start(bf16[4,4,64,512]{3,2,1,0:T(8,128)(2,1)S(1)} %collect_kernel.3.blocks), channel_id=1, source_target_pairs={{0,1},{1,0},{2,3},{3,2},{4,5},{5,4},{6,7},{7,6},{8,9},{9,8},{10,11... | collective-permute-start | bytes 3145736 | tf_op jit(solution)/shard_map/ppermute | solution.py:41
  56.1 0.9 %out_kernel.1 = (bf16[3,128,256]{2,1,0:T(8,128)(2,1)}, f32[3,7,256]{2,1,0:T(8,128)}, f32[128,256]{1,0:T(8,128)}) custom-call(bf16[6,64,128]{2,1,0:T(8,128)(2,1)S(1)} %get-tuple-element.61.o0, bf16[6,64,128]{2,1,0:T(8,128)(2,1)S(1)} %collective-permute-done.10.r1, bf16[6,64,128]{2,1,0:T(8,128)(2,1)S(1)} %collective-permute-done.11.r2, ...), custom_call_target="tpu_custom_call" | custom-call | flops 35000000512 | bytes 3500000 | tf_op jit(solution)/shard_map/out_kernel/pallas_call | solution.py:83
  57.0 1.3 %near_kernel.1.held = f32[4,2,4,64,256]{4,3,2,1,0:T(8,128)} custom-call(bf16[4,4,64,512]{3,2,1,0:T(8,128)(2,1)S(1)} %collect_kernel.3.blocks, bf16[512,256]{1,0:T(8,128)(2,1)S(1)} %copy-done.1), custom_call_target="tpu_custom_call" | custom-call | tf_op jit(solution)/shard_map/near_kernel/pallas_call | solution.py:83
  58.3 1.3 %far_kernel.1 = f32[4,2,4,64,256]{4,3,2,1,0:T(8,128)} custom-call(bf16[4,4,64,512]{3,2,1,0:T(8,128)(2,1)S(1)} %collective-permute-done.21.blocks, bf16[512,256]{1,0:T(8,128)(2,1)S(1)} %copy-done.1, f32[4,2,4,64,256]{4,3,2,1,0:T(8,128)} %near_kernel.1.held), custom_call_target="tpu_custom_call", output_to_operand_aliasing={{}: (2, {})} | custom-call | flops 70000001024 | bytes 7000000 | tf_op jit(solution)/shard_map/far_kernel/pallas_call | solution.py:83
  (33 shorter events, 1.8 us)
Async XLA Ops:
  0.6 6.9 %copy-start.2 = (f32[3,7,256]{2,1,0:T(8,128)S(1)}, f32[3,7,256]{2,1,0:T(8,128)}, u32[]{:S(2)}) copy-start(f32[3,7,256]{2,1,0:T(8,128)} %taps_ref.1) | copy-start | bytes 64516
  1.8 7.8 %collective-permute-start = (bf16[8,64,128]{2,1,0:T(8,128)(2,1)S(1)}, bf16[8,64,128]{2,1,0:T(8,128)(2,1)S(1)}, u32[]{:S(2)}, u32[]{:S(2)}) collective-permute-start(bf16[8,64,128]{2,1,0:T(8,128)(2,1)S(1)} %get-tuple-element.39), channel_id=1, source_target_pairs={{0,32},{1,33},{2,34},{3,35},{4,36},{5,37},{6,38},{7,39},{8,40},{9,... | collective-permute-start | bytes 393224 | tf_op jit(solution)/shard_map/ppermute | solution.py:41
  3.9 8.2 %collective-permute-start.1 = (bf16[8,64,128]{2,1,0:T(8,128)(2,1)S(1)}, bf16[8,64,128]{2,1,0:T(8,128)(2,1)S(1)}, u32[]{:S(2)}, u32[]{:S(2)}) collective-permute-start(bf16[8,64,128]{2,1,0:T(8,128)(2,1)S(1)} %get-tuple-element.40), channel_id=1, source_target_pairs={{0,64},{1,65},{2,66},{3,67},{4,68},{5,69},{6,70},{7,71},{8,72},{9,... | collective-permute-start | bytes 393224 | tf_op jit(solution)/shard_map/ppermute | solution.py:41
  6.4 5.7 %collective-permute-start.2 = (bf16[8,64,128]{2,1,0:T(8,128)(2,1)S(1)}, bf16[8,64,128]{2,1,0:T(8,128)(2,1)S(1)}, u32[]{:S(2)}, u32[]{:S(2)}) collective-permute-start(bf16[8,64,128]{2,1,0:T(8,128)(2,1)S(1)} %get-tuple-element.41), channel_id=1, source_target_pairs={{0,96},{1,97},{2,98},{3,99},{4,100},{5,101},{6,102},{7,103},{8,104... | collective-permute-start | bytes 393224 | tf_op jit(solution)/shard_map/ppermute | solution.py:41
  12.6 7.0 %copy-start = (bf16[512,256]{1,0:T(8,128)(2,1)}, bf16[512,256]{1,0:T(8,128)(2,1)S(1)}, u32[]{:S(2)}) copy-start(bf16[512,256]{1,0:T(8,128)(2,1)S(1)} %get-tuple-element.44.behind.whole) | copy-start | bytes 786436
  12.6 7.0 %collective-permute-start.3 = (bf16[4,4,64,512]{3,2,1,0:T(8,128)(2,1)S(1)}, bf16[4,4,64,512]{3,2,1,0:T(8,128)(2,1)S(1)}, u32[]{:S(2)}, u32[]{:S(2)}) collective-permute-start(bf16[4,4,64,512]{3,2,1,0:T(8,128)(2,1)S(1)} %get-tuple-element.43), channel_id=1, source_target_pairs={{0,1},{1,0},{2,3},{3,2},{4,5},{5,4},{6,7},{7,6},{8,9},{9,8},{10,11... | collective-permute-start | bytes 3145736 | tf_op jit(solution)/shard_map/ppermute | solution.py:41
  15.9 9.2 %collective-permute-start.13 = (bf16[64,512]{1,0:T(8,128)(2,1)S(1)}, bf16[64,512]{1,0:T(8,128)(2,1)S(1)}, u32[]{:S(2)}, u32[]{:S(2)}) collective-permute-start(bf16[64,512]{1,0:T(8,128)(2,1)S(1)} %get-tuple-element.48.behind.b0), channel_id=1, source_target_pairs={{0,16},{1,17},{2,18},{3,19},{4,20},{5,21},{6,22},{7,23},{8,24},{9,... | collective-permute-start | bytes 196616 | tf_op jit(solution)/shard_map/ppermute | solution.py:41
  20.1 13.5 %collective-permute-start.4 = (bf16[4,64,512]{2,1,0:T(8,128)(2,1)S(1)}, bf16[4,64,512]{2,1,0:T(8,128)(2,1)S(1)}, u32[]{:S(2)}, u32[]{:S(2)}) collective-permute-start(bf16[4,64,512]{2,1,0:T(8,128)(2,1)S(1)} %get-tuple-element.50), channel_id=1, source_target_pairs={{0,2},{1,3},{2,4},{3,5},{4,6},{5,7},{6,0},{7,1},{8,10},{9,11},{10,... | collective-permute-start | bytes 786440 | tf_op jit(solution)/shard_map/ppermute | solution.py:41
  21.5 14.4 %collective-permute-start.5 = (bf16[4,64,512]{2,1,0:T(8,128)(2,1)S(1)}, bf16[4,64,512]{2,1,0:T(8,128)(2,1)S(1)}, u32[]{:S(2)}, u32[]{:S(2)}) collective-permute-start(bf16[4,64,512]{2,1,0:T(8,128)(2,1)S(1)} %get-tuple-element.51), channel_id=1, source_target_pairs={{0,4},{1,5},{2,6},{3,7},{4,0},{5,1},{6,2},{7,3},{8,12},{9,13},{10,... | collective-permute-start | bytes 786440 | tf_op jit(solution)/shard_map/ppermute | solution.py:41
  24.1 11.8 %collective-permute-start.6 = (bf16[4,64,512]{2,1,0:T(8,128)(2,1)S(1)}, bf16[4,64,512]{2,1,0:T(8,128)(2,1)S(1)}, u32[]{:S(2)}, u32[]{:S(2)}) collective-permute-start(bf16[4,64,512]{2,1,0:T(8,128)(2,1)S(1)} %get-tuple-element.52.block), channel_id=1, source_target_pairs={{0,6},{1,7},{2,0},{3,1},{4,2},{5,3},{6,4},{7,5},{8,14},{9,15},{10,... | collective-permute-start | bytes 786440 | tf_op jit(solution)/shard_map/ppermute | solution.py:41
  25.2 5.1 %collective-permute-start.14 = (bf16[2,64,512]{2,1,0:T(8,128)(2,1)S(1)}, bf16[2,64,512]{2,1,0:T(8,128)(2,1)S(1)}, u32[]{:S(2)}, u32[]{:S(2)}) collective-permute-start(bf16[2,64,512]{2,1,0:T(8,128)(2,1)S(1)} %pair_kernel.1.near), channel_id=1, source_target_pairs={{0,8},{1,9},{2,10},{3,11},{4,12},{5,13},{6,14},{7,15},{8,16},{9,17... | collective-permute-start | bytes 393224 | tf_op jit(solution)/shard_map/ppermute | solution.py:41
  30.3 7.5 %collective-permute-start.15 = (bf16[64,512]{1,0:T(8,128)(2,1)S(1)}, bf16[64,512]{1,0:T(8,128)(2,1)S(1)}, u32[]{:S(2)}, u32[]{:S(2)}) collective-permute-start(bf16[64,512]{1,0:T(8,128)(2,1)S(1)} %get-tuple-element.69), channel_id=1, source_target_pairs={{0,32},{1,33},{2,34},{3,35},{4,36},{5,37},{6,38},{7,39},{8,40},{9,... | collective-permute-start | bytes 196616 | tf_op jit(solution)/shard_map/ppermute | solution.py:41
  31.5 7.8 %collective-permute-start.16 = (bf16[64,512]{1,0:T(8,128)(2,1)S(1)}, bf16[64,512]{1,0:T(8,128)(2,1)S(1)}, u32[]{:S(2)}, u32[]{:S(2)}) collective-permute-start(bf16[64,512]{1,0:T(8,128)(2,1)S(1)} %get-tuple-element.70), channel_id=1, source_target_pairs={{0,64},{1,65},{2,66},{3,67},{4,68},{5,69},{6,70},{7,71},{8,72},{9,... | collective-permute-start | bytes 196616 | tf_op jit(solution)/shard_map/ppermute | solution.py:41
  33.6 5.7 %collective-permute-start.17 = (bf16[64,512]{1,0:T(8,128)(2,1)S(1)}, bf16[64,512]{1,0:T(8,128)(2,1)S(1)}, u32[]{:S(2)}, u32[]{:S(2)}) collective-permute-start(bf16[64,512]{1,0:T(8,128)(2,1)S(1)} %get-tuple-element.71), channel_id=1, source_target_pairs={{0,96},{1,97},{2,98},{3,99},{4,100},{5,101},{6,102},{7,103},{8,104... | collective-permute-start | bytes 196616 | tf_op jit(solution)/shard_map/ppermute | solution.py:41
  36.0 7.1 %collective-permute-start.7 = (bf16[64,512]{1,0:T(8,128)(2,1)S(1)}, bf16[64,512]{1,0:T(8,128)(2,1)S(1)}, u32[]{:S(2)}, u32[]{:S(2)}) collective-permute-start(bf16[64,512]{1,0:T(8,128)(2,1)S(1)} %get-tuple-element.54), channel_id=1, source_target_pairs={{0,8},{1,9},{2,10},{3,11},{4,12},{5,13},{6,14},{7,15},{8,16},{9,17... | collective-permute-start | bytes 196616 | tf_op jit(solution)/shard_map/ppermute | solution.py:41
  36.8 6.7 %collective-permute-start.8 = (bf16[64,512]{1,0:T(8,128)(2,1)S(1)}, bf16[64,512]{1,0:T(8,128)(2,1)S(1)}, u32[]{:S(2)}, u32[]{:S(2)}) collective-permute-start(bf16[64,512]{1,0:T(8,128)(2,1)S(1)} %get-tuple-element.55), channel_id=1, source_target_pairs={{0,16},{1,17},{2,18},{3,19},{4,20},{5,21},{6,22},{7,23},{8,24},{9,... | collective-permute-start | bytes 196616 | tf_op jit(solution)/shard_map/ppermute | solution.py:41
  37.8 5.6 %collective-permute-start.9 = (bf16[64,512]{1,0:T(8,128)(2,1)S(1)}, bf16[64,512]{1,0:T(8,128)(2,1)S(1)}, u32[]{:S(2)}, u32[]{:S(2)}) collective-permute-start(bf16[64,512]{1,0:T(8,128)(2,1)S(1)} %get-tuple-element.56), channel_id=1, source_target_pairs={{0,24},{1,25},{2,26},{3,27},{4,28},{5,29},{6,30},{7,31},{8,0},{9,1... | collective-permute-start | bytes 196616 | tf_op jit(solution)/shard_map/ppermute | solution.py:41
  39.3 10.0 %collective-permute-start.18 = (bf16[4,64,512]{2,1,0:T(8,128)(2,1)S(1)}, bf16[4,64,512]{2,1,0:T(8,128)(2,1)S(1)}, u32[]{:S(2)}, u32[]{:S(2)}) collective-permute-start(bf16[4,64,512]{2,1,0:T(8,128)(2,1)S(1)} %collect_kernel.2.b0), channel_id=1, source_target_pairs={{0,2},{1,3},{2,4},{3,5},{4,6},{5,7},{6,0},{7,1},{8,10},{9,11},{10,... | collective-permute-start | bytes 786440 | tf_op jit(solution)/shard_map/ppermute | solution.py:41
  40.2 13.7 %collective-permute-start.19 = (bf16[4,64,512]{2,1,0:T(8,128)(2,1)S(1)}, bf16[4,64,512]{2,1,0:T(8,128)(2,1)S(1)}, u32[]{:S(2)}, u32[]{:S(2)}) collective-permute-start(bf16[4,64,512]{2,1,0:T(8,128)(2,1)S(1)} %collect_kernel.2.b0), channel_id=1, source_target_pairs={{0,4},{1,5},{2,6},{3,7},{4,0},{5,1},{6,2},{7,3},{8,12},{9,13},{10,... | collective-permute-start | bytes 786440 | tf_op jit(solution)/shard_map/ppermute | solution.py:41
  43.0 10.9 %collective-permute-start.20 = (bf16[4,64,512]{2,1,0:T(8,128)(2,1)S(1)}, bf16[4,64,512]{2,1,0:T(8,128)(2,1)S(1)}, u32[]{:S(2)}, u32[]{:S(2)}) collective-permute-start(bf16[4,64,512]{2,1,0:T(8,128)(2,1)S(1)} %collect_kernel.2.b0), channel_id=1, source_target_pairs={{0,6},{1,7},{2,0},{3,1},{4,2},{5,3},{6,4},{7,5},{8,14},{9,15},{10,... | collective-permute-start | bytes 786440 | tf_op jit(solution)/shard_map/ppermute | solution.py:41
  46.0 10.1 %collective-permute-start.10 = (bf16[6,64,128]{2,1,0:T(8,128)(2,1)S(1)}, bf16[6,64,128]{2,1,0:T(8,128)(2,1)S(1)}, u32[]{:S(2)}, u32[]{:S(2)}) collective-permute-start(bf16[6,64,128]{2,1,0:T(8,128)(2,1)S(1)} %get-tuple-element.62), channel_id=1, source_target_pairs={{0,32},{1,33},{2,34},{3,35},{4,36},{5,37},{6,38},{7,39},{8,40},{9,... | collective-permute-start | bytes 294920 | tf_op jit(solution)/shard_map/ppermute | solution.py:41
  47.1 8.9 %collective-permute-start.11 = (bf16[6,64,128]{2,1,0:T(8,128)(2,1)S(1)}, bf16[6,64,128]{2,1,0:T(8,128)(2,1)S(1)}, u32[]{:S(2)}, u32[]{:S(2)}) collective-permute-start(bf16[6,64,128]{2,1,0:T(8,128)(2,1)S(1)} %get-tuple-element.63), channel_id=1, source_target_pairs={{0,64},{1,65},{2,66},{3,67},{4,68},{5,69},{6,70},{7,71},{8,72},{9,... | collective-permute-start | bytes 294920 | tf_op jit(solution)/shard_map/ppermute | solution.py:41
  49.3 6.8 %collective-permute-start.12 = (bf16[6,64,128]{2,1,0:T(8,128)(2,1)S(1)}, bf16[6,64,128]{2,1,0:T(8,128)(2,1)S(1)}, u32[]{:S(2)}, u32[]{:S(2)}) collective-permute-start(bf16[6,64,128]{2,1,0:T(8,128)(2,1)S(1)} %get-tuple-element.64), channel_id=1, source_target_pairs={{0,96},{1,97},{2,98},{3,99},{4,100},{5,101},{6,102},{7,103},{8,104... | collective-permute-start | bytes 294920 | tf_op jit(solution)/shard_map/ppermute | solution.py:41
  54.0 4.3 %collective-permute-start.21 = (bf16[4,4,64,512]{3,2,1,0:T(8,128)(2,1)S(1)}, bf16[4,4,64,512]{3,2,1,0:T(8,128)(2,1)S(1)}, u32[]{:S(2)}, u32[]{:S(2)}) collective-permute-start(bf16[4,4,64,512]{3,2,1,0:T(8,128)(2,1)S(1)} %collect_kernel.3.blocks), channel_id=1, source_target_pairs={{0,1},{1,0},{2,3},{3,2},{4,5},{5,4},{6,7},{7,6},{8,9},{9,8},{10,11... | collective-permute-start | bytes 3145736 | tf_op jit(solution)/shard_map/ppermute | solution.py:41
  56.1 1.0 %copy-start.1 = (bf16[512,256]{1,0:T(8,128)(2,1)S(1)}, bf16[512,256]{1,0:T(8,128)(2,1)}, u32[]{:S(2)}) copy-start(bf16[512,256]{1,0:T(8,128)(2,1)} %copy-done) | copy-start | bytes 786436

commit v8 on v7

--- a/solution.py
+++ b/solution.py
@@ -129,12 +129,14 @@
         copy = pltpu.make_async_copy(src, dst, sems.at[place])
         copy.start()
         copies.append(copy)
-    for copy in copies:
-        copy.wait()
+    copies[0].wait()
     for stream in range(4):
+        if stream == 3:
+            copies[1].wait()
         flipped = (feat_ref[stream] if stream < 3 else filt_ref[...]).T
         for quarter in range(4):
             held[quarter, stream] = flipped[quarter * 64 : quarter * 64 + 64]
+    copies[2].wait()
     for by, out in enumerate((p0, p1, p2, p3)):
         out[0:4] = held[lax.rem(x + by, 4)]
         for row in range(2):

time: 59.8 us -> 59.8 us (level)
  no operation moved by 1% of the time
where the time goes in v8:
time: 59.8 us; the launch traced here: 59.7 us
  starting transfers between devices  35.4 us (59%)
  Pallas kernels  12.2 us (20%)
  waiting for transfers between devices  11.2 us (19%)
  between operations  0.76 us (1%)
    ppermute x22, starting transfers between devices, move(): return lax.ppermute(array, ('ctx', 'ch'), pairs)  35.4 us
    pallas_call x15, Pallas kernels, call(): pl.pallas_call(kernel, out_shape=out_shape, name=kernel.__name__, in_spec...  12.2 us
    ppermute x22, waiting for transfers between devices, move(): return lax.ppermute(array, ('ctx', 'ch'), pairs)  11.2 us
  transfers between devices with their start and end apart: 22, of which 4 were waited for; matrix products, arithmetic and copies ran while one was open for 0% of the time, Pallas kernels for 15%

profile of v8, /device:TPU:1, one launch (start us, length us, event | category | flops | bytes accessed | tf_op | source)
XLA Modules:
  0.0 59.7 jit_solution(291702303154988701)
XLA Ops:
  0.6 1.2 %pack_kernel.1 = (bf16[8,64,128]{2,1,0:T(8,128)(2,1)S(1)}, bf16[8,64,128]{2,1,0:T(8,128)(2,1)S(1)}, bf16[8,64,128]{2,1,0:T(8,128)(2,1)S(1)}, bf16[8,64,128]{2,1,0:T(8,128)(2,1)S(1)}) custom-call(bf16[3,128,256]{2,1,0:T(8,128)(2,1)} %feat_hbm.1, bf16[128,256]{1,0:T(8,128)(2,1)} %filt_hbm.1, bf16[128,256]{1,0:T(8,128)(2,1)} %grad_hbm.1), custom_call_target="tpu_custom_call" | custom-call | flops 70000001024 | bytes 7000000 | tf_op jit(solution)/shard_map/pack_kernel/pallas_call | solution.py:83
  1.8 2.1 %collective-permute-start = (bf16[8,64,128]{2,1,0:T(8,128)(2,1)S(1)}, bf16[8,64,128]{2,1,0:T(8,128)(2,1)S(1)}, u32[]{:S(2)}, u32[]{:S(2)}) collective-permute-start(bf16[8,64,128]{2,1,0:T(8,128)(2,1)S(1)} %get-tuple-element.39), channel_id=1, source_target_pairs={{0,32},{1,33},{2,34},{3,35},{4,36},{5,37},{6,38},{7,39},{8,40},{9,... | collective-permute-start | bytes 393224 | tf_op jit(solution)/shard_map/ppermute | solution.py:41
  3.9 2.5 %collective-permute-start.1 = (bf16[8,64,128]{2,1,0:T(8,128)(2,1)S(1)}, bf16[8,64,128]{2,1,0:T(8,128)(2,1)S(1)}, u32[]{:S(2)}, u32[]{:S(2)}) collective-permute-start(bf16[8,64,128]{2,1,0:T(8,128)(2,1)S(1)} %get-tuple-element.40), channel_id=1, source_target_pairs={{0,64},{1,65},{2,66},{3,67},{4,68},{5,69},{6,70},{7,71},{8,72},{9,... | collective-permute-start | bytes 393224 | tf_op jit(solution)/shard_map/ppermute | solution.py:41
  6.4 1.2 %collective-permute-start.2 = (bf16[8,64,128]{2,1,0:T(8,128)(2,1)S(1)}, bf16[8,64,128]{2,1,0:T(8,128)(2,1)S(1)}, u32[]{:S(2)}, u32[]{:S(2)}) collective-permute-start(bf16[8,64,128]{2,1,0:T(8,128)(2,1)S(1)} %get-tuple-element.41), channel_id=1, source_target_pairs={{0,96},{1,97},{2,98},{3,99},{4,100},{5,101},{6,102},{7,103},{8,104... | collective-permute-start | bytes 393224 | tf_op jit(solution)/shard_map/ppermute | solution.py:41
  7.6 2.1 %fetch_kernel.1 = (bf16[2,4,4,64,256]{4,3,2,1,0:T(8,128)(2,1)S(1)}, bf16[512,1024]{1,0:T(8,128)(2,1)S(1)}, bf16[512,1024]{1,0:T(8,128)(2,1)S(1)}, f32[64,128]{1,0:T(8,128)S(1)}) custom-call(bf16[4,4,2,4,64,256]{5,4,3,2,1,0:T(8,128)(2,1)} %bitcast.3, bf16[512,1024]{1,0:T(8,128)(2,1)} %constant.4.clone.high_hbm, bf16[512,1024]{1,0:T(8,128)(2,1)} %constant.5.clone.low_hbm, ...), custom_call_target="tpu_custom_call" | custom-call | flops 70000001024 | bytes 7000000 | tf_op jit(solution)/shard_map/fetch_kernel/pallas_call | solution.py:83
  9.6 2.5 %collective-permute-done.1.r2 = bf16[8,64,128]{2,1,0:T(8,128)(2,1)S(1)} collective-permute-done((bf16[8,64,128]{2,1,0:T(8,128)(2,1)S(1)}, bf16[8,64,128]{2,1,0:T(8,128)(2,1)S(1)}, u32[]{:S(2)}, u32[]{:S(2)}) %collective-permute-start.1) | collective-permute-done | bytes 131104 | tf_op jit(solution)/shard_map/ppermute | solution.py:41
  12.7 1.6 %collective-permute-start.3 = (bf16[4,4,64,512]{3,2,1,0:T(8,128)(2,1)S(1)}, bf16[4,4,64,512]{3,2,1,0:T(8,128)(2,1)S(1)}, u32[]{:S(2)}, u32[]{:S(2)}) collective-permute-start(bf16[4,4,64,512]{3,2,1,0:T(8,128)(2,1)S(1)} %get-tuple-element.43), channel_id=1, source_target_pairs={{0,1},{1,0},{2,3},{3,2},{4,5},{5,4},{6,7},{7,6},{8,9},{9,8},{10,11... | collective-permute-start | bytes 3145736 | tf_op jit(solution)/shard_map/ppermute | solution.py:41
  14.3 1.7 %pre_kernel.1 = (bf16[64,512]{1,0:T(8,128)(2,1)S(1)}, f32[3,64,512]{2,1,0:T(8,128)S(1)}, f32[64,512]{1,0:T(8,128)S(1)}, f32[128,1024]{1,0:T(8,128)S(1)}, bf16[3,64,512]{2,1,0:T(8,128)(2,1)S(1)}) custom-call(bf16[8,64,128]{2,1,0:T(8,128)(2,1)S(1)} %get-tuple-element.38.behind.p0, bf16[8,64,128]{2,1,0:T(8,128)(2,1)S(1)} %collective-permute-done.r1, ...), custom_call_target="tpu_custom_call" | custom-call | flops 70000001024 | bytes 7000000 | tf_op jit(solution)/shard_map/pre_kernel/pallas_call | solution.py:83
  15.9 3.7 %collective-permute-start.13 = (bf16[64,512]{1,0:T(8,128)(2,1)S(1)}, bf16[64,512]{1,0:T(8,128)(2,1)S(1)}, u32[]{:S(2)}, u32[]{:S(2)}) collective-permute-start(bf16[64,512]{1,0:T(8,128)(2,1)S(1)} %get-tuple-element.48.behind.b0), channel_id=1, source_target_pairs={{0,16},{1,17},{2,18},{3,19},{4,20},{5,21},{6,22},{7,23},{8,24},{9,... | collective-permute-start | bytes 196616 | tf_op jit(solution)/shard_map/ppermute | solution.py:41
  20.1 1.4 %collective-permute-start.4 = (bf16[4,64,512]{2,1,0:T(8,128)(2,1)S(1)}, bf16[4,64,512]{2,1,0:T(8,128)(2,1)S(1)}, u32[]{:S(2)}, u32[]{:S(2)}) collective-permute-start(bf16[4,64,512]{2,1,0:T(8,128)(2,1)S(1)} %get-tuple-element.50), channel_id=1, source_target_pairs={{0,2},{1,3},{2,4},{3,5},{4,6},{5,7},{6,0},{7,1},{8,10},{9,11},{10,... | collective-permute-start | bytes 786440 | tf_op jit(solution)/shard_map/ppermute | solution.py:41
  21.5 2.6 %collective-permute-start.5 = (bf16[4,64,512]{2,1,0:T(8,128)(2,1)S(1)}, bf16[4,64,512]{2,1,0:T(8,128)(2,1)S(1)}, u32[]{:S(2)}, u32[]{:S(2)}) collective-permute-start(bf16[4,64,512]{2,1,0:T(8,128)(2,1)S(1)} %get-tuple-element.51), channel_id=1, source_target_pairs={{0,4},{1,5},{2,6},{3,7},{4,0},{5,1},{6,2},{7,3},{8,12},{9,13},{10,... | collective-permute-start | bytes 786440 | tf_op jit(solution)/shard_map/ppermute | solution.py:41
  24.1 1.1 %collective-permute-start.6 = (bf16[4,64,512]{2,1,0:T(8,128)(2,1)S(1)}, bf16[4,64,512]{2,1,0:T(8,128)(2,1)S(1)}, u32[]{:S(2)}, u32[]{:S(2)}) collective-permute-start(bf16[4,64,512]{2,1,0:T(8,128)(2,1)S(1)} %get-tuple-element.52.block), channel_id=1, source_target_pairs={{0,6},{1,7},{2,0},{3,1},{4,2},{5,3},{6,4},{7,5},{8,14},{9,15},{10,... | collective-permute-start | bytes 786440 | tf_op jit(solution)/shard_map/ppermute | solution.py:41
  25.2 0.8 %collective-permute-start.14 = (bf16[2,64,512]{2,1,0:T(8,128)(2,1)S(1)}, bf16[2,64,512]{2,1,0:T(8,128)(2,1)S(1)}, u32[]{:S(2)}, u32[]{:S(2)}) collective-permute-start(bf16[2,64,512]{2,1,0:T(8,128)(2,1)S(1)} %pair_kernel.1.near), channel_id=1, source_target_pairs={{0,8},{1,9},{2,10},{3,11},{4,12},{5,13},{6,14},{7,15},{8,16},{9,17... | collective-permute-start | bytes 393224 | tf_op jit(solution)/shard_map/ppermute | solution.py:41
  26.0 4.3 %collective-permute-done.14.far = bf16[2,64,512]{2,1,0:T(8,128)(2,1)S(1)} collective-permute-done((bf16[2,64,512]{2,1,0:T(8,128)(2,1)S(1)}, bf16[2,64,512]{2,1,0:T(8,128)(2,1)S(1)}, u32[]{:S(2)}, u32[]{:S(2)}) %collective-permute-start.14) | collective-permute-done | bytes 131104 | tf_op jit(solution)/shard_map/ppermute | solution.py:41
  30.3 1.1 %collective-permute-start.15 = (bf16[64,512]{1,0:T(8,128)(2,1)S(1)}, bf16[64,512]{1,0:T(8,128)(2,1)S(1)}, u32[]{:S(2)}, u32[]{:S(2)}) collective-permute-start(bf16[64,512]{1,0:T(8,128)(2,1)S(1)} %get-tuple-element.69), channel_id=1, source_target_pairs={{0,32},{1,33},{2,34},{3,35},{4,36},{5,37},{6,38},{7,39},{8,40},{9,... | collective-permute-start | bytes 196616 | tf_op jit(solution)/shard_map/ppermute | solution.py:41
  31.5 2.1 %collective-permute-start.16 = (bf16[64,512]{1,0:T(8,128)(2,1)S(1)}, bf16[64,512]{1,0:T(8,128)(2,1)S(1)}, u32[]{:S(2)}, u32[]{:S(2)}) collective-permute-start(bf16[64,512]{1,0:T(8,128)(2,1)S(1)} %get-tuple-element.70), channel_id=1, source_target_pairs={{0,64},{1,65},{2,66},{3,67},{4,68},{5,69},{6,70},{7,71},{8,72},{9,... | collective-permute-start | bytes 196616 | tf_op jit(solution)/shard_map/ppermute | solution.py:41
  33.6 1.3 %collective-permute-start.17 = (bf16[64,512]{1,0:T(8,128)(2,1)S(1)}, bf16[64,512]{1,0:T(8,128)(2,1)S(1)}, u32[]{:S(2)}, u32[]{:S(2)}) collective-permute-start(bf16[64,512]{1,0:T(8,128)(2,1)S(1)} %get-tuple-element.71), channel_id=1, source_target_pairs={{0,96},{1,97},{2,98},{3,99},{4,100},{5,101},{6,102},{7,103},{8,104... | collective-permute-start | bytes 196616 | tf_op jit(solution)/shard_map/ppermute | solution.py:41
  34.9 1.0 %collective-permute-done.5.r2 = bf16[4,64,512]{2,1,0:T(8,128)(2,1)S(1)} collective-permute-done((bf16[4,64,512]{2,1,0:T(8,128)(2,1)S(1)}, bf16[4,64,512]{2,1,0:T(8,128)(2,1)S(1)}, u32[]{:S(2)}, u32[]{:S(2)}) %collective-permute-start.5) | collective-permute-done | bytes 262176 | tf_op jit(solution)/shard_map/ppermute | solution.py:41
  36.0 0.8 %collective-permute-start.7 = (bf16[64,512]{1,0:T(8,128)(2,1)S(1)}, bf16[64,512]{1,0:T(8,128)(2,1)S(1)}, u32[]{:S(2)}, u32[]{:S(2)}) collective-permute-start(bf16[64,512]{1,0:T(8,128)(2,1)S(1)} %get-tuple-element.54), channel_id=1, source_target_pairs={{0,8},{1,9},{2,10},{3,11},{4,12},{5,13},{6,14},{7,15},{8,16},{9,17... | collective-permute-start | bytes 196616 | tf_op jit(solution)/shard_map/ppermute | solution.py:41
  36.8 1.1 %collective-permute-start.8 = (bf16[64,512]{1,0:T(8,128)(2,1)S(1)}, bf16[64,512]{1,0:T(8,128)(2,1)S(1)}, u32[]{:S(2)}, u32[]{:S(2)}) collective-permute-start(bf16[64,512]{1,0:T(8,128)(2,1)S(1)} %get-tuple-element.55), channel_id=1, source_target_pairs={{0,16},{1,17},{2,18},{3,19},{4,20},{5,21},{6,22},{7,23},{8,24},{9,... | collective-permute-start | bytes 196616 | tf_op jit(solution)/shard_map/ppermute | solution.py:41
  37.8 1.4 %collective-permute-start.9 = (bf16[64,512]{1,0:T(8,128)(2,1)S(1)}, bf16[64,512]{1,0:T(8,128)(2,1)S(1)}, u32[]{:S(2)}, u32[]{:S(2)}) collective-permute-start(bf16[64,512]{1,0:T(8,128)(2,1)S(1)} %get-tuple-element.56), channel_id=1, source_target_pairs={{0,24},{1,25},{2,26},{3,27},{4,28},{5,29},{6,30},{7,31},{8,0},{9,1... | collective-permute-start | bytes 196616 | tf_op jit(solution)/shard_map/ppermute | solution.py:41
  39.3 0.9 %collective-permute-start.18 = (bf16[4,64,512]{2,1,0:T(8,128)(2,1)S(1)}, bf16[4,64,512]{2,1,0:T(8,128)(2,1)S(1)}, u32[]{:S(2)}, u32[]{:S(2)}) collective-permute-start(bf16[4,64,512]{2,1,0:T(8,128)(2,1)S(1)} %collect_kernel.2.b0), channel_id=1, source_target_pairs={{0,2},{1,3},{2,4},{3,5},{4,6},{5,7},{6,0},{7,1},{8,10},{9,11},{10,... | collective-permute-start | bytes 786440 | tf_op jit(solution)/shard_map/ppermute | solution.py:41
  40.2 2.8 %collective-permute-start.19 = (bf16[4,64,512]{2,1,0:T(8,128)(2,1)S(1)}, bf16[4,64,512]{2,1,0:T(8,128)(2,1)S(1)}, u32[]{:S(2)}, u32[]{:S(2)}) collective-permute-start(bf16[4,64,512]{2,1,0:T(8,128)(2,1)S(1)} %collect_kernel.2.b0), channel_id=1, source_target_pairs={{0,4},{1,5},{2,6},{3,7},{4,0},{5,1},{6,2},{7,3},{8,12},{9,13},{10,... | collective-permute-start | bytes 786440 | tf_op jit(solution)/shard_map/ppermute | solution.py:41
  43.5 2.5 %post_kernel.1 = (bf16[6,64,128]{2,1,0:T(8,128)(2,1)S(1)}, bf16[6,64,128]{2,1,0:T(8,128)(2,1)S(1)}, bf16[6,64,128]{2,1,0:T(8,128)(2,1)S(1)}, bf16[6,64,128]{2,1,0:T(8,128)(2,1)S(1)}) custom-call(f32[64,512]{1,0:T(8,128)S(1)} %get-tuple-element.53.own, bf16[64,512]{1,0:T(8,128)(2,1)S(1)} %collective-permute-done.7.r1, ...), custom_call_target="tpu_custom_call" | custom-call | flops 105000001536 | bytes 10500000 | tf_op jit(solution)/shard_map/post_kernel/pallas_call | solution.py:83
  46.0 1.1 %collective-permute-start.10 = (bf16[6,64,128]{2,1,0:T(8,128)(2,1)S(1)}, bf16[6,64,128]{2,1,0:T(8,128)(2,1)S(1)}, u32[]{:S(2)}, u32[]{:S(2)}) collective-permute-start(bf16[6,64,128]{2,1,0:T(8,128)(2,1)S(1)} %get-tuple-element.62), channel_id=1, source_target_pairs={{0,32},{1,33},{2,34},{3,35},{4,36},{5,37},{6,38},{7,39},{8,40},{9,... | collective-permute-start | bytes 294920 | tf_op jit(solution)/shard_map/ppermute | solution.py:41
  47.1 2.1 %collective-permute-start.11 = (bf16[6,64,128]{2,1,0:T(8,128)(2,1)S(1)}, bf16[6,64,128]{2,1,0:T(8,128)(2,1)S(1)}, u32[]{:S(2)}, u32[]{:S(2)}) collective-permute-start(bf16[6,64,128]{2,1,0:T(8,128)(2,1)S(1)} %get-tuple-element.63), channel_id=1, source_target_pairs={{0,64},{1,65},{2,66},{3,67},{4,68},{5,69},{6,70},{7,71},{8,72},{9,... | collective-permute-start | bytes 294920 | tf_op jit(solution)/shard_map/ppermute | solution.py:41
  49.3 1.3 %collective-permute-start.12 = (bf16[6,64,128]{2,1,0:T(8,128)(2,1)S(1)}, bf16[6,64,128]{2,1,0:T(8,128)(2,1)S(1)}, u32[]{:S(2)}, u32[]{:S(2)}) collective-permute-start(bf16[6,64,128]{2,1,0:T(8,128)(2,1)S(1)} %get-tuple-element.64), channel_id=1, source_target_pairs={{0,96},{1,97},{2,98},{3,99},{4,100},{5,101},{6,102},{7,103},{8,104... | collective-permute-start | bytes 294920 | tf_op jit(solution)/shard_map/ppermute | solution.py:41
  50.5 3.4 %collective-permute-done.19.b2 = bf16[4,64,512]{2,1,0:T(8,128)(2,1)S(1)} collective-permute-done((bf16[4,64,512]{2,1,0:T(8,128)(2,1)S(1)}, bf16[4,64,512]{2,1,0:T(8,128)(2,1)S(1)}, u32[]{:S(2)}, u32[]{:S(2)}) %collective-permute-start.19) | collective-permute-done | bytes 262176 | tf_op jit(solution)/shard_map/ppermute | solution.py:41
  54.0 2.1 %collective-permute-start.21 = (bf16[4,4,64,512]{3,2,1,0:T(8,128)(2,1)S(1)}, bf16[4,4,64,512]{3,2,1,0:T(8,128)(2,1)S(1)}, u32[]{:S(2)}, u32[]{:S(2)}) collective-permute-start(bf16[4,4,64,512]{3,2,1,0:T(8,128)(2,1)S(1)} %collect_kernel.3.blocks), channel_id=1, source_target_pairs={{0,1},{1,0},{2,3},{3,2},{4,5},{5,4},{6,7},{7,6},{8,9},{9,8},{10,11... | collective-permute-start | bytes 3145736 | tf_op jit(solution)/shard_map/ppermute | solution.py:41
  56.1 0.9 %out_kernel.1 = (bf16[3,128,256]{2,1,0:T(8,128)(2,1)}, f32[3,7,256]{2,1,0:T(8,128)}, f32[128,256]{1,0:T(8,128)}) custom-call(bf16[6,64,128]{2,1,0:T(8,128)(2,1)S(1)} %get-tuple-element.61.o0, bf16[6,64,128]{2,1,0:T(8,128)(2,1)S(1)} %collective-permute-done.10.r1, bf16[6,64,128]{2,1,0:T(8,128)(2,1)S(1)} %collective-permute-done.11.r2, ...), custom_call_target="tpu_custom_call" | custom-call | flops 35000000512 | bytes 3500000 | tf_op jit(solution)/shard_map/out_kernel/pallas_call | solution.py:83
  57.0 1.3 %near_kernel.1.held = f32[4,2,4,64,256]{4,3,2,1,0:T(8,128)} custom-call(bf16[4,4,64,512]{3,2,1,0:T(8,128)(2,1)S(1)} %collect_kernel.3.blocks, bf16[512,256]{1,0:T(8,128)(2,1)S(1)} %copy-done.1), custom_call_target="tpu_custom_call" | custom-call | tf_op jit(solution)/shard_map/near_kernel/pallas_call | solution.py:83
  58.4 1.3 %far_kernel.1 = f32[4,2,4,64,256]{4,3,2,1,0:T(8,128)} custom-call(bf16[4,4,64,512]{3,2,1,0:T(8,128)(2,1)S(1)} %collective-permute-done.21.blocks, bf16[512,256]{1,0:T(8,128)(2,1)S(1)} %copy-done.1, f32[4,2,4,64,256]{4,3,2,1,0:T(8,128)} %near_kernel.1.held), custom_call_target="tpu_custom_call", output_to_operand_aliasing={{}: (2, {})} | custom-call | flops 70000001024 | bytes 7000000 | tf_op jit(solution)/shard_map/far_kernel/pallas_call | solution.py:83
  (33 shorter events, 1.8 us)
Async XLA Ops:
  0.6 6.9 %copy-start.2 = (f32[3,7,256]{2,1,0:T(8,128)S(1)}, f32[3,7,256]{2,1,0:T(8,128)}, u32[]{:S(2)}) copy-start(f32[3,7,256]{2,1,0:T(8,128)} %taps_ref.1) | copy-start | bytes 64516
  1.8 7.8 %collective-permute-start = (bf16[8,64,128]{2,1,0:T(8,128)(2,1)S(1)}, bf16[8,64,128]{2,1,0:T(8,128)(2,1)S(1)}, u32[]{:S(2)}, u32[]{:S(2)}) collective-permute-start(bf16[8,64,128]{2,1,0:T(8,128)(2,1)S(1)} %get-tuple-element.39), channel_id=1, source_target_pairs={{0,32},{1,33},{2,34},{3,35},{4,36},{5,37},{6,38},{7,39},{8,40},{9,... | collective-permute-start | bytes 393224 | tf_op jit(solution)/shard_map/ppermute | solution.py:41
  3.9 8.2 %collective-permute-start.1 = (bf16[8,64,128]{2,1,0:T(8,128)(2,1)S(1)}, bf16[8,64,128]{2,1,0:T(8,128)(2,1)S(1)}, u32[]{:S(2)}, u32[]{:S(2)}) collective-permute-start(bf16[8,64,128]{2,1,0:T(8,128)(2,1)S(1)} %get-tuple-element.40), channel_id=1, source_target_pairs={{0,64},{1,65},{2,66},{3,67},{4,68},{5,69},{6,70},{7,71},{8,72},{9,... | collective-permute-start | bytes 393224 | tf_op jit(solution)/shard_map/ppermute | solution.py:41
  6.4 5.7 %collective-permute-start.2 = (bf16[8,64,128]{2,1,0:T(8,128)(2,1)S(1)}, bf16[8,64,128]{2,1,0:T(8,128)(2,1)S(1)}, u32[]{:S(2)}, u32[]{:S(2)}) collective-permute-start(bf16[8,64,128]{2,1,0:T(8,128)(2,1)S(1)} %get-tuple-element.41), channel_id=1, source_target_pairs={{0,96},{1,97},{2,98},{3,99},{4,100},{5,101},{6,102},{7,103},{8,104... | collective-permute-start | bytes 393224 | tf_op jit(solution)/shard_map/ppermute | solution.py:41
  12.6 7.0 %copy-start = (bf16[512,256]{1,0:T(8,128)(2,1)}, bf16[512,256]{1,0:T(8,128)(2,1)S(1)}, u32[]{:S(2)}) copy-start(bf16[512,256]{1,0:T(8,128)(2,1)S(1)} %get-tuple-element.44.behind.whole) | copy-start | bytes 786436
  12.7 7.0 %collective-permute-start.3 = (bf16[4,4,64,512]{3,2,1,0:T(8,128)(2,1)S(1)}, bf16[4,4,64,512]{3,2,1,0:T(8,128)(2,1)S(1)}, u32[]{:S(2)}, u32[]{:S(2)}) collective-permute-start(bf16[4,4,64,512]{3,2,1,0:T(8,128)(2,1)S(1)} %get-tuple-element.43), channel_id=1, source_target_pairs={{0,1},{1,0},{2,3},{3,2},{4,5},{5,4},{6,7},{7,6},{8,9},{9,8},{10,11... | collective-permute-start | bytes 3145736 | tf_op jit(solution)/shard_map/ppermute | solution.py:41
  15.9 9.2 %collective-permute-start.13 = (bf16[64,512]{1,0:T(8,128)(2,1)S(1)}, bf16[64,512]{1,0:T(8,128)(2,1)S(1)}, u32[]{:S(2)}, u32[]{:S(2)}) collective-permute-start(bf16[64,512]{1,0:T(8,128)(2,1)S(1)} %get-tuple-element.48.behind.b0), channel_id=1, source_target_pairs={{0,16},{1,17},{2,18},{3,19},{4,20},{5,21},{6,22},{7,23},{8,24},{9,... | collective-permute-start | bytes 196616 | tf_op jit(solution)/shard_map/ppermute | solution.py:41
  20.1 13.5 %collective-permute-start.4 = (bf16[4,64,512]{2,1,0:T(8,128)(2,1)S(1)}, bf16[4,64,512]{2,1,0:T(8,128)(2,1)S(1)}, u32[]{:S(2)}, u32[]{:S(2)}) collective-permute-start(bf16[4,64,512]{2,1,0:T(8,128)(2,1)S(1)} %get-tuple-element.50), channel_id=1, source_target_pairs={{0,2},{1,3},{2,4},{3,5},{4,6},{5,7},{6,0},{7,1},{8,10},{9,11},{10,... | collective-permute-start | bytes 786440 | tf_op jit(solution)/shard_map/ppermute | solution.py:41
  21.5 14.4 %collective-permute-start.5 = (bf16[4,64,512]{2,1,0:T(8,128)(2,1)S(1)}, bf16[4,64,512]{2,1,0:T(8,128)(2,1)S(1)}, u32[]{:S(2)}, u32[]{:S(2)}) collective-permute-start(bf16[4,64,512]{2,1,0:T(8,128)(2,1)S(1)} %get-tuple-element.51), channel_id=1, source_target_pairs={{0,4},{1,5},{2,6},{3,7},{4,0},{5,1},{6,2},{7,3},{8,12},{9,13},{10,... | collective-permute-start | bytes 786440 | tf_op jit(solution)/shard_map/ppermute | solution.py:41
  24.1 11.8 %collective-permute-start.6 = (bf16[4,64,512]{2,1,0:T(8,128)(2,1)S(1)}, bf16[4,64,512]{2,1,0:T(8,128)(2,1)S(1)}, u32[]{:S(2)}, u32[]{:S(2)}) collective-permute-start(bf16[4,64,512]{2,1,0:T(8,128)(2,1)S(1)} %get-tuple-element.52.block), channel_id=1, source_target_pairs={{0,6},{1,7},{2,0},{3,1},{4,2},{5,3},{6,4},{7,5},{8,14},{9,15},{10,... | collective-permute-start | bytes 786440 | tf_op jit(solution)/shard_map/ppermute | solution.py:41
  25.2 5.1 %collective-permute-start.14 = (bf16[2,64,512]{2,1,0:T(8,128)(2,1)S(1)}, bf16[2,64,512]{2,1,0:T(8,128)(2,1)S(1)}, u32[]{:S(2)}, u32[]{:S(2)}) collective-permute-start(bf16[2,64,512]{2,1,0:T(8,128)(2,1)S(1)} %pair_kernel.1.near), channel_id=1, source_target_pairs={{0,8},{1,9},{2,10},{3,11},{4,12},{5,13},{6,14},{7,15},{8,16},{9,17... | collective-permute-start | bytes 393224 | tf_op jit(solution)/shard_map/ppermute | solution.py:41
  30.3 7.5 %collective-permute-start.15 = (bf16[64,512]{1,0:T(8,128)(2,1)S(1)}, bf16[64,512]{1,0:T(8,128)(2,1)S(1)}, u32[]{:S(2)}, u32[]{:S(2)}) collective-permute-start(bf16[64,512]{1,0:T(8,128)(2,1)S(1)} %get-tuple-element.69), channel_id=1, source_target_pairs={{0,32},{1,33},{2,34},{3,35},{4,36},{5,37},{6,38},{7,39},{8,40},{9,... | collective-permute-start | bytes 196616 | tf_op jit(solution)/shard_map/ppermute | solution.py:41
  31.5 7.8 %collective-permute-start.16 = (bf16[64,512]{1,0:T(8,128)(2,1)S(1)}, bf16[64,512]{1,0:T(8,128)(2,1)S(1)}, u32[]{:S(2)}, u32[]{:S(2)}) collective-permute-start(bf16[64,512]{1,0:T(8,128)(2,1)S(1)} %get-tuple-element.70), channel_id=1, source_target_pairs={{0,64},{1,65},{2,66},{3,67},{4,68},{5,69},{6,70},{7,71},{8,72},{9,... | collective-permute-start | bytes 196616 | tf_op jit(solution)/shard_map/ppermute | solution.py:41
  33.6 5.7 %collective-permute-start.17 = (bf16[64,512]{1,0:T(8,128)(2,1)S(1)}, bf16[64,512]{1,0:T(8,128)(2,1)S(1)}, u32[]{:S(2)}, u32[]{:S(2)}) collective-permute-start(bf16[64,512]{1,0:T(8,128)(2,1)S(1)} %get-tuple-element.71), channel_id=1, source_target_pairs={{0,96},{1,97},{2,98},{3,99},{4,100},{5,101},{6,102},{7,103},{8,104... | collective-permute-start | bytes 196616 | tf_op jit(solution)/shard_map/ppermute | solution.py:41
  36.0 7.1 %collective-permute-start.7 = (bf16[64,512]{1,0:T(8,128)(2,1)S(1)}, bf16[64,512]{1,0:T(8,128)(2,1)S(1)}, u32[]{:S(2)}, u32[]{:S(2)}) collective-permute-start(bf16[64,512]{1,0:T(8,128)(2,1)S(1)} %get-tuple-element.54), channel_id=1, source_target_pairs={{0,8},{1,9},{2,10},{3,11},{4,12},{5,13},{6,14},{7,15},{8,16},{9,17... | collective-permute-start | bytes 196616 | tf_op jit(solution)/shard_map/ppermute | solution.py:41
  36.8 6.7 %collective-permute-start.8 = (bf16[64,512]{1,0:T(8,128)(2,1)S(1)}, bf16[64,512]{1,0:T(8,128)(2,1)S(1)}, u32[]{:S(2)}, u32[]{:S(2)}) collective-permute-start(bf16[64,512]{1,0:T(8,128)(2,1)S(1)} %get-tuple-element.55), channel_id=1, source_target_pairs={{0,16},{1,17},{2,18},{3,19},{4,20},{5,21},{6,22},{7,23},{8,24},{9,... | collective-permute-start | bytes 196616 | tf_op jit(solution)/shard_map/ppermute | solution.py:41
  37.8 5.6 %collective-permute-start.9 = (bf16[64,512]{1,0:T(8,128)(2,1)S(1)}, bf16[64,512]{1,0:T(8,128)(2,1)S(1)}, u32[]{:S(2)}, u32[]{:S(2)}) collective-permute-start(bf16[64,512]{1,0:T(8,128)(2,1)S(1)} %get-tuple-element.56), channel_id=1, source_target_pairs={{0,24},{1,25},{2,26},{3,27},{4,28},{5,29},{6,30},{7,31},{8,0},{9,1... | collective-permute-start | bytes 196616 | tf_op jit(solution)/shard_map/ppermute | solution.py:41
  39.3 10.0 %collective-permute-start.18 = (bf16[4,64,512]{2,1,0:T(8,128)(2,1)S(1)}, bf16[4,64,512]{2,1,0:T(8,128)(2,1)S(1)}, u32[]{:S(2)}, u32[]{:S(2)}) collective-permute-start(bf16[4,64,512]{2,1,0:T(8,128)(2,1)S(1)} %collect_kernel.2.b0), channel_id=1, source_target_pairs={{0,2},{1,3},{2,4},{3,5},{4,6},{5,7},{6,0},{7,1},{8,10},{9,11},{10,... | collective-permute-start | bytes 786440 | tf_op jit(solution)/shard_map/ppermute | solution.py:41
  40.2 13.7 %collective-permute-start.19 = (bf16[4,64,512]{2,1,0:T(8,128)(2,1)S(1)}, bf16[4,64,512]{2,1,0:T(8,128)(2,1)S(1)}, u32[]{:S(2)}, u32[]{:S(2)}) collective-permute-start(bf16[4,64,512]{2,1,0:T(8,128)(2,1)S(1)} %collect_kernel.2.b0), channel_id=1, source_target_pairs={{0,4},{1,5},{2,6},{3,7},{4,0},{5,1},{6,2},{7,3},{8,12},{9,13},{10,... | collective-permute-start | bytes 786440 | tf_op jit(solution)/shard_map/ppermute | solution.py:41
  43.0 10.9 %collective-permute-start.20 = (bf16[4,64,512]{2,1,0:T(8,128)(2,1)S(1)}, bf16[4,64,512]{2,1,0:T(8,128)(2,1)S(1)}, u32[]{:S(2)}, u32[]{:S(2)}) collective-permute-start(bf16[4,64,512]{2,1,0:T(8,128)(2,1)S(1)} %collect_kernel.2.b0), channel_id=1, source_target_pairs={{0,6},{1,7},{2,0},{3,1},{4,2},{5,3},{6,4},{7,5},{8,14},{9,15},{10,... | collective-permute-start | bytes 786440 | tf_op jit(solution)/shard_map/ppermute | solution.py:41
  46.0 10.1 %collective-permute-start.10 = (bf16[6,64,128]{2,1,0:T(8,128)(2,1)S(1)}, bf16[6,64,128]{2,1,0:T(8,128)(2,1)S(1)}, u32[]{:S(2)}, u32[]{:S(2)}) collective-permute-start(bf16[6,64,128]{2,1,0:T(8,128)(2,1)S(1)} %get-tuple-element.62), channel_id=1, source_target_pairs={{0,32},{1,33},{2,34},{3,35},{4,36},{5,37},{6,38},{7,39},{8,40},{9,... | collective-permute-start | bytes 294920 | tf_op jit(solution)/shard_map/ppermute | solution.py:41
  47.1 8.9 %collective-permute-start.11 = (bf16[6,64,128]{2,1,0:T(8,128)(2,1)S(1)}, bf16[6,64,128]{2,1,0:T(8,128)(2,1)S(1)}, u32[]{:S(2)}, u32[]{:S(2)}) collective-permute-start(bf16[6,64,128]{2,1,0:T(8,128)(2,1)S(1)} %get-tuple-element.63), channel_id=1, source_target_pairs={{0,64},{1,65},{2,66},{3,67},{4,68},{5,69},{6,70},{7,71},{8,72},{9,... | collective-permute-start | bytes 294920 | tf_op jit(solution)/shard_map/ppermute | solution.py:41
  49.3 6.8 %collective-permute-start.12 = (bf16[6,64,128]{2,1,0:T(8,128)(2,1)S(1)}, bf16[6,64,128]{2,1,0:T(8,128)(2,1)S(1)}, u32[]{:S(2)}, u32[]{:S(2)}) collective-permute-start(bf16[6,64,128]{2,1,0:T(8,128)(2,1)S(1)} %get-tuple-element.64), channel_id=1, source_target_pairs={{0,96},{1,97},{2,98},{3,99},{4,100},{5,101},{6,102},{7,103},{8,104... | collective-permute-start | bytes 294920 | tf_op jit(solution)/shard_map/ppermute | solution.py:41
  54.0 4.3 %collective-permute-start.21 = (bf16[4,4,64,512]{3,2,1,0:T(8,128)(2,1)S(1)}, bf16[4,4,64,512]{3,2,1,0:T(8,128)(2,1)S(1)}, u32[]{:S(2)}, u32[]{:S(2)}) collective-permute-start(bf16[4,4,64,512]{3,2,1,0:T(8,128)(2,1)S(1)} %collect_kernel.3.blocks), channel_id=1, source_target_pairs={{0,1},{1,0},{2,3},{3,2},{4,5},{5,4},{6,7},{7,6},{8,9},{9,8},{10,11... | collective-permute-start | bytes 3145736 | tf_op jit(solution)/shard_map/ppermute | solution.py:41
  56.1 1.0 %copy-start.1 = (bf16[512,256]{1,0:T(8,128)(2,1)S(1)}, bf16[512,256]{1,0:T(8,128)(2,1)}, u32[]{:S(2)}) copy-start(bf16[512,256]{1,0:T(8,128)(2,1)} %copy-done) | copy-start | bytes 786436
